TPU v7x, 768 devices: a whole 4x8x12 slice. The times are simulated.
768 devices in a mesh: sec: 2 (over x_hi), gx: 24 (over x_lo, z), az: 16 (over y, core).
Axes of the slice: x: 4 (x_hi: 2, x_lo: 2; x = x_hi * 2 + x_lo), y: 8, z: 12, core: 2. Of those that a mesh axis runs over, the one named last changes fastest.
Arguments:
- les_velocity: float32 [3, 8, 256, 6144], P(None, None, 'az', ('sec', 'gx')), may hold values from -6 to 6
- les_metric: float32 [3, 8, 256, 6144], P(None, None, 'az', ('sec', 'gx')), may hold values from 0.5 to 1.5
- caa_state: float32 [4, 8, 256, 6144], P(None, None, 'az', ('sec', 'gx')), may hold values from -6 to 6
- caa_metric: float32 [3, 8, 256, 6144], P(None, None, 'az', ('sec', 'gx')), may hold values from 0.5 to 1.5
- intersection_refs: int32 [768, 4], P(('sec', 'gx')), may hold values from 0 to 23, as said below
- offsets: int32 [768], P(('sec', 'gx')), may hold values from 0 to 8
- send_list: int32 [48, 24, 2], replicated, may hold values from -1 to 15, as said below
Outputs:
- les_out: float32 [3, 8, 256, 6144], P(None, None, 'az', ('sec', 'gx'))
- caa_out: float32 [4, 8, 256, 6144], P(None, None, 'az', ('sec', 'gx'))
Inputs may be any that keep to these rules, and one draw needn't show every extreme that they name: `intersection_refs`: row j belongs to slab r = j // 16; columns 0 and 2 are slabs of r's section (0 to 23), columns 1 and 3 slots (0 to 1). Among the 32 pairs of one slab no (slab, slot) pair repeats, at most 2 name one slab and exactly 2 name some slab, the slots towards one slab are filled from 0 upward, and send_list holds a block (not -1) at every named pair. send_list[s, d, c] is a block of slab s (0 to 15) for slot c of slab d of the same section, and -1 exactly where no row of slab d names (s, c).
All inputs are finite; a program needn't handle non-finite values.
Results may differ from a plain program's by a relative error of at most 0.00081.
Values may be sent and summed in bfloat16 or wider, within the bound.
No kernel may reach another device: no remote copies, remote signals or barrier semaphores. Data moves between devices by JAX's collectives and lax.ppermute only.
A program may use at most 32 MiB of HBM per device.

v0:
```python
import jax
import jax.numpy as jnp
import numpy as np
from jax import lax
from jax.sharding import PartitionSpec as P

LES_STEPS = 2
CAA_SUB = 4


les_step = 0.02
caa_step = 0.01
mach_number = 0.5


def with_halo(cells, sides, width, closed):
    for axis, dim in sides:
        count = lax.axis_size(axis)
        ends = count if closed else count - 1
        head = lax.slice_in_dim(cells, 0, width, axis=dim)
        tail = lax.slice_in_dim(cells, cells.shape[dim] - width, cells.shape[dim], axis=dim)
        cells = jnp.concatenate(
            [
                lax.ppermute(tail, axis, [(i, (i + 1) % count) for i in range(ends)]),
                cells,
                lax.ppermute(head, axis, [((i + 1) % count, i) for i in range(ends)]),
            ],
            axis=dim,
        )
    return cells


def slope_table():
    points = np.array([-1.0, -(0.2**0.5), 0.2**0.5, 1.0])
    identity = np.eye(4)
    differences = points[:, None] - points[None, :] + identity
    inverse_weights = 1.0 / np.prod(differences, axis=1)
    slope_matrix = inverse_weights[None, :] / inverse_weights[:, None] / differences
    slope_matrix = slope_matrix * (1.0 - identity)
    return slope_matrix - identity * slope_matrix.sum(axis=1)[:, None]


def line_matrix(length):
    slope_matrix = slope_table()
    result = np.zeros((length + 2, length))
    for element in range(length // 4):
        offset_node = 4 * element
        result[1 + offset_node : 5 + offset_node, offset_node : offset_node + 4] += slope_matrix.T
        result[offset_node + 1, offset_node] += 3.0
        result[offset_node, offset_node] -= 3.0
        result[offset_node + 5, offset_node + 3] += 3.0
        result[offset_node + 4, offset_node + 3] -= 3.0
    return jnp.asarray(result, jnp.float32)


def stream_extend(quantity):
    return with_halo(quantity, ((("sec", "gx"), 3),), 1, False)


def azimuth_extend(quantity):
    return with_halo(quantity, (("az", 2),), 1, True)


def radial_extend(quantity):
    return jnp.pad(quantity, ((0, 0), (1, 1), (0, 0), (0, 0)))


def stream_apply(extended, matrix):
    return jnp.einsum("cras,st->crat", extended, matrix, precision=lax.Precision.HIGHEST)


def azimuth_apply(extended, matrix):
    return jnp.einsum("cras,at->crts", extended, matrix, precision=lax.Precision.HIGHEST)


def radial_apply(extended, matrix):
    return jnp.einsum("cras,rt->ctas", extended, matrix, precision=lax.Precision.HIGHEST)


def les_rates(velocity, metric, matrices, extended):
    stacked = jnp.concatenate([extended, extended[0:1] * extended], axis=0)
    stream_slope = metric[0] * stream_apply(stacked, matrices[0])
    extended = azimuth_extend(velocity)
    stacked = jnp.concatenate([extended, extended[1:2] * extended], axis=0)
    azimuth_slope = metric[1] * azimuth_apply(stacked, matrices[1])
    extended = radial_extend(velocity)
    stacked = jnp.concatenate([extended, extended[2:3] * extended], axis=0)
    radial_slope = metric[2] * radial_apply(stacked, matrices[2])
    slopes = (stream_slope[:3], azimuth_slope[:3], radial_slope[:3])
    fluxes = (stream_slope[3:], azimuth_slope[3:], radial_slope[3:])
    omega_first = slopes[1][2] - slopes[2][1]
    omega_second = slopes[2][0] - slopes[0][2]
    omega_third = slopes[0][1] - slopes[1][0]
    lamb_vector = jnp.stack(
        [
            omega_second * velocity[2] - omega_third * velocity[1],
            omega_third * velocity[0] - omega_first * velocity[2],
            omega_first * velocity[1] - omega_second * velocity[0],
        ]
    )
    return (slopes, fluxes, lamb_vector)


def caa_rates(acoustic, metric, source, matrices, stream_fn):
    stream_slope = metric[0] * stream_apply(stream_fn(acoustic), matrices[0])
    paired = jnp.stack([acoustic[0], acoustic[2]])
    azimuth_slope = metric[1] * azimuth_apply(azimuth_extend(paired), matrices[1])
    paired = jnp.stack([acoustic[0], acoustic[3]])
    radial_slope = metric[2] * radial_apply(radial_extend(paired), matrices[2])
    return jnp.stack(
        [
            -(mach_number * stream_slope[0] + stream_slope[1] + azimuth_slope[1] + radial_slope[1]),
            -(mach_number * stream_slope[1] + stream_slope[0]) + source[0],
            -(mach_number * stream_slope[2] + azimuth_slope[0]) + source[1],
            -(mach_number * stream_slope[3] + radial_slope[0]) + source[2],
        ]
    )


def couple(lamb_vector, intersection_refs, offsets, send_list):
    rounded = lamb_vector.astype(jnp.bfloat16)
    components, radial_nodes, sector_nodes, stream_nodes = rounded.shape
    block_count = stream_nodes // 8
    packed = rounded.reshape(components, radial_nodes, sector_nodes, block_count, 8)
    packed = packed.transpose(3, 0, 1, 2, 4).reshape(block_count, -1)
    section = lax.axis_index("sec")
    own_slab = lax.axis_index("gx")
    slab_count = lax.axis_size("gx")
    gathered = lax.all_gather(packed, "gx", axis=0, tiled=True)

    def fetch_block(owner_slab, slot_index):
        local_block = send_list[section * slab_count + owner_slab, own_slab, slot_index]
        return gathered[owner_slab * block_count + local_block]

    leading = fetch_block(intersection_refs[:, 0], intersection_refs[:, 1]).astype(jnp.float32)
    trailing = fetch_block(intersection_refs[:, 2], intersection_refs[:, 3]).astype(jnp.float32)
    fraction = offsets.astype(jnp.float32)[:, None]
    blended = ((8.0 - fraction) * leading + fraction * trailing) / 8.0
    blended = blended.reshape(block_count, components, radial_nodes, sector_nodes, 8)
    return blended.transpose(1, 2, 3, 0, 4).reshape(
        components, radial_nodes, sector_nodes, stream_nodes
    )


def body(les_velocity, les_metric, caa_state, caa_metric, intersection_refs, offsets, send_list):
    radial_nodes = les_velocity.shape[1]
    sector_nodes = les_velocity.shape[2]
    stream_nodes = les_velocity.shape[3]
    matrices = (line_matrix(stream_nodes), line_matrix(sector_nodes), line_matrix(radial_nodes))
    velocity = les_velocity
    acoustic = caa_state
    for les_round in range(LES_STEPS):
        slopes, fluxes, lamb_vector = les_rates(
            velocity, les_metric, matrices, stream_extend(velocity)
        )
        source = couple(lamb_vector, intersection_refs, offsets, send_list)
        change = -0.5 * sum((fluxes[j] + velocity[j][None] * slopes[j] for j in range(3)))
        velocity = velocity + les_step * change
        for substep in range(CAA_SUB):
            acoustic = acoustic + caa_step * caa_rates(
                acoustic, caa_metric, source, matrices, stream_extend
            )
    return (velocity, acoustic)


def solution(mesh):
    in_specs = (
        P(None, None, "az", ("sec", "gx")),
        P(None, None, "az", ("sec", "gx")),
        P(None, None, "az", ("sec", "gx")),
        P(None, None, "az", ("sec", "gx")),
        P(("sec", "gx"), None),
        P(("sec", "gx")),
        P(),
    )
    out_specs = (P(None, None, "az", ("sec", "gx")), P(None, None, "az", ("sec", "gx")))
    return jax.shard_map(body, mesh=mesh, in_specs=in_specs, out_specs=out_specs, check_vma=False)
```

profile of v0, /device:TPU:4, one launch (start us, length us, event | category | flops | bytes accessed | tf_op | source)
XLA Modules:
  0.0 402.3 jit_solution(15986280422252828558)
XLA Ops:
  8.3 2.9 collective-permute-start.3
  11.2 1.2 fusion.293
  12.4 4.3 %collective-permute-start = (f32[3,8,16,1]{3,2,1,0:T(8,128)S(1)}, f32[3,8,16,1]{3,2,1,0:T(8,128)S(1)}, u32[]{:S(2)}, u32[]{:S(2)}) collective-permute-start(f32[3,8,16,1]{3,2,1,0:T(8,128)S(1)} %get-tuple-element.104), channel_id=1, source_target_pairs={{0,16},{16,32},{32,48},{48,64},{64,80},{80,96},{96,112},{112,128},... | collective-permute-start | bytes 4616 | tf_op jit(solution)/shard_map/ppermute | solution.py:24
  16.7 12.2 %collective-permute-start.1 = (f32[3,8,16,1]{3,2,1,0:T(8,128)S(1)}, f32[3,8,16,1]{3,2,1,0:T(8,128)S(1)}, u32[]{:S(2)}, u32[]{:S(2)}) collective-permute-start(f32[3,8,16,1]{3,2,1,0:T(8,128)S(1)} %get-tuple-element.105), channel_id=1, source_target_pairs={{16,0},{32,16},{48,32},{64,48},{80,64},{96,80},{112,96},{128,112},... | collective-permute-start | bytes 4616 | tf_op jit(solution)/shard_map/ppermute | solution.py:26
  30.8 1.3 collective-permute-done.1
  36.9 2.9 collective-permute-start.7
  39.9 1.9 collective-permute-start.4
  41.9 6.5 %collective-permute-start.5 = (f32[3,8,16,1]{3,2,1,0:T(8,128)S(1)}, f32[3,8,16,1]{3,2,1,0:T(8,128)S(1)}, u32[]{:S(2)}, u32[]{:S(2)}) collective-permute-start(f32[3,8,16,1]{3,2,1,0:T(8,128)S(1)} %get-tuple-element.94), channel_id=1, source_target_pairs={{16,0},{32,16},{48,32},{64,48},{80,64},{96,80},{112,96},{128,112},... | collective-permute-start | bytes 4616 | tf_op jit(solution)/shard_map/ppermute | solution.py:26
  50.1 1.4 collective-permute-done.5
  56.2 2.9 collective-permute-start.11
  59.3 1.9 collective-permute-start.8
  61.2 6.7 %collective-permute-start.9 = (f32[4,8,16,1]{3,2,1,0:T(8,128)S(1)}, f32[4,8,16,1]{3,2,1,0:T(8,128)S(1)}, u32[]{:S(2)}, u32[]{:S(2)}) collective-permute-start(f32[4,8,16,1]{3,2,1,0:T(8,128)S(1)} %get-tuple-element.85), channel_id=1, source_target_pairs={{16,0},{32,16},{48,32},{64,48},{80,64},{96,80},{112,96},{128,112},... | collective-permute-start | bytes 6152 | tf_op jit(solution)/shard_map/ppermute | solution.py:26
  73.1 1.2 collective-permute-done.9
  74.3 1.4 convolution_multiply_fusion.9
  77.5 65.4 %all-gather.3.cloned.1.call-done = bf16[384,3072]{1,0:T(8,128)(2,1)} async-done(((bf16[16,3072]{1,0:T(8,128)(2,1)}), bf16[384,3072]{1,0:T(8,128)(2,1)}) %all-gather.3.cloned.1.call-update) | async-done | bytes 2359312 | tf_op jit(solution)/shard_map/all_gather | solution.py:129
  142.9 2.7 gather_fusion.1
  145.9 3.3 gather_fusion.3
  149.2 1.2 copy.50
  150.3 96.9 %all-gather.5.cloned.1.call-done = bf16[384,3072]{1,0:T(8,128)(2,1)} async-done(((bf16[16,3072]{1,0:T(8,128)(2,1)}), bf16[384,3072]{1,0:T(8,128)(2,1)}) %all-gather.5.cloned.1.call-update) | async-done | bytes 2359312 | tf_op jit(solution)/shard_map/all_gather | solution.py:129
  247.3 3.3 gather_fusion.4
  250.6 2.4 copy.79
  252.9 3.3 gather_fusion.5
  256.3 2.3 copy.80
  258.6 2.7 multiply_bitcast_fusion
  261.3 1.1 fusion.272
  262.3 2.0 copy.53
  264.4 1.2 copy.54
  266.6 1.2 copy.56
  272.2 2.9 collective-permute-start.15
  275.5 1.9 collective-permute-start.12
  277.4 6.0 %collective-permute-start.13 = (f32[4,8,16,1]{3,2,1,0:T(8,128)S(1)}, f32[4,8,16,1]{3,2,1,0:T(8,128)S(1)}, u32[]{:S(2)}, u32[]{:S(2)}) collective-permute-start(f32[4,8,16,1]{3,2,1,0:T(8,128)S(1)} %copy-done.10), channel_id=1, source_target_pairs={{16,0},{32,16},{48,32},{64,48},{80,64},{96,80},{112,96},{128,112},... | collective-permute-start | bytes 6152 | tf_op jit(solution)/shard_map/ppermute | solution.py:26
  283.5 2.8 collective-permute-done.12
  286.4 1.2 collective-permute-done.13
  288.3 1.1 fusion.8
  289.7 2.9 collective-permute-start.19
  293.1 1.9 collective-permute-start.16
  295.0 6.5 %collective-permute-start.17 = (f32[4,8,16,1]{3,2,1,0:T(8,128)S(1)}, f32[4,8,16,1]{3,2,1,0:T(8,128)S(1)}, u32[]{:S(2)}, u32[]{:S(2)}) collective-permute-start(f32[4,8,16,1]{3,2,1,0:T(8,128)S(1)} %get-tuple-element.73), channel_id=1, source_target_pairs={{16,0},{32,16},{48,32},{64,48},{80,64},{96,80},{112,96},{128,112},... | collective-permute-start | bytes 6152 | tf_op jit(solution)/shard_map/ppermute | solution.py:26
  301.5 3.1 collective-permute-done.16
  304.7 1.2 collective-permute-done.17
  307.2 2.9 collective-permute-start.23
  310.5 1.9 collective-permute-start.20
  312.5 6.7 %collective-permute-start.21 = (f32[4,8,16,1]{3,2,1,0:T(8,128)S(1)}, f32[4,8,16,1]{3,2,1,0:T(8,128)S(1)}, u32[]{:S(2)}, u32[]{:S(2)}) collective-permute-start(f32[4,8,16,1]{3,2,1,0:T(8,128)S(1)} %get-tuple-element.67), channel_id=1, source_target_pairs={{16,0},{32,16},{48,32},{64,48},{80,64},{96,80},{112,96},{128,112},... | collective-permute-start | bytes 6152 | tf_op jit(solution)/shard_map/ppermute | solution.py:26
  319.2 2.9 collective-permute-done.20
  322.2 1.2 collective-permute-done.21
  324.7 2.9 collective-permute-start.27
  328.0 1.9 collective-permute-start.24
  330.0 6.5 %collective-permute-start.25 = (f32[4,8,16,1]{3,2,1,0:T(8,128)S(1)}, f32[4,8,16,1]{3,2,1,0:T(8,128)S(1)}, u32[]{:S(2)}, u32[]{:S(2)}) collective-permute-start(f32[4,8,16,1]{3,2,1,0:T(8,128)S(1)} %get-tuple-element.61), channel_id=1, source_target_pairs={{16,0},{32,16},{48,32},{64,48},{80,64},{96,80},{112,96},{128,112},... | collective-permute-start | bytes 6152 | tf_op jit(solution)/shard_map/ppermute | solution.py:26
  336.5 4.2 %collective-permute-done.24 = f32[4,8,16,1]{3,2,1,0:T(8,128)S(1)} collective-permute-done((f32[4,8,16,1]{3,2,1,0:T(8,128)S(1)}, f32[4,8,16,1]{3,2,1,0:T(8,128)S(1)}, u32[]{:S(2)}, u32[]{:S(2)}) %collective-permute-start.24) | collective-permute-done | bytes 2080 | tf_op jit(solution)/shard_map/ppermute | solution.py:24
  340.7 1.2 collective-permute-done.25
  343.2 2.9 collective-permute-start.31
  346.6 1.9 collective-permute-start.28
  348.5 6.5 %collective-permute-start.29 = (f32[4,8,16,1]{3,2,1,0:T(8,128)S(1)}, f32[4,8,16,1]{3,2,1,0:T(8,128)S(1)}, u32[]{:S(2)}, u32[]{:S(2)}) collective-permute-start(f32[4,8,16,1]{3,2,1,0:T(8,128)S(1)} %get-tuple-element.55), channel_id=1, source_target_pairs={{16,0},{32,16},{48,32},{64,48},{80,64},{96,80},{112,96},{128,112},... | collective-permute-start | bytes 6152 | tf_op jit(solution)/shard_map/ppermute | solution.py:26
  355.0 3.1 collective-permute-done.28
  358.2 1.2 collective-permute-done.29
  360.8 2.9 collective-permute-start.35
  364.1 1.9 collective-permute-start.32
  366.0 6.5 %collective-permute-start.33 = (f32[4,8,16,1]{3,2,1,0:T(8,128)S(1)}, f32[4,8,16,1]{3,2,1,0:T(8,128)S(1)}, u32[]{:S(2)}, u32[]{:S(2)}) collective-permute-start(f32[4,8,16,1]{3,2,1,0:T(8,128)S(1)} %get-tuple-element.49), channel_id=1, source_target_pairs={{16,0},{32,16},{48,32},{64,48},{80,64},{96,80},{112,96},{128,112},... | collective-permute-start | bytes 6152 | tf_op jit(solution)/shard_map/ppermute | solution.py:26
  372.5 2.7 collective-permute-done.32
  375.2 1.2 collective-permute-done.33
  377.8 2.9 collective-permute-start.39
  381.1 1.9 collective-permute-start.36
  383.1 6.5 %collective-permute-start.37 = (f32[4,8,16,1]{3,2,1,0:T(8,128)S(1)}, f32[4,8,16,1]{3,2,1,0:T(8,128)S(1)}, u32[]{:S(2)}, u32[]{:S(2)}) collective-permute-start(f32[4,8,16,1]{3,2,1,0:T(8,128)S(1)} %get-tuple-element.43), channel_id=1, source_target_pairs={{16,0},{32,16},{48,32},{64,48},{80,64},{96,80},{112,96},{128,112},... | collective-permute-start | bytes 6152 | tf_op jit(solution)/shard_map/ppermute | solution.py:26
  389.6 2.6 collective-permute-done.36
  392.3 1.2 collective-permute-done.37
  (239 shorter events, 38.7 us)
Async XLA Ops:
  7.2 60.8 %copy-start = (s32[48,24,2]{0,2,1:T(2,128)S(1)}, s32[48,24,2]{0,2,1:T(2,128)}, u32[]{:S(2)}) copy-start(s32[48,24,2]{0,2,1:T(2,128)} %param.16) | copy-start | bytes 27652
  7.2 22.9 %copy-start.9 = (f32[10,8,1,1]{0,1,3,2:T(8,128)S(1)}, f32[10,8,1,1]{0,1,3,2:T(8,128)}, u32[]{:S(2)}) copy-start(f32[10,8,1,1]{0,1,3,2:T(8,128)} %constant.115) | copy-start | bytes 964
  7.2 22.7 %copy-start.13 = (f32[3,8,16,128]{3,2,1,0:T(8,128)S(1)}, f32[3,8,16,128]{3,2,1,0:T(8,128)}, u32[]{:S(2)}) copy-start(f32[3,8,16,128]{3,2,1,0:T(8,128)} %param.11) | copy-start | bytes 589828
  7.2 135.7 %all-gather.3.cloned.1.call-start = ((), (), s32[]{:S(2)}) async-start(), calls=%async_computation | async-start | bytes 2457600 | tf_op jit(solution)/shard_map/all_gather | solution.py:129
  8.3 25.2 %collective-permute-start.2 = (f32[3,8,1,128]{3,2,1,0:T(1,128)S(1)}, f32[3,8,1,128]{3,2,1,0:T(1,128)S(1)}, u32[]{:S(2)}, u32[]{:S(2)}) collective-permute-start(f32[3,8,1,128]{3,2,1,0:T(1,128)S(1)} %get-tuple-element.106), channel_id=1, source_target_pairs={{0,1},{1,2},{2,3},{3,4},{4,5},{5,6},{6,7},{7,8},{8,9},{9,10},{10,1... | collective-permute-start | bytes 36872 | tf_op jit(solution)/shard_map/ppermute | solution.py:24
  8.3 25.2 %collective-permute-start.3 = (f32[3,8,1,128]{3,2,1,0:T(1,128)S(1)}, f32[3,8,1,128]{3,2,1,0:T(1,128)S(1)}, u32[]{:S(2)}, u32[]{:S(2)}) collective-permute-start(f32[3,8,1,128]{3,2,1,0:T(1,128)S(1)} %get-tuple-element.107), channel_id=1, source_target_pairs={{1,0},{2,1},{3,2},{4,3},{5,4},{6,5},{7,6},{8,7},{9,8},{10,9},{11,1... | collective-permute-start | bytes 36872 | tf_op jit(solution)/shard_map/ppermute | solution.py:26
  12.4 18.4 %collective-permute-start = (f32[3,8,16,1]{3,2,1,0:T(8,128)S(1)}, f32[3,8,16,1]{3,2,1,0:T(8,128)S(1)}, u32[]{:S(2)}, u32[]{:S(2)}) collective-permute-start(f32[3,8,16,1]{3,2,1,0:T(8,128)S(1)} %get-tuple-element.104), channel_id=1, source_target_pairs={{0,16},{16,32},{32,48},{48,64},{64,80},{80,96},{96,112},{112,128},... | collective-permute-start | bytes 4616 | tf_op jit(solution)/shard_map/ppermute | solution.py:24
  16.7 15.4 %collective-permute-start.1 = (f32[3,8,16,1]{3,2,1,0:T(8,128)S(1)}, f32[3,8,16,1]{3,2,1,0:T(8,128)S(1)}, u32[]{:S(2)}, u32[]{:S(2)}) collective-permute-start(f32[3,8,16,1]{3,2,1,0:T(8,128)S(1)} %get-tuple-element.105), channel_id=1, source_target_pairs={{16,0},{32,16},{48,32},{64,48},{80,64},{96,80},{112,96},{128,112},... | collective-permute-start | bytes 4616 | tf_op jit(solution)/shard_map/ppermute | solution.py:26
  29.9 3.6 copy-start.18
  30.0 2.1 copy-start.2
  30.7 1.9 copy-start.3
  32.5 1.1 copy-start.21
  36.6 210.6 %all-gather.5.cloned.1.call-start = ((), (), s32[]{:S(2)}) async-start(), calls=%async_computation.1 | async-start | bytes 2457600 | tf_op jit(solution)/shard_map/all_gather | solution.py:129
  36.8 16.0 %collective-permute-start.6 = (f32[3,8,1,128]{3,2,1,0:T(1,128)S(1)}, f32[3,8,1,128]{3,2,1,0:T(1,128)S(1)}, u32[]{:S(2)}, u32[]{:S(2)}) collective-permute-start(f32[3,8,1,128]{3,2,1,0:T(1,128)S(1)} %get-tuple-element.95), channel_id=1, source_target_pairs={{0,1},{1,2},{2,3},{3,4},{4,5},{5,6},{6,7},{7,8},{8,9},{9,10},{10,1... | collective-permute-start | bytes 36872 | tf_op jit(solution)/shard_map/ppermute | solution.py:24
  36.9 16.0 %collective-permute-start.7 = (f32[3,8,1,128]{3,2,1,0:T(1,128)S(1)}, f32[3,8,1,128]{3,2,1,0:T(1,128)S(1)}, u32[]{:S(2)}, u32[]{:S(2)}) collective-permute-start(f32[3,8,1,128]{3,2,1,0:T(1,128)S(1)} %get-tuple-element.96), channel_id=1, source_target_pairs={{1,0},{2,1},{3,2},{4,3},{5,4},{6,5},{7,6},{8,7},{9,8},{10,9},{11,1... | collective-permute-start | bytes 36872 | tf_op jit(solution)/shard_map/ppermute | solution.py:26
  39.9 10.2 %collective-permute-start.4 = (f32[3,8,16,1]{3,2,1,0:T(8,128)S(1)}, f32[3,8,16,1]{3,2,1,0:T(8,128)S(1)}, u32[]{:S(2)}, u32[]{:S(2)}) collective-permute-start(f32[3,8,16,1]{3,2,1,0:T(8,128)S(1)} %get-tuple-element.93), channel_id=1, source_target_pairs={{0,16},{16,32},{32,48},{48,64},{64,80},{80,96},{96,112},{112,128},... | collective-permute-start | bytes 4616 | tf_op jit(solution)/shard_map/ppermute | solution.py:24
  41.9 9.7 %collective-permute-start.5 = (f32[3,8,16,1]{3,2,1,0:T(8,128)S(1)}, f32[3,8,16,1]{3,2,1,0:T(8,128)S(1)}, u32[]{:S(2)}, u32[]{:S(2)}) collective-permute-start(f32[3,8,16,1]{3,2,1,0:T(8,128)S(1)} %get-tuple-element.94), channel_id=1, source_target_pairs={{16,0},{32,16},{48,32},{64,48},{80,64},{96,80},{112,96},{128,112},... | collective-permute-start | bytes 4616 | tf_op jit(solution)/shard_map/ppermute | solution.py:26
  54.4 1.7 copy-start.1
  55.2 12.8 %copy-start.20 = (s32[16,4]{0,1:T(4,128)S(1)}, s32[16,4]{0,1:T(4,128)}, u32[]{:S(2)}) copy-start(s32[16,4]{0,1:T(4,128)} %param.14) | copy-start | bytes 772
  56.2 14.3 %copy-start.14 = (f32[3,8,16,128]{3,2,1,0:T(8,128)S(1)}, f32[3,8,16,128]{3,2,1,0:T(8,128)}, u32[]{:S(2)}) copy-start(f32[3,8,16,128]{3,2,1,0:T(8,128)} %param.13) | copy-start | bytes 589828
  56.2 19.5 %collective-permute-start.10 = (f32[2,8,1,128]{3,2,1,0:T(1,128)S(1)}, f32[2,8,1,128]{3,2,1,0:T(1,128)S(1)}, u32[]{:S(2)}, u32[]{:S(2)}) collective-permute-start(f32[2,8,1,128]{3,2,1,0:T(1,128)S(1)} %get-tuple-element.124), channel_id=1, source_target_pairs={{0,1},{1,2},{2,3},{3,4},{4,5},{5,6},{6,7},{7,8},{8,9},{9,10},{10,1... | collective-permute-start | bytes 24584 | tf_op jit(solution)/shard_map/ppermute | solution.py:24
  56.2 19.5 %collective-permute-start.11 = (f32[2,8,1,128]{3,2,1,0:T(1,128)S(1)}, f32[2,8,1,128]{3,2,1,0:T(1,128)S(1)}, u32[]{:S(2)}, u32[]{:S(2)}) collective-permute-start(f32[2,8,1,128]{3,2,1,0:T(1,128)S(1)} %get-tuple-element.125), channel_id=1, source_target_pairs={{1,0},{2,1},{3,2},{4,3},{5,4},{6,5},{7,6},{8,7},{9,8},{10,9},{11,1... | collective-permute-start | bytes 24584 | tf_op jit(solution)/shard_map/ppermute | solution.py:26
  59.3 13.8 %collective-permute-start.8 = (f32[4,8,16,1]{3,2,1,0:T(8,128)S(1)}, f32[4,8,16,1]{3,2,1,0:T(8,128)S(1)}, u32[]{:S(2)}, u32[]{:S(2)}) collective-permute-start(f32[4,8,16,1]{3,2,1,0:T(8,128)S(1)} %get-tuple-element.84), channel_id=1, source_target_pairs={{0,16},{16,32},{32,48},{48,64},{64,80},{80,96},{96,112},{112,128},... | collective-permute-start | bytes 6152 | tf_op jit(solution)/shard_map/ppermute | solution.py:24
  61.2 13.1 %collective-permute-start.9 = (f32[4,8,16,1]{3,2,1,0:T(8,128)S(1)}, f32[4,8,16,1]{3,2,1,0:T(8,128)S(1)}, u32[]{:S(2)}, u32[]{:S(2)}) collective-permute-start(f32[4,8,16,1]{3,2,1,0:T(8,128)S(1)} %get-tuple-element.85), channel_id=1, source_target_pairs={{16,0},{32,16},{48,32},{64,48},{80,64},{96,80},{112,96},{128,112},... | collective-permute-start | bytes 6152 | tf_op jit(solution)/shard_map/ppermute | solution.py:26
  69.4 6.3 %copy-start.22 = (f32[18,16,1,1]{0,1,3,2:T(8,128)S(1)}, f32[18,16,1,1]{0,1,3,2:T(8,128)}, u32[]{:S(2)}) copy-start(f32[18,16,1,1]{0,1,3,2:T(8,128)} %constant.114) | copy-start | bytes 3460
  70.5 3.8 copy-start.4
  70.5 5.2 %copy-start.16 = (f32[8,16,128]{2,1,0:T(8,128)}, f32[8,16,128]{2,1,0:T(8,128)S(1)}, u32[]{:S(2)}) copy-start(f32[8,16,128]{2,1,0:T(8,128)S(1)} %get-tuple-element.87) | copy-start | bytes 196612
  265.6 2.7 copy-start.8
  265.6 2.7 copy-start.15
  271.2 3.9 copy-start.12
  271.5 12.0 %copy-start.7 = (f32[8,16,128]{2,1,0:T(8,128)S(1)}, f32[8,16,128]{2,1,0:T(8,128)}, u32[]{:S(2)}) copy-start(f32[8,16,128]{2,1,0:T(8,128)} %copy-done.6) | copy-start | bytes 196612
  271.7 3.8 copy-start.11
  271.7 5.8 %copy-start.10 = (f32[4,8,16,1]{3,2,1,0:T(8,128)S(1)}, f32[4,8,16,1]{3,2,1,0:T(8,128)}, u32[]{:S(2)}) copy-start(f32[4,8,16,1]{3,2,1,0:T(8,128)} %get-tuple-element.79) | copy-start | bytes 6148
  271.7 15.9 %copy-start.5 = (f32[8,16,128]{2,1,0:T(8,128)S(1)}, f32[8,16,128]{2,1,0:T(8,128)}, u32[]{:S(2)}) copy-start(f32[8,16,128]{2,1,0:T(8,128)} %copy-done.4) | copy-start | bytes 196612
  271.9 16.3 %copy-start.23 = (f32[18,16,1,1]{0,1,3,2:T(8,128)S(1)}, f32[18,16,1,1]{0,1,3,2:T(8,128)}, u32[]{:S(2)}) copy-start(f32[18,16,1,1]{0,1,3,2:T(8,128)} %constant.114) | copy-start | bytes 3460
  272.1 16.1 %collective-permute-start.14 = (f32[2,8,1,128]{3,2,1,0:T(1,128)S(1)}, f32[2,8,1,128]{3,2,1,0:T(1,128)S(1)}, u32[]{:S(2)}, u32[]{:S(2)}) collective-permute-start(f32[2,8,1,128]{3,2,1,0:T(1,128)S(1)} %get-tuple-element.122), channel_id=1, source_target_pairs={{0,1},{1,2},{2,3},{3,4},{4,5},{5,6},{6,7},{7,8},{8,9},{9,10},{10,1... | collective-permute-start | bytes 24584 | tf_op jit(solution)/shard_map/ppermute | solution.py:24
  272.2 16.1 %collective-permute-start.15 = (f32[2,8,1,128]{3,2,1,0:T(1,128)S(1)}, f32[2,8,1,128]{3,2,1,0:T(1,128)S(1)}, u32[]{:S(2)}, u32[]{:S(2)}) collective-permute-start(f32[2,8,1,128]{3,2,1,0:T(1,128)S(1)} %get-tuple-element.123), channel_id=1, source_target_pairs={{1,0},{2,1},{3,2},{4,3},{5,4},{6,5},{7,6},{8,7},{9,8},{10,9},{11,1... | collective-permute-start | bytes 24584 | tf_op jit(solution)/shard_map/ppermute | solution.py:26
  275.5 10.9 %collective-permute-start.12 = (f32[4,8,16,1]{3,2,1,0:T(8,128)S(1)}, f32[4,8,16,1]{3,2,1,0:T(8,128)S(1)}, u32[]{:S(2)}, u32[]{:S(2)}) collective-permute-start(f32[4,8,16,1]{3,2,1,0:T(8,128)S(1)} %copy-done.11), channel_id=1, source_target_pairs={{0,16},{16,32},{32,48},{48,64},{64,80},{80,96},{96,112},{112,128},... | collective-permute-start | bytes 6152 | tf_op jit(solution)/shard_map/ppermute | solution.py:24
  277.4 10.1 %collective-permute-start.13 = (f32[4,8,16,1]{3,2,1,0:T(8,128)S(1)}, f32[4,8,16,1]{3,2,1,0:T(8,128)S(1)}, u32[]{:S(2)}, u32[]{:S(2)}) collective-permute-start(f32[4,8,16,1]{3,2,1,0:T(8,128)S(1)} %copy-done.10), channel_id=1, source_target_pairs={{16,0},{32,16},{48,32},{64,48},{80,64},{96,80},{112,96},{128,112},... | collective-permute-start | bytes 6152 | tf_op jit(solution)/shard_map/ppermute | solution.py:26
  289.6 17.0 %copy-start.17 = (f32[8,16,128]{2,1,0:T(8,128)S(1)}, f32[8,16,128]{2,1,0:T(8,128)}, u32[]{:S(2)}) copy-start(f32[8,16,128]{2,1,0:T(8,128)} %copy-done.16) | copy-start | bytes 196612
  289.7 16.8 %collective-permute-start.18 = (f32[2,8,1,128]{3,2,1,0:T(1,128)S(1)}, f32[2,8,1,128]{3,2,1,0:T(1,128)S(1)}, u32[]{:S(2)}, u32[]{:S(2)}) collective-permute-start(f32[2,8,1,128]{3,2,1,0:T(1,128)S(1)} %get-tuple-element.120), channel_id=1, source_target_pairs={{0,1},{1,2},{2,3},{3,4},{4,5},{5,6},{6,7},{7,8},{8,9},{9,10},{10,1... | collective-permute-start | bytes 24584 | tf_op jit(solution)/shard_map/ppermute | solution.py:24
  289.7 16.8 %collective-permute-start.19 = (f32[2,8,1,128]{3,2,1,0:T(1,128)S(1)}, f32[2,8,1,128]{3,2,1,0:T(1,128)S(1)}, u32[]{:S(2)}, u32[]{:S(2)}) collective-permute-start(f32[2,8,1,128]{3,2,1,0:T(1,128)S(1)} %get-tuple-element.121), channel_id=1, source_target_pairs={{1,0},{2,1},{3,2},{4,3},{5,4},{6,5},{7,6},{8,7},{9,8},{10,9},{11,1... | collective-permute-start | bytes 24584 | tf_op jit(solution)/shard_map/ppermute | solution.py:26
  293.1 11.6 %collective-permute-start.16 = (f32[4,8,16,1]{3,2,1,0:T(8,128)S(1)}, f32[4,8,16,1]{3,2,1,0:T(8,128)S(1)}, u32[]{:S(2)}, u32[]{:S(2)}) collective-permute-start(f32[4,8,16,1]{3,2,1,0:T(8,128)S(1)} %get-tuple-element.72), channel_id=1, source_target_pairs={{0,16},{16,32},{32,48},{48,64},{64,80},{80,96},{96,112},{112,128},... | collective-permute-start | bytes 6152 | tf_op jit(solution)/shard_map/ppermute | solution.py:24
  295.0 10.9 %collective-permute-start.17 = (f32[4,8,16,1]{3,2,1,0:T(8,128)S(1)}, f32[4,8,16,1]{3,2,1,0:T(8,128)S(1)}, u32[]{:S(2)}, u32[]{:S(2)}) collective-permute-start(f32[4,8,16,1]{3,2,1,0:T(8,128)S(1)} %get-tuple-element.73), channel_id=1, source_target_pairs={{16,0},{32,16},{48,32},{64,48},{80,64},{96,80},{112,96},{128,112},... | collective-permute-start | bytes 6152 | tf_op jit(solution)/shard_map/ppermute | solution.py:26
  307.2 16.8 %collective-permute-start.22 = (f32[2,8,1,128]{3,2,1,0:T(1,128)S(1)}, f32[2,8,1,128]{3,2,1,0:T(1,128)S(1)}, u32[]{:S(2)}, u32[]{:S(2)}) collective-permute-start(f32[2,8,1,128]{3,2,1,0:T(1,128)S(1)} %get-tuple-element.118), channel_id=1, source_target_pairs={{0,1},{1,2},{2,3},{3,4},{4,5},{5,6},{6,7},{7,8},{8,9},{9,10},{10,1... | collective-permute-start | bytes 24584 | tf_op jit(solution)/shard_map/ppermute | solution.py:24
  307.2 16.8 %collective-permute-start.23 = (f32[2,8,1,128]{3,2,1,0:T(1,128)S(1)}, f32[2,8,1,128]{3,2,1,0:T(1,128)S(1)}, u32[]{:S(2)}, u32[]{:S(2)}) collective-permute-start(f32[2,8,1,128]{3,2,1,0:T(1,128)S(1)} %get-tuple-element.119), channel_id=1, source_target_pairs={{1,0},{2,1},{3,2},{4,3},{5,4},{6,5},{7,6},{8,7},{9,8},{10,9},{11,1... | collective-permute-start | bytes 24584 | tf_op jit(solution)/shard_map/ppermute | solution.py:26
  310.5 11.6 %collective-permute-start.20 = (f32[4,8,16,1]{3,2,1,0:T(8,128)S(1)}, f32[4,8,16,1]{3,2,1,0:T(8,128)S(1)}, u32[]{:S(2)}, u32[]{:S(2)}) collective-permute-start(f32[4,8,16,1]{3,2,1,0:T(8,128)S(1)} %get-tuple-element.66), channel_id=1, source_target_pairs={{0,16},{16,32},{32,48},{48,64},{64,80},{80,96},{96,112},{112,128},... | collective-permute-start | bytes 6152 | tf_op jit(solution)/shard_map/ppermute | solution.py:24
  312.5 10.9 %collective-permute-start.21 = (f32[4,8,16,1]{3,2,1,0:T(8,128)S(1)}, f32[4,8,16,1]{3,2,1,0:T(8,128)S(1)}, u32[]{:S(2)}, u32[]{:S(2)}) collective-permute-start(f32[4,8,16,1]{3,2,1,0:T(8,128)S(1)} %get-tuple-element.67), channel_id=1, source_target_pairs={{16,0},{32,16},{48,32},{64,48},{80,64},{96,80},{112,96},{128,112},... | collective-permute-start | bytes 6152 | tf_op jit(solution)/shard_map/ppermute | solution.py:26
  324.7 17.8 %collective-permute-start.26 = (f32[2,8,1,128]{3,2,1,0:T(1,128)S(1)}, f32[2,8,1,128]{3,2,1,0:T(1,128)S(1)}, u32[]{:S(2)}, u32[]{:S(2)}) collective-permute-start(f32[2,8,1,128]{3,2,1,0:T(1,128)S(1)} %get-tuple-element.116), channel_id=1, source_target_pairs={{0,1},{1,2},{2,3},{3,4},{4,5},{5,6},{6,7},{7,8},{8,9},{9,10},{10,1... | collective-permute-start | bytes 24584 | tf_op jit(solution)/shard_map/ppermute | solution.py:24
  324.7 17.8 %collective-permute-start.27 = (f32[2,8,1,128]{3,2,1,0:T(1,128)S(1)}, f32[2,8,1,128]{3,2,1,0:T(1,128)S(1)}, u32[]{:S(2)}, u32[]{:S(2)}) collective-permute-start(f32[2,8,1,128]{3,2,1,0:T(1,128)S(1)} %get-tuple-element.117), channel_id=1, source_target_pairs={{1,0},{2,1},{3,2},{4,3},{5,4},{6,5},{7,6},{8,7},{9,8},{10,9},{11,1... | collective-permute-start | bytes 24584 | tf_op jit(solution)/shard_map/ppermute | solution.py:26
  328.0 12.6 %collective-permute-start.24 = (f32[4,8,16,1]{3,2,1,0:T(8,128)S(1)}, f32[4,8,16,1]{3,2,1,0:T(8,128)S(1)}, u32[]{:S(2)}, u32[]{:S(2)}) collective-permute-start(f32[4,8,16,1]{3,2,1,0:T(8,128)S(1)} %get-tuple-element.60), channel_id=1, source_target_pairs={{0,16},{16,32},{32,48},{48,64},{64,80},{80,96},{96,112},{112,128},... | collective-permute-start | bytes 6152 | tf_op jit(solution)/shard_map/ppermute | solution.py:24
  330.0 11.9 %collective-permute-start.25 = (f32[4,8,16,1]{3,2,1,0:T(8,128)S(1)}, f32[4,8,16,1]{3,2,1,0:T(8,128)S(1)}, u32[]{:S(2)}, u32[]{:S(2)}) collective-permute-start(f32[4,8,16,1]{3,2,1,0:T(8,128)S(1)} %get-tuple-element.61), channel_id=1, source_target_pairs={{16,0},{32,16},{48,32},{64,48},{80,64},{96,80},{112,96},{128,112},... | collective-permute-start | bytes 6152 | tf_op jit(solution)/shard_map/ppermute | solution.py:26
  343.2 16.8 %collective-permute-start.30 = (f32[2,8,1,128]{3,2,1,0:T(1,128)S(1)}, f32[2,8,1,128]{3,2,1,0:T(1,128)S(1)}, u32[]{:S(2)}, u32[]{:S(2)}) collective-permute-start(f32[2,8,1,128]{3,2,1,0:T(1,128)S(1)} %get-tuple-element.114), channel_id=1, source_target_pairs={{0,1},{1,2},{2,3},{3,4},{4,5},{5,6},{6,7},{7,8},{8,9},{9,10},{10,1... | collective-permute-start | bytes 24584 | tf_op jit(solution)/shard_map/ppermute | solution.py:24
  343.2 16.8 %collective-permute-start.31 = (f32[2,8,1,128]{3,2,1,0:T(1,128)S(1)}, f32[2,8,1,128]{3,2,1,0:T(1,128)S(1)}, u32[]{:S(2)}, u32[]{:S(2)}) collective-permute-start(f32[2,8,1,128]{3,2,1,0:T(1,128)S(1)} %get-tuple-element.115), channel_id=1, source_target_pairs={{1,0},{2,1},{3,2},{4,3},{5,4},{6,5},{7,6},{8,7},{9,8},{10,9},{11,1... | collective-permute-start | bytes 24584 | tf_op jit(solution)/shard_map/ppermute | solution.py:26
  346.6 11.6 %collective-permute-start.28 = (f32[4,8,16,1]{3,2,1,0:T(8,128)S(1)}, f32[4,8,16,1]{3,2,1,0:T(8,128)S(1)}, u32[]{:S(2)}, u32[]{:S(2)}) collective-permute-start(f32[4,8,16,1]{3,2,1,0:T(8,128)S(1)} %get-tuple-element.54), channel_id=1, source_target_pairs={{0,16},{16,32},{32,48},{48,64},{64,80},{80,96},{96,112},{112,128},... | collective-permute-start | bytes 6152 | tf_op jit(solution)/shard_map/ppermute | solution.py:24
  348.5 10.8 %collective-permute-start.29 = (f32[4,8,16,1]{3,2,1,0:T(8,128)S(1)}, f32[4,8,16,1]{3,2,1,0:T(8,128)S(1)}, u32[]{:S(2)}, u32[]{:S(2)}) collective-permute-start(f32[4,8,16,1]{3,2,1,0:T(8,128)S(1)} %get-tuple-element.55), channel_id=1, source_target_pairs={{16,0},{32,16},{48,32},{64,48},{80,64},{96,80},{112,96},{128,112},... | collective-permute-start | bytes 6152 | tf_op jit(solution)/shard_map/ppermute | solution.py:26
  360.7 16.3 %collective-permute-start.34 = (f32[2,8,1,128]{3,2,1,0:T(1,128)S(1)}, f32[2,8,1,128]{3,2,1,0:T(1,128)S(1)}, u32[]{:S(2)}, u32[]{:S(2)}) collective-permute-start(f32[2,8,1,128]{3,2,1,0:T(1,128)S(1)} %get-tuple-element.112), channel_id=1, source_target_pairs={{0,1},{1,2},{2,3},{3,4},{4,5},{5,6},{6,7},{7,8},{8,9},{9,10},{10,1... | collective-permute-start | bytes 24584 | tf_op jit(solution)/shard_map/ppermute | solution.py:24
  360.8 16.3 %collective-permute-start.35 = (f32[2,8,1,128]{3,2,1,0:T(1,128)S(1)}, f32[2,8,1,128]{3,2,1,0:T(1,128)S(1)}, u32[]{:S(2)}, u32[]{:S(2)}) collective-permute-start(f32[2,8,1,128]{3,2,1,0:T(1,128)S(1)} %get-tuple-element.113), channel_id=1, source_target_pairs={{1,0},{2,1},{3,2},{4,3},{5,4},{6,5},{7,6},{8,7},{9,8},{10,9},{11,1... | collective-permute-start | bytes 24584 | tf_op jit(solution)/shard_map/ppermute | solution.py:26
  364.1 11.1 %collective-permute-start.32 = (f32[4,8,16,1]{3,2,1,0:T(8,128)S(1)}, f32[4,8,16,1]{3,2,1,0:T(8,128)S(1)}, u32[]{:S(2)}, u32[]{:S(2)}) collective-permute-start(f32[4,8,16,1]{3,2,1,0:T(8,128)S(1)} %get-tuple-element.48), channel_id=1, source_target_pairs={{0,16},{16,32},{32,48},{48,64},{64,80},{80,96},{96,112},{112,128},... | collective-permute-start | bytes 6152 | tf_op jit(solution)/shard_map/ppermute | solution.py:24
  366.0 10.4 %collective-permute-start.33 = (f32[4,8,16,1]{3,2,1,0:T(8,128)S(1)}, f32[4,8,16,1]{3,2,1,0:T(8,128)S(1)}, u32[]{:S(2)}, u32[]{:S(2)}) collective-permute-start(f32[4,8,16,1]{3,2,1,0:T(8,128)S(1)} %get-tuple-element.49), channel_id=1, source_target_pairs={{16,0},{32,16},{48,32},{64,48},{80,64},{96,80},{112,96},{128,112},... | collective-permute-start | bytes 6152 | tf_op jit(solution)/shard_map/ppermute | solution.py:26
  377.8 16.3 %collective-permute-start.38 = (f32[2,8,1,128]{3,2,1,0:T(1,128)S(1)}, f32[2,8,1,128]{3,2,1,0:T(1,128)S(1)}, u32[]{:S(2)}, u32[]{:S(2)}) collective-permute-start(f32[2,8,1,128]{3,2,1,0:T(1,128)S(1)} %get-tuple-element.110), channel_id=1, source_target_pairs={{0,1},{1,2},{2,3},{3,4},{4,5},{5,6},{6,7},{7,8},{8,9},{9,10},{10,1... | collective-permute-start | bytes 24584 | tf_op jit(solution)/shard_map/ppermute | solution.py:24
  377.8 16.3 %collective-permute-start.39 = (f32[2,8,1,128]{3,2,1,0:T(1,128)S(1)}, f32[2,8,1,128]{3,2,1,0:T(1,128)S(1)}, u32[]{:S(2)}, u32[]{:S(2)}) collective-permute-start(f32[2,8,1,128]{3,2,1,0:T(1,128)S(1)} %get-tuple-element.111), channel_id=1, source_target_pairs={{1,0},{2,1},{3,2},{4,3},{5,4},{6,5},{7,6},{8,7},{9,8},{10,9},{11,1... | collective-permute-start | bytes 24584 | tf_op jit(solution)/shard_map/ppermute | solution.py:26
  381.1 11.1 %collective-permute-start.36 = (f32[4,8,16,1]{3,2,1,0:T(8,128)S(1)}, f32[4,8,16,1]{3,2,1,0:T(8,128)S(1)}, u32[]{:S(2)}, u32[]{:S(2)}) collective-permute-start(f32[4,8,16,1]{3,2,1,0:T(8,128)S(1)} %get-tuple-element.42), channel_id=1, source_target_pairs={{0,16},{16,32},{32,48},{48,64},{64,80},{80,96},{96,112},{112,128},... | collective-permute-start | bytes 6152 | tf_op jit(solution)/shard_map/ppermute | solution.py:24
  383.1 10.4 %collective-permute-start.37 = (f32[4,8,16,1]{3,2,1,0:T(8,128)S(1)}, f32[4,8,16,1]{3,2,1,0:T(8,128)S(1)}, u32[]{:S(2)}, u32[]{:S(2)}) collective-permute-start(f32[4,8,16,1]{3,2,1,0:T(8,128)S(1)} %get-tuple-element.43), channel_id=1, source_target_pairs={{16,0},{32,16},{48,32},{64,48},{80,64},{96,80},{112,96},{128,112},... | collective-permute-start | bytes 6152 | tf_op jit(solution)/shard_map/ppermute | solution.py:26
  (2 other events, 1.7 us)
Sparse Core Ops, SparseCore 0:
  36.8 106.0 all-gather.2
  145.3 101.9 all-gather.4
where the time goes:
time: 403 us; the launch traced here: 402 us
  waiting for transfers between devices  197 us (49%)
  starting transfers between devices  122 us (30%)
  local copies, waits for them, and re-layouts  39.7 us (10%)
  matrix products  16.6 us (4%)
  between operations  15.7 us (4%)
  other arithmetic  10.9 us (3%)
    all_gather x2, waiting for transfers between devices, couple(): gathered = lax.all_gather(packed, 'gx', axis=0, tiled=True)  162 us
    ppermute x20, starting transfers between devices, with_halo(): lax.ppermute(head, axis, [((i + 1) % count, i) for i in range(ends)])  100 us
    ppermute x20, waiting for transfers between devices, with_halo(): lax.ppermute(tail, axis, [(i, (i + 1) % count) for i in range(ends)])  22.9 us
    ppermute x20, starting transfers between devices, with_halo(): lax.ppermute(tail, axis, [(i, (i + 1) % count) for i in range(ends)])  21.7 us
    gather x4, local copies, waits for them, and re-layouts, fetch_block(): return gathered[owner_slab * block_count + local_block]  12.6 us
    ppermute x20, waiting for transfers between devices, with_halo(): lax.ppermute(head, axis, [((i + 1) % count, i) for i in range(ends)])  12.2 us
  transfers between devices with their start and end apart: 42, of which 21 were waited for; matrix products, arithmetic and copies ran while one was open for 8% of the time, Pallas kernels for 0%

commit v1 on v0

v1 whole, which is shorter than its diff:
```python
import functools

import jax
import jax.numpy as jnp
import numpy as np
from jax import lax
from jax.experimental import pallas as pl
from jax.experimental.pallas import tpu as pltpu
from jax.sharding import PartitionSpec as P


les_step = 0.02
caa_step = 0.01
mach_number = 0.5

STREAM = ("sec", "gx")
F32 = jnp.float32
BF16 = jnp.bfloat16
VMEM_LIMIT = 24 * 1024 * 1024


def slope_table():
    points = np.array([-1.0, -(0.2**0.5), 0.2**0.5, 1.0])
    identity = np.eye(4)
    differences = points[:, None] - points[None, :] + identity
    inverse_weights = 1.0 / np.prod(differences, axis=1)
    slope_matrix = inverse_weights[None, :] / inverse_weights[:, None] / differences
    slope_matrix = slope_matrix * (1.0 - identity)
    return slope_matrix - identity * slope_matrix.sum(axis=1)[:, None]


DM = slope_table() + np.diag([3.0, 0.0, 0.0, -3.0])
DM[np.abs(DM) < 1e-12] = 0.0


def lane_matrix(run):
    result = np.zeros((128, 128))
    for e in range(32):
        result[4 * e : 4 * e + 4, 4 * e : 4 * e + 4] = DM.T
        if (4 * e) % run:
            result[4 * e - 1, 4 * e] = -3.0
        if (4 * e + 4) % run:
            result[4 * e + 4, 4 * e + 3] = 3.0
    return result


def split_matrix(run):
    full = lane_matrix(run).astype(np.float32)
    high = full.astype(jnp.bfloat16)
    low = (full - high.astype(np.float32)).astype(jnp.bfloat16)
    return np.block([[high, low], [high, np.zeros_like(low)]])


OFFSETS = (-3, -2, -1, 1, 2, 3)
RAD, AZT, AZP, AZN, EDGE_M, EDGE_T = 0, 6, 12, 13, 14, 15


def coefficients():
    c = np.zeros((16, 8, 128), np.float32)
    for n, k in enumerate(OFFSETS):
        for s in range(8):
            i = s % 4
            if 0 <= i + k <= 3:
                c[RAD + n, s, :] = DM[i, i + k]
        for lane in range(128):
            i = (lane % 64) // 16
            if 0 <= i + k <= 3:
                c[AZT + n, :, lane] = DM[i, i + k]
    c[RAD + OFFSETS.index(1), 3, :] = 3.0
    c[RAD + OFFSETS.index(-1), 4, :] = -3.0
    for lane in range(128):
        i = (lane % 64) // 16
        if i == 0:
            c[AZP, :, lane] = -3.0
        if i == 3:
            c[AZN, :, lane] = 3.0
    c[EDGE_M, :, 127] = 3.0
    c[EDGE_M, :, 0] = -3.0
    for i in range(4):
        c[EDGE_T, :, 16 * i] = -3.0
        c[EDGE_T, :, 79 + 16 * i] = 3.0
    return c


def lanes_of():
    return lax.broadcasted_iota(jnp.int32, (8, 128), 1)


def lane_roll(x, shift):
    shift %= 128
    return pltpu.roll(x, shift, axis=1) if shift else x


def times(rows, weights):
    x = jnp.concatenate(rows, axis=0)
    high = x.astype(BF16)
    low = (x - high.astype(F32)).astype(BF16)
    y = jnp.dot(jnp.concatenate([high, low], axis=1), weights, preferred_element_type=F32)
    y = y[:, :128] + y[:, 128:]
    return [y[8 * n : 8 * n + 8] for n in range(len(rows))]


def stream_main(fields, halos, weights, coef):
    lane = lanes_of()
    out = times([row for rows in fields for row in rows], weights)
    results = []
    at = 0
    for rows, tiles in zip(fields, halos):
        result = []
        for n in range(len(rows)):
            tile, i = tiles[n // 4], n % 4
            edge = jnp.where(lane == 127, lane_roll(tile, 127 - 16 * i), lane_roll(tile, 49 - 16 * i))
            result.append(out[at] + coef[EDGE_M] * edge)
            at += 1
        results.append(result)
    return results


def stream_halo(fields, halos, weights, coef):
    lane = lanes_of()
    out = times([tile for tiles in halos for tile in tiles], weights)
    results = []
    at = 0
    for rows, tiles in zip(fields, halos):
        result = []
        for e in range(len(tiles)):
            edge = None
            for i in range(4):
                low, high = lane_roll(rows[4 * e + i], 16 * i + 1), lane_roll(rows[4 * e + i], 79 + 16 * i)
                edge = low if edge is None else jnp.where(lane == 16 * i, low, edge)
                edge = jnp.where(lane == 79 + 16 * i, high, edge)
            result.append(out[at] + coef[EDGE_T] * edge)
            at += 1
        results.append(result)
    return results


def azimuth_main(rows, before, after):
    out = []
    for e in range(len(rows) // 4):
        f = rows[4 * e : 4 * e + 4]
        prev = before if e == 0 else rows[4 * e - 1]
        following = after if 4 * e + 4 == len(rows) else rows[4 * e + 4]
        a, b, c = float(DM[0, 1]), float(DM[0, 2]), float(DM[0, 3])
        d, g, h = float(DM[1, 0]), float(DM[1, 2]), float(DM[1, 3])
        out.append(a * f[1] + b * f[2] + c * f[3] - 3.0 * prev)
        out.append(d * f[0] + g * f[2] + h * f[3])
        out.append(-(h * f[0] + g * f[1] + d * f[3]))
        out.append(3.0 * following - (c * f[0] + b * f[1] + a * f[2]))
    return out


def azimuth_halo(tiles, before, after, coef):
    out = []
    for e, tile in enumerate(tiles):
        prev = before if e == 0 else tiles[e - 1]
        following = after if e + 1 == len(tiles) else tiles[e + 1]
        total = coef[AZP] * lane_roll(prev, -48) + coef[AZN] * lane_roll(following, 48)
        for n, k in enumerate(OFFSETS):
            total = total + coef[AZT + n] * lane_roll(tile, -16 * k)
        out.append(total)
    return out


def radial(tiles, coef):
    out = []
    for tile in tiles:
        total = None
        for n, k in enumerate(OFFSETS):
            term = coef[RAD + n] * pltpu.roll(tile, (-k) % 8, axis=0)
            total = term if total is None else total + term
        out.append(total)
    return out


def pack(rows, last):
    lane = lanes_of()
    out = None
    for g, row in enumerate(rows):
        moved = lane_roll(row, 16 * g + (16 if last else 0))
        out = moved if out is None else jnp.where(lane >= 16 * g, moved, out)
    return out


def halo_tile(from_left, from_right, n):
    left, right = from_left[n // 2].astype(F32), from_right[n // 2].astype(F32)
    if n % 2:
        right = lane_roll(right, 64)
    else:
        left = lane_roll(left, 64)
    return jnp.where(lanes_of() < 64, right, left)


def turn(tiles):
    group = lanes_of() // 8
    tiles = list(tiles)
    for bit in range(4):
        step = 1 << bit
        high = (group & step) != 0
        for p in range(16):
            if p & step:
                continue
            x, y = tiles[p], tiles[p | step]
            tiles[p] = jnp.where(high, lane_roll(y, 8 * step), x)
            tiles[p | step] = jnp.where(high, y, lane_roll(x, -8 * step))
    return tiles


def column(ref, c, az, sector):
    return ref[c, pl.ds(az, 8, stride=sector), :]


def first_kernel(sector, u, lm, w, m, low, high, both):
    for c in range(3):
        for i in range(4):
            low[4 * c + i] = column(u, c, i, sector)
            high[4 * c + i] = column(u, c, sector - 4 + i, sector)
        low[12 + c] = column(lm, c, 0, sector)
        high[12 + c] = column(lm, c, sector - 1, sector)
    for f in range(7):
        for az in range(sector):
            value = column(w, f, az, sector) if f < 4 else column(m, f - 4, az, sector)
            both[f * sector + az] = value.astype(BF16)


def les_pack_kernel(sector, u, lm, before, after, first, last):
    entries = []
    for c in range(3):
        for e in range(-1, 5):
            if e < 0:
                entries.append([before[4 * c + i] for i in range(4)])
            elif e == 4:
                entries.append([after[4 * c + i] for i in range(4)])
            else:
                entries.append([column(u, c, 4 * e + i, sector) for i in range(4)])
    for c in range(3):
        for e in range(4):
            entries.append([column(lm, c, 4 * e + i, sector) for i in range(4)])
    for n in range(len(entries) // 2):
        rows = entries[2 * n] + entries[2 * n + 1]
        first[n] = pack(rows, False)
        last[n] = pack(rows, True)


def les_kernel(sector, sends, u, lm, before, after, from_left, from_right, weights, coef, out, sent, um, ut, mm, mt, lamb, blk):
    w_main, w_halo = weights[0], weights[1]
    zero = jnp.zeros((8, 128), F32)
    for c in range(3):
        for i in range(4):
            um[0, c, i] = before[4 * c + i]
            um[0, c, 4 + sector + i] = after[4 * c + i]
            mm[c, i] = before[12 + c] if i == 3 else zero
            mm[c, 4 + sector + i] = after[12 + c] if i == 0 else zero
        for az in range(sector):
            um[0, c, 4 + az] = column(u, c, az, sector)
            mm[c, 4 + az] = column(lm, c, az, sector)
        for e in range(6):
            ut[0, c, e] = halo_tile(from_left, from_right, 6 * c + e)
            mt[c, e] = halo_tile(from_left, from_right, 18 + 4 * c + e - 1) if 1 <= e <= 4 else zero

    def element(step, e):
        rows = [[um[step, c, 4 * e + i] for i in range(4)] for c in range(3)]
        tiles = [[ut[step, c, e]] for c in range(3)]
        if isinstance(e, int):
            below, above, tile_below, tile_above = max(4 * e - 1, 0), min(4 * e + 4, sector + 7), max(e - 1, 0), min(e + 1, 5)
        else:
            below, above = jnp.maximum(4 * e - 1, 0), jnp.minimum(4 * e + 4, sector + 7)
            tile_below, tile_above = jnp.maximum(e - 1, 0), jnp.minimum(e + 1, 5)
        prev = [um[step, c, below] for c in range(3)]
        following = [um[step, c, above] for c in range(3)]
        metric = [[mm[c, 4 * e + i] for i in range(4)] for c in range(3)]

        fields = rows + [[x * y for x, y in zip(rows[0], rows[c])] for c in range(3)]
        halos = tiles + [[tiles[0][0] * tiles[c][0]] for c in range(3)]
        stream = stream_main(fields, halos, w_main, coef)
        slopes = [[[a * b for a, b in zip(metric[0], stream[c])] for c in range(3)]]
        fluxes = [[[a * b for a, b in zip(metric[0], stream[3 + c])] for c in range(3)]]
        slopes.append([])
        fluxes.append([])
        for c in range(3):
            slopes[1].append([a * b for a, b in zip(metric[1], azimuth_main(rows[c], prev[c], following[c]))])
            product = [x * y for x, y in zip(rows[1], rows[c])]
            product = azimuth_main(product, prev[1] * prev[c], following[1] * following[c])
            fluxes[1].append([a * b for a, b in zip(metric[1], product)])
        slopes.append([])
        fluxes.append([])
        for c in range(3):
            slopes[2].append([a * b for a, b in zip(metric[2], radial(rows[c], coef))])
            product = radial([x * y for x, y in zip(rows[2], rows[c])], coef)
            fluxes[2].append([a * b for a, b in zip(metric[2], product)])
        for i in range(4):
            first = slopes[1][2][i] - slopes[2][1][i]
            second = slopes[2][0][i] - slopes[0][2][i]
            third = slopes[0][1][i] - slopes[1][0][i]
            at = 4 * e + i
            lamb[0, at] = second * rows[2][i] - third * rows[1][i]
            lamb[1, at] = third * rows[0][i] - first * rows[2][i]
            lamb[2, at] = first * rows[1][i] - second * rows[0][i]
            for c in range(3):
                total = None
                for j in range(3):
                    term = fluxes[j][c][i] + rows[j][i] * slopes[j][c][i]
                    total = term if total is None else total + term
                value = rows[c][i] - (0.5 * les_step) * total
                if step == 0:
                    um[1, c, at] = value
                else:
                    out[c, pl.ds(at - 4, 8, stride=sector), :] = value
        if step == 0:
            low = [ut[step, c, tile_below] for c in range(3)]
            high = [ut[step, c, tile_above] for c in range(3)]
            metric = [mt[c, e] for c in range(3)]
            stream = stream_halo(fields, halos, w_halo, coef)
            for c in range(3):
                total = metric[0] * (stream[3 + c][0] + tiles[0][0] * stream[c][0])
                slope = azimuth_halo(tiles[c], low[c], high[c], coef)[0]
                flux = azimuth_halo([tiles[1][0] * tiles[c][0]], low[1] * low[c], high[1] * high[c], coef)[0]
                total = total + metric[1] * (flux + tiles[1][0] * slope)
                slope = radial(tiles[c], coef)[0]
                flux = radial([tiles[2][0] * tiles[c][0]], coef)[0]
                total = total + metric[2] * (flux + tiles[2][0] * slope)
                ut[1, c, e] = tiles[c][0] - (0.5 * les_step) * total

    for step in range(2):

        @pl.loop(0 if step == 0 else 1, 6 if step == 0 else 5)
        def _(e):
            element(step, e)

        for c in range(3):
            blocks = turn([lamb[c, 4 + az] for az in range(sector)])
            for j in range(16):
                blk[j, 3 * step + c] = blocks[j].astype(BF16)

    @pl.loop(0, sends.shape[0])
    def _(n):
        index = jnp.clip(sends[n], 0, 15)
        slab, slot = n // 2, n % 2
        for step in range(2):
            for c in range(3):
                sent[4 * slab + 2 * step + slot, c] = blk[index, 3 * step + c]


def blend_kernel(sector, slabs, refs, offsets, got, own, up, down):
    for step in range(2):
        for c in range(3):
            tiles = []
            for j in range(16):
                a = jnp.clip(refs[4 * j], 0, slabs - 1) * 4 + 2 * step + jnp.clip(refs[4 * j + 1], 0, 1)
                b = jnp.clip(refs[4 * j + 2], 0, slabs - 1) * 4 + 2 * step + jnp.clip(refs[4 * j + 3], 0, 1)
                fraction = offsets[j].astype(F32)
                blend = (8.0 - fraction) * got[a, c].astype(F32) + fraction * got[b, c].astype(F32)
                tiles.append(blend * 0.125)
            tiles = turn(tiles)
            for az in range(sector):
                own[step, c, az] = tiles[az]
                narrow = tiles[az].astype(BF16)
                if step == 0:
                    up[c * 16 + az] = narrow
                    down[c * 16 + az] = narrow
                else:
                    if az >= 8:
                        up[48 + c * 8 + az - 8] = narrow
                    else:
                        down[48 + c * 8 + az] = narrow


def caa_pack_kernel(sector, own, below, above, w, m, caa_below, caa_above, first, last):
    entries = []
    for c in range(3):
        for e in range(12):
            if e < 4:
                entries.append([(below, c * 16 + 4 * e + i) for i in range(4)])
            elif e < 8:
                entries.append([(own, (0, c, 4 * (e - 4) + i)) for i in range(4)])
            else:
                entries.append([(above, c * 16 + 4 * (e - 8) + i) for i in range(4)])
    for c in range(3):
        for e in range(2, 10):
            if e < 4:
                entries.append([(below, 48 + c * 8 + 4 * (e - 2) + i) for i in range(4)])
            elif e < 8:
                entries.append([(own, (1, c, 4 * (e - 4) + i)) for i in range(4)])
            else:
                entries.append([(above, 48 + c * 8 + 4 * (e - 8) + i) for i in range(4)])
    for f in range(7):
        for e in range(12):
            if e < 4:
                entries.append([(caa_below, f * sector + 4 * e + i) for i in range(4)])
            elif e < 8:
                ref, c = (w, f) if f < 4 else (m, f - 4)
                entries.append([(ref, (c, pl.ds(4 * (e - 4) + i, 8, stride=sector), slice(None))) for i in range(4)])
            else:
                entries.append([(caa_above, f * sector + 4 * (e - 8) + i) for i in range(4)])
    for n in range(len(entries) // 2):
        rows = [ref[at].astype(F32) for ref, at in entries[2 * n] + entries[2 * n + 1]]
        first[n] = pack(rows, False).astype(BF16)
        last[n] = pack(rows, True).astype(BF16)


CAA_RANGES = ((0, 12), (1, 11), (1, 11), (2, 10), (2, 10), (3, 9), (3, 9), (4, 8))


def caa_kernel(sector, w, m, own, below, above, caa_below, caa_above, from_left, from_right, weights, coef, out, wm, wt, mm, mt, sm, st):
    w_main, w_halo = weights[0], weights[1]

    for f in range(7):
        for az in range(3 * sector):
            if az < sector:
                value = caa_below[f * sector + az].astype(F32)
            elif az < 2 * sector:
                value = column(w, f, az - sector, sector) if f < 4 else column(m, f - 4, az - sector, sector)
            else:
                value = caa_above[f * sector + az - 2 * sector].astype(F32)
            if f < 4:
                wm[0, f, az] = value
            else:
                mm[f - 4, az] = value * caa_step
        for e in range(12):
            value = halo_tile(from_left, from_right, 60 + 12 * f + e)
            if f < 4:
                wt[0, f, e] = value
            else:
                mt[f - 4, e] = value * caa_step
    for c in range(3):
        for az in range(16):
            sm[0, c, az] = below[c * 16 + az].astype(F32) * caa_step
            sm[0, c, 16 + az] = own[0, c, az] * caa_step
            sm[0, c, 32 + az] = above[c * 16 + az].astype(F32) * caa_step
            sm[1, c, 16 + az] = own[1, c, az] * caa_step
        for az in range(8):
            sm[1, c, 8 + az] = below[48 + c * 8 + az].astype(F32) * caa_step
            sm[1, c, 32 + az] = above[48 + c * 8 + az].astype(F32) * caa_step
        for e in range(12):
            st[0, c, e] = halo_tile(from_left, from_right, 12 * c + e) * caa_step
        for e in range(8):
            st[1, c, 2 + e] = halo_tile(from_left, from_right, 36 + 8 * c + e) * caa_step

    def pair(now, source, e, final):
        rows = [[wm[now, f, 4 * e + i] for i in range(8)] for f in range(4)]
        tiles = [[wt[now, f, e + n] for n in range(2)] for f in range(4)]
        below, above = jnp.maximum(4 * e - 1, 0), jnp.minimum(4 * e + 8, 47)
        tile_below, tile_above = jnp.maximum(e - 1, 0), jnp.minimum(e + 2, 11)

        def rates(values, metric, sources, stream, around, up):
            p, v0, v1, v2 = values
            count = len(p)
            azimuth_p, azimuth_v = around
            radial_p, radial_v = up
            for n in range(count):
                m0, m1, m2 = metric[0](n), metric[1](n), metric[2](n)
                half = mach_number * m0
                yield (
                    n,
                    p[n] - m0 * stream[0][n] - m1 * azimuth_v[n] - m2 * radial_v[n],
                    v0[n] - m0 * stream[1][n] + sources[0](n),
                    v1[n] - half * stream[2][n] - m1 * azimuth_p[n] + sources[1](n),
                    v2[n] - half * stream[3][n] - m2 * radial_p[n] + sources[2](n),
                )

        def mixed(values):
            p, v0, v1, v2 = values
            return [
                [mach_number * a + b for a, b in zip(p, v0)],
                [mach_number * b + a for a, b in zip(p, v0)],
                v1,
                v2,
            ]

        fields, halos = mixed(rows), mixed(tiles)
        stream = stream_main(fields, halos, w_main, coef)
        around = [azimuth_main(rows[f], wm[now, f, below], wm[now, f, above]) for f in (0, 2)]
        up = [radial(rows[f], coef) for f in (0, 3)]
        metric = [lambda n, c=c: mm[c, 4 * e + n] for c in range(3)]
        sources = [lambda n, c=c: sm[source, c, 4 * e + n] for c in range(3)]
        for n, *values in rates(rows, metric, sources, stream, around, up):
            for f in range(4):
                if final:
                    out[f, pl.ds(4 * e + n - 16, 8, stride=sector), :] = values[f]
                else:
                    wm[1 - now, f, 4 * e + n] = values[f]
        if not final:
            stream = stream_halo(fields, halos, w_halo, coef)
            around = [azimuth_halo(tiles[f], wt[now, f, tile_below], wt[now, f, tile_above], coef) for f in (0, 2)]
            up = [radial(tiles[f], coef) for f in (0, 3)]
            metric = [lambda n, c=c: mt[c, e + n] for c in range(3)]
            sources = [lambda n, c=c: st[source, c, e + n] for c in range(3)]
            for n, *values in rates(tiles, metric, sources, stream, around, up):
                for f in range(4):
                    wt[1 - now, f, e + n] = values[f]

    for step, (start, stop) in enumerate(CAA_RANGES):

        @pl.loop(0, (stop - start) // 2)
        def _(n):
            pair(step % 2, step // 4, start + 2 * n, step == 7)


def call(kernel, name, outs, *args, smem=0, scratch=()):
    whole = pl.BlockSpec(memory_space=pltpu.VMEM)
    return pl.pallas_call(
        kernel,
        name=name,
        out_shape=[jax.ShapeDtypeStruct(shape, dtype) for shape, dtype in outs],
        in_specs=[pl.BlockSpec(memory_space=pltpu.SMEM)] * smem + [whole] * (len(args) - smem),
        out_specs=[whole] * len(outs),
        scratch_shapes=[pltpu.VMEM(shape, dtype) for shape, dtype in scratch],
        compiler_params=pltpu.CompilerParams(vmem_limit_bytes=VMEM_LIMIT),
    )(*args)


def both_ways(low, high, axis, closed):
    count = lax.axis_size(axis)
    ends = count if closed else count - 1
    below = lax.ppermute(high, axis, [(i, (i + 1) % count) for i in range(ends)])
    above = lax.ppermute(low, axis, [((i + 1) % count, i) for i in range(ends)])
    return below, above


def body(les_velocity, les_metric, caa_state, caa_metric, intersection_refs, offsets, send_list):
    _, radial_nodes, sector, length = les_velocity.shape
    slabs = lax.axis_size("gx")
    assert (radial_nodes, sector, length) == (8, 16, 128)
    lines = radial_nodes * sector
    u, lm, w, m = (x.reshape(-1, lines, length) for x in (les_velocity, les_metric, caa_state, caa_metric))
    weights = jnp.asarray(np.stack([split_matrix(128), split_matrix(16)]))
    coef = jnp.asarray(coefficients())
    own_row = lax.axis_index("sec") * slabs + lax.axis_index("gx")
    sends = lax.dynamic_slice_in_dim(send_list, own_row, 1, axis=0).reshape(-1)
    tile = (8, 128)

    low, high, both = call(
        functools.partial(first_kernel, sector),
        "first",
        [((15, *tile), F32), ((15, *tile), F32), ((7 * sector, *tile), BF16)],
        u, lm, w, m,
    )
    before, after = both_ways(low, high, "az", True)
    caa_below, caa_above = both_ways(both, both, "az", True)
    first, last = call(
        functools.partial(les_pack_kernel, sector),
        "les_pack",
        [((15, *tile), F32)] * 2,
        u, lm, before, after,
    )
    from_left, from_right = both_ways(first, last, STREAM, False)
    les_out, sent = call(
        functools.partial(les_kernel, sector),
        "les",
        [((3, lines, length), F32), ((slabs * 4, 3, *tile), BF16)],
        sends, u, lm, before, after, from_left, from_right, weights, coef,
        smem=1,
        scratch=[
            ((2, 3, 24, *tile), F32),
            ((2, 3, 6, *tile), F32),
            ((3, 24, *tile), F32),
            ((3, 6, *tile), F32),
            ((3, 24, *tile), F32),
            ((16, 6, *tile), BF16),
        ],
    )
    got = lax.all_to_all(sent.reshape(slabs, 96, 128), "gx", 0, 0, tiled=True).reshape(slabs * 4, 3, *tile)
    own, up, down = call(
        functools.partial(blend_kernel, sector, slabs),
        "blend",
        [((2, 3, sector, *tile), F32), ((72, *tile), BF16), ((72, *tile), BF16)],
        intersection_refs.reshape(-1), offsets, got,
        smem=2,
    )
    below, above = both_ways(down, up, "az", True)
    first, last = call(
        functools.partial(caa_pack_kernel, sector),
        "caa_pack",
        [((72, *tile), BF16)] * 2,
        own, below, above, w, m, caa_below, caa_above,
    )
    from_left, from_right = both_ways(first, last, STREAM, False)
    (caa_out,) = call(
        functools.partial(caa_kernel, sector),
        "caa",
        [((4, lines, length), F32)],
        w, m, own, below, above, caa_below, caa_above, from_left, from_right, weights, coef,
        scratch=[
            ((2, 4, 48, *tile), F32),
            ((2, 4, 12, *tile), F32),
            ((3, 48, *tile), F32),
            ((3, 12, *tile), F32),
            ((2, 3, 48, *tile), F32),
            ((2, 3, 12, *tile), F32),
        ],
    )
    return les_out.reshape(les_velocity.shape), caa_out.reshape(caa_state.shape)


def solution(mesh):
    field = P(None, None, "az", STREAM)
    in_specs = (field, field, field, field, P(STREAM, None), P(STREAM), P())
    return jax.shard_map(body, mesh=mesh, in_specs=in_specs, out_specs=(field, field), check_vma=False)
```

time: 403 us -> 97.7 us (0.24)
  the two profiles are of different devices: /device:TPU:4 before, /device:TPU:29 now
where the time goes in v1:
time: 97.7 us; the launch traced here: 97.3 us
  starting transfers between devices  38.1 us (39%)
  waiting for transfers between devices  36.2 us (37%)
  Pallas kernels  17.6 us (18%)
  local copies, waits for them, and re-layouts  4.59 us (5%)
    all_to_all x1, waiting for transfers between devices, body(): lax.all_to_all(sent.reshape(slabs, 96, 128), 'gx', 0, 0, tiled=True)  22.9 us
    ppermute x5, starting transfers between devices, both_ways(): above = lax.ppermute(low, axis, [((i + 1) % count, i) for i in range(ends)])  17.7 us
    pallas_call x6, Pallas kernels, call(): pl.pallas_call(kernel, name=name, out_shape=[jax.ShapeDtypeStruct(shape,...  17.6 us
    ppermute x5, starting transfers between devices, both_ways(): lax.ppermute(high, axis, [(i, (i + 1) % count) for i in range(ends)])  12.7 us
    ppermute x5, waiting for transfers between devices, both_ways(): above = lax.ppermute(low, axis, [((i + 1) % count, i) for i in range(ends)])  9.32 us
    all_to_all x1, starting transfers between devices, body(): lax.all_to_all(sent.reshape(slabs, 96, 128), 'gx', 0, 0, tiled=True)  7.67 us
    ppermute x5, waiting for transfers between devices, both_ways(): lax.ppermute(high, axis, [(i, (i + 1) % count) for i in range(ends)])  3.97 us
    unnamed x27, local copies, waits for them, and re-layouts  3.86 us
  transfers between devices with their start and end apart: 11, of which 8 were waited for; matrix products, arithmetic and copies ran while one was open for 1% of the time, Pallas kernels for 2%

profile of v1, /device:TPU:29, one launch (start us, length us, event | category | flops | bytes accessed | tf_op | source)
XLA Modules:
  0.0 97.3 jit_solution(13291557878841202849)
XLA Ops:
  0.6 0.0 copy-start
  0.6 0.0 copy-start.1
  0.7 0.9 copy-done.1
  1.6 0.0 copy-start.3
  1.6 0.9 copy-done.3
  2.5 0.0 copy-start.5
  2.5 0.9 copy-done.5
  3.5 0.0 copy-start.7
  3.5 0.9 copy-done.7
  4.4 0.0 copy-start.9
  4.4 0.2 first.1
  4.6 3.1 %collective-permute-start = (f32[15,8,128]{2,1,0:T(8,128)S(1)}, f32[15,8,128]{2,1,0:T(8,128)S(1)}, u32[]{:S(2)}, u32[]{:S(2)}) collective-permute-start(f32[15,8,128]{2,1,0:T(8,128)S(1)} %get-tuple-element.14), channel_id=1, source_target_pairs={{0,1},{1,2},{2,3},{3,4},{4,5},{5,6},{6,7},{7,8},{8,9},{9,10},{10,1... | collective-permute-start | bytes 184328 | tf_op jit(solution)/shard_map/ppermute | solution.py:515
  7.7 0.0 copy-start.6
  7.7 0.0 copy-start.8
  7.7 0.0 collective-permute-start.1
  7.7 1.3 %collective-permute-done.before = f32[15,8,128]{2,1,0:T(8,128)S(1)} collective-permute-done((f32[15,8,128]{2,1,0:T(8,128)S(1)}, f32[15,8,128]{2,1,0:T(8,128)S(1)}, u32[]{:S(2)}, u32[]{:S(2)}) %collective-permute-start) | collective-permute-done | bytes 61472 | tf_op jit(solution)/shard_map/ppermute | solution.py:515
  9.0 3.6 %collective-permute-done.1.after = f32[15,8,128]{2,1,0:T(8,128)S(1)} collective-permute-done((f32[15,8,128]{2,1,0:T(8,128)S(1)}, f32[15,8,128]{2,1,0:T(8,128)S(1)}, u32[]{:S(2)}, u32[]{:S(2)}) %collective-permute-start.1) | collective-permute-done | bytes 61472 | tf_op jit(solution)/shard_map/ppermute | solution.py:516
  12.5 0.3 les_pack.1
  12.8 0.0 copy-start.10
  12.8 4.1 %collective-permute-start.2 = (f32[15,8,128]{2,1,0:T(8,128)S(1)}, f32[15,8,128]{2,1,0:T(8,128)S(1)}, u32[]{:S(2)}, u32[]{:S(2)}) collective-permute-start(f32[15,8,128]{2,1,0:T(8,128)S(1)} %get-tuple-element.16), channel_id=1, source_target_pairs={{0,16},{16,32},{32,48},{48,64},{64,80},{80,96},{96,112},{112,128},... | collective-permute-start | bytes 184328 | tf_op jit(solution)/shard_map/ppermute | solution.py:515
  17.0 12.2 %collective-permute-start.3 = (f32[15,8,128]{2,1,0:T(8,128)S(1)}, f32[15,8,128]{2,1,0:T(8,128)S(1)}, u32[]{:S(2)}, u32[]{:S(2)}) collective-permute-start(f32[15,8,128]{2,1,0:T(8,128)S(1)} %get-tuple-element.17), channel_id=1, source_target_pairs={{16,0},{32,16},{48,32},{64,48},{80,64},{96,80},{112,96},{128,112},... | collective-permute-start | bytes 184328 | tf_op jit(solution)/shard_map/ppermute | solution.py:516
  29.2 0.0 copy-done
  29.2 0.6 dynamic-slice_reduce_fusion
  29.8 0.1 reshape.34.sends
  29.9 0.0 collective-permute-done.2.from_left
  29.9 0.6 collective-permute-done.3.from_right
  30.4 0.0 copy-done.9
  30.4 0.0 copy-done.6
  30.4 0.0 copy-done.8
  30.5 0.0 copy-done.10
  30.5 5.3 %les.1 = (f32[3,128,128]{2,1,0:T(8,128)}, bf16[96,3,8,128]{3,2,1,0:T(8,128)(2,1)}) custom-call(s32[48]{0:T(128)S(1)} %reshape.34.sends, f32[3,128,128]{2,1,0:T(8,128)S(1)} %bitcast.17, f32[3,128,128]{2,1,0:T(8,128)S(1)} %bitcast.20, f32[15,8,128]{2,1,0:T(8,128)S(1)} %collective-permute-done.before, f32[15,8,128]{2,1,0:T(8,128)S(1)} %collective-permute-done.1.after, ...), custom_call_target="tpu_custom_call" | custom-call | tf_op jit(solution)/shard_map/les/pallas_call | solution.py:501
  35.8 0.0 copy-start.12
  35.8 7.7 %all-to-all-start = ((bf16[24,96,128]{2,1,0:T(8,128)(2,1)}), bf16[24,96,128]{2,1,0:T(8,128)(2,1)S(1)}, u32[]{:S(2)}, u32[]{:S(2)}) async-start(bf16[24,96,128]{2,1,0:T(8,128)(2,1)} %bitcast.5), calls=%async_computation | async-start | bytes 1179648 | tf_op jit(solution)/shard_map/all_to_all | solution.py:562
  43.5 1.7 %collective-permute-start.6 = (bf16[112,8,128]{2,1,0:T(8,128)(2,1)S(1)}, bf16[112,8,128]{2,1,0:T(8,128)(2,1)S(1)}, u32[]{:S(2)}, u32[]{:S(2)}) collective-permute-start(bf16[112,8,128]{2,1,0:T(8,128)(2,1)S(1)} %get-tuple-element.23), channel_id=1, source_target_pairs={{0,1},{1,2},{2,3},{3,4},{4,5},{5,6},{6,7},{7,8},{8,9},{9,10},{10,1... | collective-permute-start | bytes 688136 | tf_op jit(solution)/shard_map/ppermute | solution.py:515
  45.2 0.0 collective-permute-start.7
  45.2 0.0 copy-done.12
  45.2 0.1 copy.12
  45.3 0.1 reshape.40.refs
  45.4 0.0 copy-start.11
  45.4 22.9 %all-to-all-done = bf16[24,96,128]{2,1,0:T(8,128)(2,1)S(1)} async-done(((bf16[24,96,128]{2,1,0:T(8,128)(2,1)}), bf16[24,96,128]{2,1,0:T(8,128)(2,1)S(1)}, u32[]{:S(2)}, u32[]{:S(2)}) %all-to-all-start) | async-done | bytes 589856 | tf_op jit(solution)/shard_map/all_to_all | solution.py:562
  68.3 0.0 copy-done.11
  68.3 0.0 copy-start.2
  68.3 0.0 copy-start.4
  68.3 1.9 %blend.1 = (f32[2,3,16,8,128]{4,3,2,1,0:T(8,128)S(1)}, bf16[72,8,128]{2,1,0:T(8,128)(2,1)S(1)}, bf16[72,8,128]{2,1,0:T(8,128)(2,1)S(1)}) custom-call(s32[64]{0:T(128)S(1)} %reshape.40.refs, s32[16]{0:T(128)S(1)} %copy-done.11, bf16[96,3,8,128]{3,2,1,0:T(8,128)(2,1)S(1)} %bitcast.11), custom_call_target="tpu_custom_call" | custom-call | tf_op jit(solution)/shard_map/blend/pallas_call | solution.py:501
  70.2 1.9 %collective-permute-start.4 = (bf16[72,8,128]{2,1,0:T(8,128)(2,1)S(1)}, bf16[72,8,128]{2,1,0:T(8,128)(2,1)S(1)}, u32[]{:S(2)}, u32[]{:S(2)}) collective-permute-start(bf16[72,8,128]{2,1,0:T(8,128)(2,1)S(1)} %get-tuple-element.21), channel_id=1, source_target_pairs={{0,1},{1,2},{2,3},{3,4},{4,5},{5,6},{6,7},{7,8},{8,9},{9,10},{10,1... | collective-permute-start | bytes 442376 | tf_op jit(solution)/shard_map/ppermute | solution.py:515
  72.1 0.0 collective-permute-start.5
  72.1 0.0 collective-permute-done.6.caa_below
  72.1 0.0 collective-permute-done.7.caa_above
  72.1 2.1 %collective-permute-done.4.below = bf16[72,8,128]{2,1,0:T(8,128)(2,1)S(1)} collective-permute-done((bf16[72,8,128]{2,1,0:T(8,128)(2,1)S(1)}, bf16[72,8,128]{2,1,0:T(8,128)(2,1)S(1)}, u32[]{:S(2)}, u32[]{:S(2)}) %collective-permute-start.4) | collective-permute-done | bytes 147488 | tf_op jit(solution)/shard_map/ppermute | solution.py:515
  74.2 3.7 %collective-permute-done.5.above = bf16[72,8,128]{2,1,0:T(8,128)(2,1)S(1)} collective-permute-done((bf16[72,8,128]{2,1,0:T(8,128)(2,1)S(1)}, bf16[72,8,128]{2,1,0:T(8,128)(2,1)S(1)}, u32[]{:S(2)}, u32[]{:S(2)}) %collective-permute-start.5) | collective-permute-done | bytes 147488 | tf_op jit(solution)/shard_map/ppermute | solution.py:516
  77.8 0.0 copy-done.2
  77.8 0.0 copy-done.4
  77.9 0.6 caa_pack.1
  78.5 1.9 %collective-permute-start.8 = (bf16[72,8,128]{2,1,0:T(8,128)(2,1)S(1)}, bf16[72,8,128]{2,1,0:T(8,128)(2,1)S(1)}, u32[]{:S(2)}, u32[]{:S(2)}) collective-permute-start(bf16[72,8,128]{2,1,0:T(8,128)(2,1)S(1)} %get-tuple-element.24), channel_id=1, source_target_pairs={{0,16},{16,32},{32,48},{48,64},{64,80},{80,96},{96,112},{112,128},... | collective-permute-start | bytes 442376 | tf_op jit(solution)/shard_map/ppermute | solution.py:515
  80.4 5.5 %collective-permute-start.9 = (bf16[72,8,128]{2,1,0:T(8,128)(2,1)S(1)}, bf16[72,8,128]{2,1,0:T(8,128)(2,1)S(1)}, u32[]{:S(2)}, u32[]{:S(2)}) collective-permute-start(bf16[72,8,128]{2,1,0:T(8,128)(2,1)S(1)} %get-tuple-element.25), channel_id=1, source_target_pairs={{16,0},{32,16},{48,32},{64,48},{80,64},{96,80},{112,96},{128,112},... | collective-permute-start | bytes 442376 | tf_op jit(solution)/shard_map/ppermute | solution.py:516
  85.9 0.6 collective-permute-done.8.from_left
  86.5 1.5 %collective-permute-done.9.from_right = bf16[72,8,128]{2,1,0:T(8,128)(2,1)S(1)} collective-permute-done((bf16[72,8,128]{2,1,0:T(8,128)(2,1)S(1)}, bf16[72,8,128]{2,1,0:T(8,128)(2,1)S(1)}, u32[]{:S(2)}, u32[]{:S(2)}) %collective-permute-start.9) | collective-permute-done | bytes 147488 | tf_op jit(solution)/shard_map/ppermute | solution.py:516
  87.9 9.3 %caa.1 = f32[4,128,128]{2,1,0:T(8,128)} custom-call(f32[4,128,128]{2,1,0:T(8,128)S(1)} %bitcast.10, f32[3,128,128]{2,1,0:T(8,128)S(1)} %bitcast.14, f32[2,3,16,8,128]{4,3,2,1,0:T(8,128)S(1)} %get-tuple-element.20.own, bf16[72,8,128]{2,1,0:T(8,128)(2,1)S(1)} %collective-permute-done.4.below, bf16[72,8,128]{2,1,0:T(8,128)(2,1)S(1)} %collective-permute-done.5.above, ...), custom_call_target="tpu_custom_call" | custom-call | tf_op jit(solution)/shard_map/caa/pallas_call | solution.py:501
Async XLA Ops:
  0.6 28.6 %copy-start = (s32[48,24,2]{0,2,1:T(2,128)S(1)}, s32[48,24,2]{0,2,1:T(2,128)}, u32[]{:S(2)}) copy-start(s32[48,24,2]{0,2,1:T(2,128)} %param.15) | copy-start | bytes 27652
  0.6 1.0 copy-start.1
  1.6 0.9 copy-start.3
  2.5 0.9 copy-start.5
  3.5 0.9 copy-start.7
  4.4 26.1 %copy-start.9 = (bf16[2,256,256]{2,1,0:T(8,128)(2,1)S(1)}, bf16[2,256,256]{2,1,0:T(8,128)(2,1)}, u32[]{:S(2)}) copy-start(bf16[2,256,256]{2,1,0:T(8,128)(2,1)} %constant.20.clone.weights) | copy-start | bytes 786436
  4.6 4.4 %collective-permute-start = (f32[15,8,128]{2,1,0:T(8,128)S(1)}, f32[15,8,128]{2,1,0:T(8,128)S(1)}, u32[]{:S(2)}, u32[]{:S(2)}) collective-permute-start(f32[15,8,128]{2,1,0:T(8,128)S(1)} %get-tuple-element.14), channel_id=1, source_target_pairs={{0,1},{1,2},{2,3},{3,4},{4,5},{5,6},{6,7},{7,8},{8,9},{9,10},{10,1... | collective-permute-start | bytes 184328 | tf_op jit(solution)/shard_map/ppermute | solution.py:515
  7.7 22.8 %copy-start.6 = (f32[3,8,16,128]{3,2,1,0:T(8,128)S(1)}, f32[3,8,16,128]{3,2,1,0:T(8,128)}, u32[]{:S(2)}) copy-start(f32[3,8,16,128]{3,2,1,0:T(8,128)} %param.9) | copy-start | bytes 589828
  7.7 22.8 %copy-start.8 = (f32[3,8,16,128]{3,2,1,0:T(8,128)S(1)}, f32[3,8,16,128]{3,2,1,0:T(8,128)}, u32[]{:S(2)}) copy-start(f32[3,8,16,128]{3,2,1,0:T(8,128)} %param.10) | copy-start | bytes 589828
  7.7 4.9 %collective-permute-start.1 = (f32[15,8,128]{2,1,0:T(8,128)S(1)}, f32[15,8,128]{2,1,0:T(8,128)S(1)}, u32[]{:S(2)}, u32[]{:S(2)}) collective-permute-start(f32[15,8,128]{2,1,0:T(8,128)S(1)} %get-tuple-element.15), channel_id=1, source_target_pairs={{1,0},{2,1},{3,2},{4,3},{5,4},{6,5},{7,6},{8,7},{9,8},{10,9},{11,1... | collective-permute-start | bytes 184328 | tf_op jit(solution)/shard_map/ppermute | solution.py:516
  12.8 17.6 %copy-start.10 = (f32[16,8,128]{2,1,0:T(8,128)S(1)}, f32[16,8,128]{2,1,0:T(8,128)}, u32[]{:S(2)}) copy-start(f32[16,8,128]{2,1,0:T(8,128)} %constant.21.clone.coef) | copy-start | bytes 196612
  12.8 17.0 %collective-permute-start.2 = (f32[15,8,128]{2,1,0:T(8,128)S(1)}, f32[15,8,128]{2,1,0:T(8,128)S(1)}, u32[]{:S(2)}, u32[]{:S(2)}) collective-permute-start(f32[15,8,128]{2,1,0:T(8,128)S(1)} %get-tuple-element.16), channel_id=1, source_target_pairs={{0,16},{16,32},{32,48},{48,64},{64,80},{80,96},{96,112},{112,128},... | collective-permute-start | bytes 184328 | tf_op jit(solution)/shard_map/ppermute | solution.py:515
  17.0 13.5 %collective-permute-start.3 = (f32[15,8,128]{2,1,0:T(8,128)S(1)}, f32[15,8,128]{2,1,0:T(8,128)S(1)}, u32[]{:S(2)}, u32[]{:S(2)}) collective-permute-start(f32[15,8,128]{2,1,0:T(8,128)S(1)} %get-tuple-element.17), channel_id=1, source_target_pairs={{16,0},{32,16},{48,32},{64,48},{80,64},{96,80},{112,96},{128,112},... | collective-permute-start | bytes 184328 | tf_op jit(solution)/shard_map/ppermute | solution.py:516
  35.8 9.4 %copy-start.12 = (s32[16,4]{0,1:T(4,128)S(1)}, s32[16,4]{0,1:T(4,128)}, u32[]{:S(2)}) copy-start(s32[16,4]{0,1:T(4,128)} %param.13) | copy-start | bytes 772
  35.8 32.5 %all-to-all-start = ((bf16[24,96,128]{2,1,0:T(8,128)(2,1)}), bf16[24,96,128]{2,1,0:T(8,128)(2,1)S(1)}, u32[]{:S(2)}, u32[]{:S(2)}) async-start(bf16[24,96,128]{2,1,0:T(8,128)(2,1)} %bitcast.5), calls=%async_computation | async-start | bytes 1179648 | tf_op jit(solution)/shard_map/all_to_all | solution.py:562
  43.5 28.6 %collective-permute-start.6 = (bf16[112,8,128]{2,1,0:T(8,128)(2,1)S(1)}, bf16[112,8,128]{2,1,0:T(8,128)(2,1)S(1)}, u32[]{:S(2)}, u32[]{:S(2)}) collective-permute-start(bf16[112,8,128]{2,1,0:T(8,128)(2,1)S(1)} %get-tuple-element.23), channel_id=1, source_target_pairs={{0,1},{1,2},{2,3},{3,4},{4,5},{5,6},{6,7},{7,8},{8,9},{9,10},{10,1... | collective-permute-start | bytes 688136 | tf_op jit(solution)/shard_map/ppermute | solution.py:515
  45.2 26.9 %collective-permute-start.7 = (bf16[112,8,128]{2,1,0:T(8,128)(2,1)S(1)}, bf16[112,8,128]{2,1,0:T(8,128)(2,1)S(1)}, u32[]{:S(2)}, u32[]{:S(2)}) collective-permute-start(bf16[112,8,128]{2,1,0:T(8,128)(2,1)S(1)} %get-tuple-element.23), channel_id=1, source_target_pairs={{1,0},{2,1},{3,2},{4,3},{5,4},{6,5},{7,6},{8,7},{9,8},{10,9},{11,1... | collective-permute-start | bytes 688136 | tf_op jit(solution)/shard_map/ppermute | solution.py:516
  45.4 23.0 %copy-start.11 = (s32[16]{0:T(128)S(1)}, s32[16]{0:T(128)}, u32[]{:S(2)}) copy-start(s32[16]{0:T(128)} %offsets.1) | copy-start | bytes 196
  68.3 9.5 %copy-start.2 = (f32[4,8,16,128]{3,2,1,0:T(8,128)S(1)}, f32[4,8,16,128]{3,2,1,0:T(8,128)}, u32[]{:S(2)}) copy-start(f32[4,8,16,128]{3,2,1,0:T(8,128)} %param.11) | copy-start | bytes 786436
  68.3 9.5 %copy-start.4 = (f32[3,8,16,128]{3,2,1,0:T(8,128)S(1)}, f32[3,8,16,128]{3,2,1,0:T(8,128)}, u32[]{:S(2)}) copy-start(f32[3,8,16,128]{3,2,1,0:T(8,128)} %param.12) | copy-start | bytes 589828
  70.2 4.0 %collective-permute-start.4 = (bf16[72,8,128]{2,1,0:T(8,128)(2,1)S(1)}, bf16[72,8,128]{2,1,0:T(8,128)(2,1)S(1)}, u32[]{:S(2)}, u32[]{:S(2)}) collective-permute-start(bf16[72,8,128]{2,1,0:T(8,128)(2,1)S(1)} %get-tuple-element.21), channel_id=1, source_target_pairs={{0,1},{1,2},{2,3},{3,4},{4,5},{5,6},{6,7},{7,8},{8,9},{9,10},{10,1... | collective-permute-start | bytes 442376 | tf_op jit(solution)/shard_map/ppermute | solution.py:515
  72.1 5.8 %collective-permute-start.5 = (bf16[72,8,128]{2,1,0:T(8,128)(2,1)S(1)}, bf16[72,8,128]{2,1,0:T(8,128)(2,1)S(1)}, u32[]{:S(2)}, u32[]{:S(2)}) collective-permute-start(bf16[72,8,128]{2,1,0:T(8,128)(2,1)S(1)} %get-tuple-element.22), channel_id=1, source_target_pairs={{1,0},{2,1},{3,2},{4,3},{5,4},{6,5},{7,6},{8,7},{9,8},{10,9},{11,1... | collective-permute-start | bytes 442376 | tf_op jit(solution)/shard_map/ppermute | solution.py:516
  78.5 8.0 %collective-permute-start.8 = (bf16[72,8,128]{2,1,0:T(8,128)(2,1)S(1)}, bf16[72,8,128]{2,1,0:T(8,128)(2,1)S(1)}, u32[]{:S(2)}, u32[]{:S(2)}) collective-permute-start(bf16[72,8,128]{2,1,0:T(8,128)(2,1)S(1)} %get-tuple-element.24), channel_id=1, source_target_pairs={{0,16},{16,32},{32,48},{48,64},{64,80},{80,96},{96,112},{112,128},... | collective-permute-start | bytes 442376 | tf_op jit(solution)/shard_map/ppermute | solution.py:515
  80.4 7.6 %collective-permute-start.9 = (bf16[72,8,128]{2,1,0:T(8,128)(2,1)S(1)}, bf16[72,8,128]{2,1,0:T(8,128)(2,1)S(1)}, u32[]{:S(2)}, u32[]{:S(2)}) collective-permute-start(bf16[72,8,128]{2,1,0:T(8,128)(2,1)S(1)} %get-tuple-element.25), channel_id=1, source_target_pairs={{16,0},{32,16},{48,32},{64,48},{80,64},{96,80},{112,96},{128,112},... | collective-permute-start | bytes 442376 | tf_op jit(solution)/shard_map/ppermute | solution.py:516

commit v2 on v1

v2 whole, which is shorter than its diff:
```python
import functools

import jax
import jax.numpy as jnp
import numpy as np
from jax import lax
from jax.experimental import pallas as pl
from jax.experimental.pallas import tpu as pltpu
from jax.sharding import PartitionSpec as P


les_step = 0.02
caa_step = 0.01
mach_number = 0.5

STREAM = ("sec", "gx")
F32 = jnp.float32
BF16 = jnp.bfloat16
VMEM_LIMIT = 24 * 1024 * 1024


def slope_table():
    points = np.array([-1.0, -(0.2**0.5), 0.2**0.5, 1.0])
    identity = np.eye(4)
    differences = points[:, None] - points[None, :] + identity
    inverse_weights = 1.0 / np.prod(differences, axis=1)
    slope_matrix = inverse_weights[None, :] / inverse_weights[:, None] / differences
    slope_matrix = slope_matrix * (1.0 - identity)
    return slope_matrix - identity * slope_matrix.sum(axis=1)[:, None]


DM = slope_table() + np.diag([3.0, 0.0, 0.0, -3.0])
DM[np.abs(DM) < 1e-12] = 0.0


def lane_matrix(run):
    result = np.zeros((128, 128))
    for e in range(32):
        result[4 * e : 4 * e + 4, 4 * e : 4 * e + 4] = DM.T
        if (4 * e) % run:
            result[4 * e - 1, 4 * e] = -3.0
        if (4 * e + 4) % run:
            result[4 * e + 4, 4 * e + 3] = 3.0
    return result


def split_matrix(run):
    full = lane_matrix(run).astype(np.float32)
    high = full.astype(jnp.bfloat16)
    low = (full - high.astype(np.float32)).astype(jnp.bfloat16)
    return np.block([[high, low], [high, np.zeros_like(low)]])


OFFSETS = (-3, -2, -1, 1, 2, 3)
RAD, AZT, AZP, AZN, EDGE_M, EDGE_T = 0, 6, 12, 13, 14, 15
LES_WIDTH, CAA_WIDTH = 4, 16


def coefficients(width):
    c = np.zeros((16, 8, 128), np.float32)
    for n, k in enumerate(OFFSETS):
        for s in range(8):
            i = s % 4
            if 0 <= i + k <= 3:
                c[RAD + n, s, :] = DM[i, i + k]
        for lane in range(128):
            i = (lane % 64) // width
            if i <= 3 and 0 <= i + k <= 3:
                c[AZT + n, :, lane] = DM[i, i + k]
    c[RAD + OFFSETS.index(1), 3, :] = 3.0
    c[RAD + OFFSETS.index(-1), 4, :] = -3.0
    for lane in range(128):
        i = (lane % 64) // width
        if i == 0:
            c[AZP, :, lane] = -3.0
        if i == 3:
            c[AZN, :, lane] = 3.0
    c[EDGE_M, :, 127] = 3.0
    c[EDGE_M, :, 0] = -3.0
    for i in range(4):
        c[EDGE_T, :, width * i] = -3.0
        c[EDGE_T, :, 63 + width * (i + 1)] = 3.0
    return c


def lanes_of():
    return lax.broadcasted_iota(jnp.int32, (8, 128), 1)


def lane_roll(x, shift):
    shift %= 128
    return pltpu.roll(x, shift, axis=1) if shift else x


def times(rows, weights):
    x = jnp.concatenate(rows, axis=0)
    high = x.astype(BF16)
    low = (x - high.astype(F32)).astype(BF16)
    y = jnp.dot(jnp.concatenate([high, low], axis=1), weights, preferred_element_type=F32)
    y = y[:, :128] + y[:, 128:]
    return [y[8 * n : 8 * n + 8] for n in range(len(rows))]


def edge_main(tile, i, width):
    return jnp.where(lanes_of() == 127, lane_roll(tile, 127 - width * i), lane_roll(tile, 65 - width * (i + 1)))


def stream_main(fields, halos, weights, coef, width):
    out = times([row for rows in fields for row in rows], weights)
    results = []
    at = 0
    for rows, tiles in zip(fields, halos):
        result = []
        for n in range(len(rows)):
            result.append(out[at] + coef[EDGE_M] * edge_main(tiles[n // 4], n % 4, width))
            at += 1
        results.append(result)
    return results


def stream_halo(fields, halos, weights, coef, width):
    lane = lanes_of()
    out = times([tile for tiles in halos for tile in tiles], weights)
    results = []
    at = 0
    for rows, tiles in zip(fields, halos):
        result = []
        for e in range(len(tiles)):
            edge = None
            for i in range(4):
                row, near, far = rows[4 * e + i], width * i, 63 + width * (i + 1)
                low, high = lane_roll(row, near + 1), lane_roll(row, far)
                edge = low if edge is None else jnp.where(lane == near, low, edge)
                edge = jnp.where(lane == far, high, edge)
            result.append(out[at] + coef[EDGE_T] * edge)
            at += 1
        results.append(result)
    return results


def azimuth_main(rows, before, after):
    out = []
    for e in range(len(rows) // 4):
        f = rows[4 * e : 4 * e + 4]
        prev = before if e == 0 else rows[4 * e - 1]
        following = after if 4 * e + 4 == len(rows) else rows[4 * e + 4]
        a, b, c = float(DM[0, 1]), float(DM[0, 2]), float(DM[0, 3])
        d, g, h = float(DM[1, 0]), float(DM[1, 2]), float(DM[1, 3])
        out.append(a * f[1] + b * f[2] + c * f[3] - 3.0 * prev)
        out.append(d * f[0] + g * f[2] + h * f[3])
        out.append(-(h * f[0] + g * f[1] + d * f[3]))
        out.append(3.0 * following - (c * f[0] + b * f[1] + a * f[2]))
    return out


def azimuth_halo(tiles, before, after, coef, width):
    out = []
    for e, tile in enumerate(tiles):
        prev = before if e == 0 else tiles[e - 1]
        following = after if e + 1 == len(tiles) else tiles[e + 1]
        total = coef[AZP] * lane_roll(prev, -3 * width) + coef[AZN] * lane_roll(following, 3 * width)
        for n, k in enumerate(OFFSETS):
            total = total + coef[AZT + n] * lane_roll(tile, -width * k)
        out.append(total)
    return out


def radial(tiles, coef):
    out = []
    for tile in tiles:
        total = None
        for n, k in enumerate(OFFSETS):
            term = coef[RAD + n] * pltpu.roll(tile, (-k) % 8, axis=0)
            total = term if total is None else total + term
        out.append(total)
    return out


def pack(rows, last, width):
    lane = lanes_of()
    out = None
    for g, row in enumerate(rows):
        moved = lane_roll(row, width * g + (width if last else 0))
        out = moved if out is None else jnp.where(lane >= width * g, moved, out)
    return out


def halo_tile(from_left, from_right, n, width):
    count = 32 // width
    left, right = from_left[n // count].astype(F32), from_right[n // count].astype(F32)
    shift = 4 * width * (n % count)
    left, right = lane_roll(left, 64 - shift), lane_roll(right, -shift)
    lane = lanes_of()
    if width == 16:
        return jnp.where(lane < 64, right, left)
    both = jnp.where(lane < 64, right, left)
    return jnp.where(lane % 64 < 4 * width, both, 0.0)


def turn(tiles):
    group = lanes_of() // 8
    tiles = list(tiles)
    for bit in range(4):
        step = 1 << bit
        high = (group & step) != 0
        for p in range(16):
            if p & step:
                continue
            x, y = tiles[p], tiles[p | step]
            tiles[p] = jnp.where(high, lane_roll(y, 8 * step), x)
            tiles[p | step] = jnp.where(high, y, lane_roll(x, -8 * step))
    return tiles


def column(ref, c, az, sector):
    return ref[c, pl.ds(az, 8, stride=sector), :]


def first_kernel(sector, u_far, lm_far, low, high, u, lm, arrived):
    copies = [pltpu.make_async_copy(a, b, arrived.at[n]) for n, (a, b) in enumerate([(u_far, u), (lm_far, lm)])]
    for copy in copies:
        copy.start()
    for copy in copies:
        copy.wait()
    for c in range(3):
        for i in range(4):
            low[4 * c + i] = column(u, c, i, sector)
            high[4 * c + i] = column(u, c, sector - 4 + i, sector)
        low[12 + c] = column(lm, c, 0, sector)
        high[12 + c] = column(lm, c, sector - 1, sector)


def narrow_kernel(sector, w, m, both):
    for f in range(7):
        for az in range(sector):
            value = column(w, f, az, sector) if f < 4 else column(m, f - 4, az, sector)
            both[f * sector + az] = value.astype(BF16)


def les_pack_kernel(sector, u, lm, before, after, first, last):
    entries = []
    for c in range(3):
        for e in range(-1, 5):
            if e < 0:
                entries.append([(before, 4 * c + i) for i in range(4)])
            elif e == 4:
                entries.append([(after, 4 * c + i) for i in range(4)])
            else:
                entries.append([(u, (c, pl.ds(4 * e + i, 8, stride=sector), slice(None))) for i in range(4)])
    for c in range(3):
        for e in range(4):
            entries.append([(lm, (c, pl.ds(4 * e + i, 8, stride=sector), slice(None))) for i in range(4)])
    for n in range(4):
        rows = [ref[at] for entry in entries[8 * n : 8 * n + 8] for ref, at in entry]
        first[n] = pack(rows, False, LES_WIDTH)
        last[n] = pack(rows, True, LES_WIDTH)


def les_element(um, ut, mm, e, weights, coef, with_flux):
    rows = [[um[c, 4 * e + i] for i in range(4)] for c in range(3)]
    tiles = [[ut[c, e]] for c in range(3)]
    prev = [um[c, 4 * e - 1] for c in range(3)]
    following = [um[c, 4 * e + 4] for c in range(3)]
    metric = [[mm[c, 4 * e + i] for i in range(4)] for c in range(3)]
    fields, halos = list(rows), list(tiles)
    if with_flux:
        fields += [[x * y for x, y in zip(rows[0], rows[c])] for c in range(3)]
        halos += [[tiles[0][0] * tiles[c][0]] for c in range(3)]
    stream = stream_main(fields, halos, weights[0], coef, LES_WIDTH)
    scaled = lambda j, values: [a * b for a, b in zip(metric[j], values)]
    slopes = [[scaled(0, stream[c]) for c in range(3)], [], []]
    fluxes = [[scaled(0, stream[3 + c]) for c in range(3)] if with_flux else [], [], []]
    for c in range(3):
        slopes[1].append(scaled(1, azimuth_main(rows[c], prev[c], following[c])))
        slopes[2].append(scaled(2, radial(rows[c], coef)))
        if with_flux:
            product = [x * y for x, y in zip(rows[1], rows[c])]
            fluxes[1].append(scaled(1, azimuth_main(product, prev[1] * prev[c], following[1] * following[c])))
            fluxes[2].append(scaled(2, radial([x * y for x, y in zip(rows[2], rows[c])], coef)))
    return rows, tiles, fields, halos, slopes, fluxes


def les_change(rows, slopes, fluxes, c, i):
    total = None
    for j in range(3):
        term = fluxes[j][c][i] + rows[j][i] * slopes[j][c][i]
        total = term if total is None else total + term
    return (0.5 * les_step) * total


def lamb_of(rows, slopes, lamb, e):
    for i in range(4):
        first = slopes[1][2][i] - slopes[2][1][i]
        second = slopes[2][0][i] - slopes[0][2][i]
        third = slopes[0][1][i] - slopes[1][0][i]
        lamb[0, 4 * e + i] = second * rows[2][i] - third * rows[1][i]
        lamb[1, 4 * e + i] = third * rows[0][i] - first * rows[2][i]
        lamb[2, 4 * e + i] = first * rows[1][i] - second * rows[0][i]


def les_kernel(sector, sends, u, lm, before, after, from_left, from_right, weights, coef, sent, um1, ut1, um, ut, mm, mt, lamb, blk):
    for c in range(3):
        for i in range(4):
            um[c, i] = before[4 * c + i]
            um[c, 4 + sector + i] = after[4 * c + i]
        mm[c, 3] = before[12 + c]
        mm[c, 4 + sector] = after[12 + c]
        for az in range(sector):
            um[c, 4 + az] = column(u, c, az, sector)
            mm[c, 4 + az] = column(lm, c, az, sector)
        for e in range(6):
            ut[c, e] = halo_tile(from_left, from_right, 6 * c + e, LES_WIDTH)
        for e in range(4):
            mt[c, e + 1] = halo_tile(from_left, from_right, 18 + 4 * c + e, LES_WIDTH)

    tiles, fields, ends = [], [], []
    for e, i in ((0, 3), (5, 0)):
        near = 4 if e == 0 else 3 + sector
        rows = [um[c, 4 * e + i] for c in range(3)]
        others = [[um[c, 4 * e + k] for k in range(4)] for c in range(3)]
        beyond = [um[c, near] for c in range(3)]
        halo = [ut[c, e] for c in range(3)]
        fields += rows + [rows[0] * rows[c] for c in range(3)]
        tiles += [(t, i) for t in halo + [halo[0] * halo[c] for c in range(3)]]
        ends.append((4 * e + i, i, rows, others, beyond))
    out = times(fields, weights[0])
    out = [y + coef[EDGE_M] * edge_main(t, i, LES_WIDTH) for y, (t, i) in zip(out, tiles)]
    for n, (at, i, rows, others, beyond) in enumerate(ends):
        metric = [mm[j, at] for j in range(3)]
        for c in range(3):
            slope = azimuth_main(others[c], beyond[c], beyond[c])[i]
            flux = azimuth_main([x * y for x, y in zip(others[1], others[c])], *[beyond[1] * beyond[c]] * 2)[i]
            total = metric[0] * (out[6 * n + 3 + c] + rows[0] * out[6 * n + c]) + metric[1] * (flux + rows[1] * slope)
            slope, flux = radial([rows[c], rows[2] * rows[c]], coef)
            total = total + metric[2] * (flux + rows[2] * slope)
            um1[c, at] = rows[c] - (0.5 * les_step) * total
        if i == 3:
            for c in range(3):
                for k in range(3):
                    um1[c, k] = rows[c]
                    um1[c, 5 + sector + k] = rows[c]

    @pl.loop(1, 5)
    def _(e):
        rows, tiles, fields, halos, slopes, fluxes = les_element(um, ut, mm, e, weights, coef, True)
        lamb_of(rows, slopes, lamb, e)
        for c in range(3):
            for i in range(4):
                um1[c, 4 * e + i] = rows[c][i] - les_change(rows, slopes, fluxes, c, i)
        low = [ut[c, e - 1] for c in range(3)]
        high = [ut[c, e + 1] for c in range(3)]
        metric = [mt[c, e] for c in range(3)]
        stream = stream_halo(fields, halos, weights[1], coef, LES_WIDTH)
        for c in range(3):
            total = metric[0] * (stream[3 + c][0] + tiles[0][0] * stream[c][0])
            slope = azimuth_halo(tiles[c], low[c], high[c], coef, LES_WIDTH)[0]
            product = tiles[1][0] * tiles[c][0]
            flux = azimuth_halo([product], low[1] * low[c], high[1] * high[c], coef, LES_WIDTH)[0]
            total = total + metric[1] * (flux + tiles[1][0] * slope)
            slope, flux = radial([tiles[c][0], tiles[2][0] * tiles[c][0]], coef)
            total = total + metric[2] * (flux + tiles[2][0] * slope)
            ut1[c, e - 1] = tiles[c][0] - (0.5 * les_step) * total

    def blocks(step):
        for c in range(3):
            tiles = turn([lamb[c, 4 + az] for az in range(sector)])
            for j in range(16):
                blk[j, 3 * step + c] = tiles[j].astype(BF16)

    blocks(0)

    @pl.loop(1, 5)
    def _(e):
        rows, _, _, _, slopes, _ = les_element(um1, Shifted(ut1), mm, e, weights, coef, False)
        lamb_of(rows, slopes, lamb, e)

    blocks(1)
    for n in range(sends.shape[0]):
        index = jnp.maximum(sends[n], 0)
        for k in range(6):
            sent[n, k] = blk[index, k]


class Shifted:
    def __init__(self, ref):
        self.ref = ref

    def __getitem__(self, at):
        return self.ref[at[0], at[1] - 1]


def les_out_kernel(sector, lm, um1, ut1, weights, coef, out, mm):
    for c in range(3):
        for az in range(sector):
            mm[c, 4 + az] = column(lm, c, az, sector)

    @pl.loop(1, 5)
    def _(e):
        rows, _, _, _, slopes, fluxes = les_element(um1, Shifted(ut1), mm, e, weights, coef, True)
        for c in range(3):
            for i in range(4):
                out[c, pl.ds(4 * (e - 1) + i, 8, stride=sector), :] = rows[c][i] - les_change(rows, slopes, fluxes, c, i)


def blend_kernel(sector, refs, offsets, got, own, up, down, mixed):
    for j in range(16):
        a = jnp.clip(refs[4 * j] * 2 + refs[4 * j + 1], 0, got.shape[0] - 1)
        b = jnp.clip(refs[4 * j + 2] * 2 + refs[4 * j + 3], 0, got.shape[0] - 1)
        fraction = offsets[j].astype(F32)
        for k in range(6):
            blend = (8.0 - fraction) * got[a, k].astype(F32) + fraction * got[b, k].astype(F32)
            mixed[k, j] = blend * 0.125
    for step in range(2):
        for c in range(3):
            tiles = turn([mixed[3 * step + c, j] for j in range(16)])
            for az in range(sector):
                own[step, c, az] = tiles[az]
                narrow = tiles[az].astype(BF16)
                if step == 0:
                    up[c * 16 + az] = narrow
                    down[c * 16 + az] = narrow
                elif az >= 8:
                    up[48 + c * 8 + az - 8] = narrow
                else:
                    down[48 + c * 8 + az] = narrow


def pack_entries(entries, first, last):
    for n in range(len(entries) // 2):
        rows = [ref[at].astype(F32) for ref, at in entries[2 * n] + entries[2 * n + 1]]
        first[n] = pack(rows, False, CAA_WIDTH).astype(BF16)
        last[n] = pack(rows, True, CAA_WIDTH).astype(BF16)


def state_pack_kernel(sector, below, above, both, first, last):
    entries = []
    for f in range(7):
        for e in range(12):
            ref = (below, both, above)[e // 4]
            entries.append([(ref, f * sector + 4 * (e % 4) + i) for i in range(4)])
    pack_entries(entries, first, last)


def source_pack_kernel(sector, own, below, above, first, last):
    entries = []
    for c in range(3):
        for e in range(12):
            if 4 <= e < 8:
                entries.append([(own, (0, c, 4 * (e - 4) + i)) for i in range(4)])
            else:
                entries.append([(below if e < 4 else above, c * 16 + 4 * (e % 4) + i) for i in range(4)])
    for c in range(3):
        for e in range(2, 10):
            if 4 <= e < 8:
                entries.append([(own, (1, c, 4 * (e - 4) + i)) for i in range(4)])
            elif e < 4:
                entries.append([(below, 48 + c * 8 + 4 * (e - 2) + i) for i in range(4)])
            else:
                entries.append([(above, 48 + c * 8 + 4 * (e - 8) + i) for i in range(4)])
    pack_entries(entries, first, last)


CAA_RANGES = ((0, 12), (1, 11), (1, 11), (2, 10), (2, 10), (3, 9), (3, 9), (4, 8))


def caa_kernel(
    sector, w, m, own, below, above, caa_below, caa_above, state_left, state_right, from_left, from_right, weights, coef,
    out, wm, wt, mm, mt, sm, st,
):
    w_main, w_halo = weights[0], weights[1]

    for f in range(7):
        for az in range(3 * sector):
            if az < sector:
                value = caa_below[f * sector + az].astype(F32)
            elif az < 2 * sector:
                value = column(w, f, az - sector, sector) if f < 4 else column(m, f - 4, az - sector, sector)
            else:
                value = caa_above[f * sector + az - 2 * sector].astype(F32)
            if f < 4:
                wm[0, f, az] = value
            else:
                mm[f - 4, az] = value * caa_step
        for e in range(12):
            value = halo_tile(state_left, state_right, 12 * f + e, CAA_WIDTH)
            if f < 4:
                wt[0, f, e] = value
            else:
                mt[f - 4, e] = value * caa_step
    for c in range(3):
        for az in range(16):
            sm[0, c, az] = below[c * 16 + az].astype(F32) * caa_step
            sm[0, c, 16 + az] = own[0, c, az] * caa_step
            sm[0, c, 32 + az] = above[c * 16 + az].astype(F32) * caa_step
            sm[1, c, 16 + az] = own[1, c, az] * caa_step
        for az in range(8):
            sm[1, c, 8 + az] = below[48 + c * 8 + az].astype(F32) * caa_step
            sm[1, c, 32 + az] = above[48 + c * 8 + az].astype(F32) * caa_step
        for e in range(12):
            st[0, c, e] = halo_tile(from_left, from_right, 12 * c + e, CAA_WIDTH) * caa_step
        for e in range(8):
            st[1, c, 2 + e] = halo_tile(from_left, from_right, 36 + 8 * c + e, CAA_WIDTH) * caa_step

    def pair(now, source, e, final):
        rows = [[wm[now, f, 4 * e + i] for i in range(8)] for f in range(4)]
        tiles = [[wt[now, f, e + n] for n in range(2)] for f in range(4)]
        below, above = jnp.maximum(4 * e - 1, 0), jnp.minimum(4 * e + 8, 47)
        tile_below, tile_above = jnp.maximum(e - 1, 0), jnp.minimum(e + 2, 11)

        def rates(values, metric, sources, stream, around, up):
            p, v0, v1, v2 = values
            count = len(p)
            azimuth_p, azimuth_v = around
            radial_p, radial_v = up
            for n in range(count):
                m0, m1, m2 = metric[0](n), metric[1](n), metric[2](n)
                half = mach_number * m0
                yield (
                    n,
                    p[n] - m0 * stream[0][n] - m1 * azimuth_v[n] - m2 * radial_v[n],
                    v0[n] - m0 * stream[1][n] + sources[0](n),
                    v1[n] - half * stream[2][n] - m1 * azimuth_p[n] + sources[1](n),
                    v2[n] - half * stream[3][n] - m2 * radial_p[n] + sources[2](n),
                )

        def mixed(values):
            p, v0, v1, v2 = values
            return [
                [mach_number * a + b for a, b in zip(p, v0)],
                [mach_number * b + a for a, b in zip(p, v0)],
                v1,
                v2,
            ]

        fields, halos = mixed(rows), mixed(tiles)
        stream = stream_main(fields, halos, w_main, coef, CAA_WIDTH)
        around = [azimuth_main(rows[f], wm[now, f, below], wm[now, f, above]) for f in (0, 2)]
        up = [radial(rows[f], coef) for f in (0, 3)]
        metric = [lambda n, c=c: mm[c, 4 * e + n] for c in range(3)]
        sources = [lambda n, c=c: sm[source, c, 4 * e + n] for c in range(3)]
        for n, *values in rates(rows, metric, sources, stream, around, up):
            for f in range(4):
                if final:
                    out[f, pl.ds(4 * e + n - 16, 8, stride=sector), :] = values[f]
                else:
                    wm[1 - now, f, 4 * e + n] = values[f]
        if not final:
            stream = stream_halo(fields, halos, w_halo, coef, CAA_WIDTH)
            around = [azimuth_halo(tiles[f], wt[now, f, tile_below], wt[now, f, tile_above], coef, CAA_WIDTH) for f in (0, 2)]
            up = [radial(tiles[f], coef) for f in (0, 3)]
            metric = [lambda n, c=c: mt[c, e + n] for c in range(3)]
            sources = [lambda n, c=c: st[source, c, e + n] for c in range(3)]
            for n, *values in rates(tiles, metric, sources, stream, around, up):
                for f in range(4):
                    wt[1 - now, f, e + n] = values[f]

    for step, (start, stop) in enumerate(CAA_RANGES):

        @pl.loop(0, (stop - start) // 2)
        def _(n):
            pair(step % 2, step // 4, start + 2 * n, step == 7)


def call(kernel, name, outs, *args, smem=0, far=0, scratch=()):
    whole = pl.BlockSpec(memory_space=pltpu.VMEM)
    specs = [pl.BlockSpec(memory_space=pltpu.SMEM)] * smem + [pl.BlockSpec(memory_space=pltpu.HBM)] * far
    return pl.pallas_call(
        kernel,
        name=name,
        out_shape=[jax.ShapeDtypeStruct(shape, dtype) for shape, dtype in outs],
        in_specs=specs + [whole] * (len(args) - smem - far),
        out_specs=[whole] * len(outs),
        scratch_shapes=list(scratch),
        compiler_params=pltpu.CompilerParams(vmem_limit_bytes=None if far else VMEM_LIMIT),
    )(*args)


def both_ways(low, high, axis, closed):
    count = lax.axis_size(axis)
    ends = count if closed else count - 1
    below = lax.ppermute(high, axis, [(i, (i + 1) % count) for i in range(ends)])
    above = lax.ppermute(low, axis, [((i + 1) % count, i) for i in range(ends)])
    return below, above


def body(les_velocity, les_metric, caa_state, caa_metric, intersection_refs, offsets, send_list):
    _, radial_nodes, sector, length = les_velocity.shape
    slabs = lax.axis_size("gx")
    assert (radial_nodes, sector, length) == (8, 16, 128)
    lines = radial_nodes * sector
    u, lm, w, m = (x.reshape(-1, lines, length) for x in (les_velocity, les_metric, caa_state, caa_metric))
    les_weights = jnp.asarray(np.stack([split_matrix(128), split_matrix(LES_WIDTH)]))
    caa_weights = jnp.asarray(np.stack([split_matrix(128), split_matrix(CAA_WIDTH)]))
    les_coef, caa_coef = jnp.asarray(coefficients(LES_WIDTH)), jnp.asarray(coefficients(CAA_WIDTH))
    own_row = lax.axis_index("sec") * slabs + lax.axis_index("gx")
    sends = lax.dynamic_slice_in_dim(send_list, own_row, 1, axis=0).reshape(-1)
    tile = (8, 128)
    vmem = lambda *shape, dtype=F32: pltpu.VMEM((*shape, *tile), dtype)

    low, high = call(
        functools.partial(first_kernel, sector),
        "first",
        [((15, *tile), F32)] * 2,
        u, lm,
        far=2,
        scratch=[pltpu.VMEM(u.shape, F32), pltpu.VMEM(lm.shape, F32), pltpu.SemaphoreType.DMA((2,))],
    )
    before, after = both_ways(low, high, "az", True)
    first, last = call(
        functools.partial(les_pack_kernel, sector),
        "les_pack",
        [((4, *tile), F32)] * 2,
        u, lm, before, after,
    )
    from_left, from_right = both_ways(first, last, STREAM, False)
    sent, um1, ut1 = call(
        functools.partial(les_kernel, sector),
        "les",
        [((slabs * 2, 6, *tile), BF16), ((3, 24, *tile), F32), ((3, 4, *tile), F32)],
        sends, u, lm, before, after, from_left, from_right, les_weights, les_coef,
        smem=1,
        scratch=[vmem(3, 24), vmem(3, 6), vmem(3, 24), vmem(3, 6), vmem(3, 24), vmem(16, 6, dtype=BF16)],
    )
    got = lax.all_to_all(sent.reshape(slabs, 96, 128), "gx", 0, 0, tiled=True).reshape(slabs * 2, 6, *tile)

    (both,) = call(functools.partial(narrow_kernel, sector), "narrow", [((7 * sector, *tile), BF16)], w, m)
    caa_below, caa_above = both_ways(both, both, "az", True)
    (les_out,) = call(
        functools.partial(les_out_kernel, sector),
        "les_out",
        [((3, lines, length), F32)],
        lm, um1, ut1, les_weights, les_coef,
        scratch=[vmem(3, 24)],
    )
    first, last = call(
        functools.partial(state_pack_kernel, sector),
        "state_pack",
        [((42, *tile), BF16)] * 2,
        caa_below, caa_above, both,
    )
    state_left, state_right = both_ways(first, last, STREAM, False)
    got, state_left, state_right, les_out = lax.optimization_barrier((got, state_left, state_right, les_out))

    own, up, down = call(
        functools.partial(blend_kernel, sector),
        "blend",
        [((2, 3, sector, *tile), F32), ((72, *tile), BF16), ((72, *tile), BF16)],
        intersection_refs.reshape(-1), offsets, got,
        smem=2,
        scratch=[vmem(6, 16)],
    )
    below, above = both_ways(down, up, "az", True)
    first, last = call(
        functools.partial(source_pack_kernel, sector),
        "source_pack",
        [((30, *tile), BF16)] * 2,
        own, below, above,
    )
    from_left, from_right = both_ways(first, last, STREAM, False)
    (caa_out,) = call(
        functools.partial(caa_kernel, sector),
        "caa",
        [((4, lines, length), F32)],
        w, m, own, below, above, caa_below, caa_above, state_left, state_right, from_left, from_right, caa_weights, caa_coef,
        scratch=[vmem(2, 4, 48), vmem(2, 4, 12), vmem(3, 48), vmem(3, 12), vmem(2, 3, 48), vmem(2, 3, 12)],
    )
    return les_out.reshape(les_velocity.shape), caa_out.reshape(caa_state.shape)


def solution(mesh):
    field = P(None, None, "az", STREAM)
    in_specs = (field, field, field, field, P(STREAM, None), P(STREAM), P())
    return jax.shard_map(body, mesh=mesh, in_specs=in_specs, out_specs=(field, field), check_vma=False)
```

time: 97.7 us -> 92.3 us (0.945)
  waiting for transfers between devices: 36.2 us -> 25.6 us
  starting transfers between devices: 38.1 us -> 45.2 us
  local copies, waits for them, and re-layouts: 4.59 us -> 0.88 us
  Pallas kernels: 17.6 us -> 19.3 us
    all_to_all x1, waiting for transfers between devices: 22.9 us -> 1.89 us  [body(): lax.all_to_all(sent.reshape(slabs, 96, 128), 'gx', 0, 0, tiled=True)]
    ppermute x5 -> x6, waiting for transfers between devices: 3.97 us -> 11.2 us  [both_ways(): lax.ppermute(high, axis, [(i, (i + 1) % count) for i in range(ends)])]
    unnamed x27 -> x23, local copies, waits for them, and re-layouts: 3.86 us -> 0.14 us
    ppermute x5 -> x6, starting transfers between devices: 12.7 us -> 16.4 us  [both_ways(): lax.ppermute(high, axis, [(i, (i + 1) % count) for i in range(ends)])]
    ppermute x5 -> x6, starting transfers between devices: 17.7 us -> 21.2 us  [both_ways(): above = lax.ppermute(low, axis, [((i + 1) % count, i) for i in range(ends)])]
    ppermute x5 -> x6, waiting for transfers between devices: 9.32 us -> 12.5 us  [both_ways(): above = lax.ppermute(low, axis, [((i + 1) % count, i) for i in range(ends)])]
    pallas_call x6 -> x9, Pallas kernels: 17.6 us -> 19.3 us  [call(): pl.pallas_call(kernel, name=name, out_shape=[jax.ShapeDtypeStruct(shape,...]
  transfers between devices with their start and end apart: 11 -> 13, of which waited for: 8 -> 10; matrix products, arithmetic and copies ran while one was open for 1% -> 1% of each run, Pallas kernels for 2% -> 2%
where the time goes in v2:
time: 92.3 us; the launch traced here: 91.9 us
  starting transfers between devices  45.2 us (49%)
  waiting for transfers between devices  25.6 us (28%)
  Pallas kernels  19.3 us (21%)
    ppermute x6, starting transfers between devices, both_ways(): above = lax.ppermute(low, axis, [((i + 1) % count, i) for i in range(ends)])  21.2 us
    pallas_call x9, Pallas kernels, call(): pl.pallas_call(kernel, name=name, out_shape=[jax.ShapeDtypeStruct(shape,...  19.3 us
    ppermute x6, starting transfers between devices, both_ways(): lax.ppermute(high, axis, [(i, (i + 1) % count) for i in range(ends)])  16.4 us
    ppermute x6, waiting for transfers between devices, both_ways(): above = lax.ppermute(low, axis, [((i + 1) % count, i) for i in range(ends)])  12.5 us
    ppermute x6, waiting for transfers between devices, both_ways(): lax.ppermute(high, axis, [(i, (i + 1) % count) for i in range(ends)])  11.2 us
    all_to_all x1, starting transfers between devices, body(): lax.all_to_all(sent.reshape(slabs, 96, 128), 'gx', 0, 0, tiled=True)  7.6 us
    all_to_all x1, waiting for transfers between devices, body(): lax.all_to_all(sent.reshape(slabs, 96, 128), 'gx', 0, 0, tiled=True)  1.89 us
  transfers between devices with their start and end apart: 13, of which 10 were waited for; matrix products, arithmetic and copies ran while one was open for 1% of the time, Pallas kernels for 2%

profile of v2, /device:TPU:29, one launch (start us, length us, event | category | flops | bytes accessed | tf_op | source)
XLA Modules:
  0.0 91.9 jit_solution(10427826406026360218)
XLA Ops:
  0.6 0.0 copy-start
  0.6 0.0 copy-start.1
  0.7 0.0 copy-start.2
  0.7 1.8 %first.1 = (f32[15,8,128]{2,1,0:T(8,128)}, f32[15,8,128]{2,1,0:T(8,128)}) custom-call(f32[3,128,128]{2,1,0:T(8,128)} %bitcast.13, f32[3,128,128]{2,1,0:T(8,128)} %bitcast.8), custom_call_target="tpu_custom_call" | custom-call | tf_op jit(solution)/shard_map/first/pallas_call | solution.py:567
  2.4 3.1 %collective-permute-start = (f32[15,8,128]{2,1,0:T(8,128)}, f32[15,8,128]{2,1,0:T(8,128)S(1)}, u32[]{:S(2)}, u32[]{:S(2)}) collective-permute-start(f32[15,8,128]{2,1,0:T(8,128)} %get-tuple-element.20), channel_id=1, source_target_pairs={{0,1},{1,2},{2,3},{3,4},{4,5},{5,6},{6,7},{7,8},{8,9},{9,10},{10,1... | collective-permute-start | bytes 184328 | tf_op jit(solution)/shard_map/ppermute | solution.py:581
  5.5 0.0 copy-start.4
  5.5 0.0 collective-permute-start.1
  5.5 1.6 %collective-permute-done.before = f32[15,8,128]{2,1,0:T(8,128)S(1)} collective-permute-done((f32[15,8,128]{2,1,0:T(8,128)}, f32[15,8,128]{2,1,0:T(8,128)S(1)}, u32[]{:S(2)}, u32[]{:S(2)}) %collective-permute-start) | collective-permute-done | bytes 61472 | tf_op jit(solution)/shard_map/ppermute | solution.py:581
  7.1 3.5 %collective-permute-done.1.after = f32[15,8,128]{2,1,0:T(8,128)S(1)} collective-permute-done((f32[15,8,128]{2,1,0:T(8,128)}, f32[15,8,128]{2,1,0:T(8,128)S(1)}, u32[]{:S(2)}, u32[]{:S(2)}) %collective-permute-start.1) | collective-permute-done | bytes 61472 | tf_op jit(solution)/shard_map/ppermute | solution.py:582
  10.6 0.0 copy-done.1
  10.6 0.0 copy-done.2
  10.6 0.3 les_pack.1
  10.9 0.0 copy-start.7
  10.9 4.1 %collective-permute-start.2 = (f32[4,8,128]{2,1,0:T(8,128)S(1)}, f32[4,8,128]{2,1,0:T(8,128)S(1)}, u32[]{:S(2)}, u32[]{:S(2)}) collective-permute-start(f32[4,8,128]{2,1,0:T(8,128)S(1)} %get-tuple-element.22), channel_id=1, source_target_pairs={{0,16},{16,32},{32,48},{48,64},{64,80},{80,96},{96,112},{112,128},... | collective-permute-start | bytes 49160 | tf_op jit(solution)/shard_map/ppermute | solution.py:581
  15.1 12.2 %collective-permute-start.3 = (f32[4,8,128]{2,1,0:T(8,128)S(1)}, f32[4,8,128]{2,1,0:T(8,128)S(1)}, u32[]{:S(2)}, u32[]{:S(2)}) collective-permute-start(f32[4,8,128]{2,1,0:T(8,128)S(1)} %get-tuple-element.23), channel_id=1, source_target_pairs={{16,0},{32,16},{48,32},{64,48},{80,64},{96,80},{112,96},{128,112},... | collective-permute-start | bytes 49160 | tf_op jit(solution)/shard_map/ppermute | solution.py:582
  27.3 0.0 copy-done
  27.3 0.6 dynamic-slice_reduce_fusion
  27.9 0.1 reshape.34.sends
  28.0 0.0 collective-permute-done.2.from_left
  28.0 0.2 collective-permute-done.3.from_right
  28.1 0.0 copy-done.4
  28.1 0.0 copy-done.7
  28.1 4.1 %les.1 = (bf16[48,6,8,128]{3,2,1,0:T(8,128)(2,1)}, f32[3,24,8,128]{3,2,1,0:T(8,128)S(1)}, f32[3,4,8,128]{3,2,1,0:T(8,128)S(1)}) custom-call(s32[48]{0:T(128)S(1)} %reshape.34.sends, f32[3,128,128]{2,1,0:T(8,128)S(1)} %bitcast.15, f32[3,128,128]{2,1,0:T(8,128)S(1)} %bitcast.10, f32[15,8,128]{2,1,0:T(8,128)S(1)} %collective-permute-done.before, ...), custom_call_target="tpu_custom_call" | custom-call | tf_op jit(solution)/shard_map/les/pallas_call | solution.py:567
  32.2 0.0 copy-start.3
  32.2 0.0 copy-start.5
  32.2 7.6 %all-to-all-start = ((bf16[24,96,128]{2,1,0:T(8,128)(2,1)}), bf16[24,96,128]{2,1,0:T(8,128)(2,1)S(1)}, u32[]{:S(2)}, u32[]{:S(2)}) async-start(bf16[24,96,128]{2,1,0:T(8,128)(2,1)} %bitcast.2), calls=%async_computation | async-start | bytes 1179648 | tf_op jit(solution)/shard_map/all_to_all | solution.py:624
  39.8 0.0 copy-done.3
  39.8 0.0 copy-done.5
  39.8 0.2 narrow.1.both
  40.0 1.8 %collective-permute-start.4 = (bf16[112,8,128]{2,1,0:T(8,128)(2,1)S(1)}, bf16[112,8,128]{2,1,0:T(8,128)(2,1)S(1)}, u32[]{:S(2)}, u32[]{:S(2)}) collective-permute-start(bf16[112,8,128]{2,1,0:T(8,128)(2,1)S(1)} %narrow.1.both), channel_id=1, source_target_pairs={{0,1},{1,2},{2,3},{3,4},{4,5},{5,6},{6,7},{7,8},{8,9},{9,10},{10,1... | collective-permute-start | bytes 688136 | tf_op jit(solution)/shard_map/ppermute | solution.py:581
  41.8 0.0 collective-permute-start.5
  41.8 3.0 %collective-permute-done.4.below.caa_below = bf16[112,8,128]{2,1,0:T(8,128)(2,1)S(1)} collective-permute-done((bf16[112,8,128]{2,1,0:T(8,128)(2,1)S(1)}, bf16[112,8,128]{2,1,0:T(8,128)(2,1)S(1)}, u32[]{:S(2)}, u32[]{:S(2)}) %collective-permute-start.4) | collective-permute-done | bytes 229408 | tf_op jit(solution)/shard_map/ppermute | solution.py:581
  44.8 4.0 %collective-permute-done.5.above.caa_above = bf16[112,8,128]{2,1,0:T(8,128)(2,1)S(1)} collective-permute-done((bf16[112,8,128]{2,1,0:T(8,128)(2,1)S(1)}, bf16[112,8,128]{2,1,0:T(8,128)(2,1)S(1)}, u32[]{:S(2)}, u32[]{:S(2)}) %collective-permute-start.5) | collective-permute-done | bytes 229408 | tf_op jit(solution)/shard_map/ppermute | solution.py:582
  48.7 0.4 state_pack.1
  49.1 0.0 copy-start.10
  49.1 3.5 %collective-permute-start.6 = (bf16[42,8,128]{2,1,0:T(8,128)(2,1)S(1)}, bf16[42,8,128]{2,1,0:T(8,128)(2,1)S(1)}, u32[]{:S(2)}, u32[]{:S(2)}) collective-permute-start(bf16[42,8,128]{2,1,0:T(8,128)(2,1)S(1)} %get-tuple-element.25), channel_id=1, source_target_pairs={{0,16},{16,32},{32,48},{48,64},{64,80},{80,96},{96,112},{112,128},... | collective-permute-start | bytes 258056 | tf_op jit(solution)/shard_map/ppermute | solution.py:581
  52.6 3.9 %collective-permute-start.7 = (bf16[42,8,128]{2,1,0:T(8,128)(2,1)S(1)}, bf16[42,8,128]{2,1,0:T(8,128)(2,1)S(1)}, u32[]{:S(2)}, u32[]{:S(2)}) collective-permute-start(bf16[42,8,128]{2,1,0:T(8,128)(2,1)S(1)} %get-tuple-element.26), channel_id=1, source_target_pairs={{16,0},{32,16},{48,32},{64,48},{80,64},{96,80},{112,96},{128,112},... | collective-permute-start | bytes 258056 | tf_op jit(solution)/shard_map/ppermute | solution.py:582
  56.6 0.0 copy-done.10
  56.6 0.1 copy.14
  56.6 0.1 reshape.42.refs
  56.7 1.6 %les_out.1 = f32[3,128,128]{2,1,0:T(8,128)} custom-call(f32[3,128,128]{2,1,0:T(8,128)S(1)} %bitcast.11, f32[3,24,8,128]{3,2,1,0:T(8,128)S(1)} %get-tuple-element.27.um1, f32[3,4,8,128]{3,2,1,0:T(8,128)S(1)} %get-tuple-element.28.ut1, bf16[2,256,256]{2,1,0:T(8,128)(2,1)S(1)} %copy-done.4, f32[16,8,128]{2,1,0:T(8,128)S(1)} %copy-done.7), custom_call_target="tpu_custom_call" | custom-call | tf_op jit(solution)/shard_map/les_out/pallas_call | solution.py:567
  58.3 0.0 copy-start.9
  58.3 4.5 %collective-permute-done.6.state_left = bf16[42,8,128]{2,1,0:T(8,128)(2,1)S(1)} collective-permute-done((bf16[42,8,128]{2,1,0:T(8,128)(2,1)S(1)}, bf16[42,8,128]{2,1,0:T(8,128)(2,1)S(1)}, u32[]{:S(2)}, u32[]{:S(2)}) %collective-permute-start.6) | collective-permute-done | bytes 86048 | tf_op jit(solution)/shard_map/ppermute | solution.py:581
  62.9 0.0 collective-permute-done.7.state_right
  62.9 1.9 %all-to-all-done = bf16[24,96,128]{2,1,0:T(8,128)(2,1)S(1)} async-done(((bf16[24,96,128]{2,1,0:T(8,128)(2,1)}), bf16[24,96,128]{2,1,0:T(8,128)(2,1)S(1)}, u32[]{:S(2)}, u32[]{:S(2)}) %all-to-all-start) | async-done | bytes 589856 | tf_op jit(solution)/shard_map/all_to_all | solution.py:624
  64.8 0.0 copy-done.9
  64.8 1.4 %blend.1 = (f32[2,3,16,8,128]{4,3,2,1,0:T(8,128)S(1)}, bf16[72,8,128]{2,1,0:T(8,128)(2,1)S(1)}, bf16[72,8,128]{2,1,0:T(8,128)(2,1)S(1)}) custom-call(s32[64]{0:T(128)S(1)} %reshape.42.refs, s32[16]{0:T(128)S(1)} %copy-done.9, bf16[48,6,8,128]{3,2,1,0:T(8,128)(2,1)S(1)} %bitcast.12), custom_call_target="tpu_custom_call" | custom-call | tf_op jit(solution)/shard_map/blend/pallas_call | solution.py:567
  66.2 1.6 %collective-permute-start.8 = (bf16[72,8,128]{2,1,0:T(8,128)(2,1)S(1)}, bf16[72,8,128]{2,1,0:T(8,128)(2,1)S(1)}, u32[]{:S(2)}, u32[]{:S(2)}) collective-permute-start(bf16[72,8,128]{2,1,0:T(8,128)(2,1)S(1)} %get-tuple-element.32), channel_id=1, source_target_pairs={{0,1},{1,2},{2,3},{3,4},{4,5},{5,6},{6,7},{7,8},{8,9},{9,10},{10,1... | collective-permute-start | bytes 442376 | tf_op jit(solution)/shard_map/ppermute | solution.py:581
  67.8 0.0 collective-permute-start.9
  67.8 2.1 %collective-permute-done.8.below = bf16[72,8,128]{2,1,0:T(8,128)(2,1)S(1)} collective-permute-done((bf16[72,8,128]{2,1,0:T(8,128)(2,1)S(1)}, bf16[72,8,128]{2,1,0:T(8,128)(2,1)S(1)}, u32[]{:S(2)}, u32[]{:S(2)}) %collective-permute-start.8) | collective-permute-done | bytes 147488 | tf_op jit(solution)/shard_map/ppermute | solution.py:581
  69.9 3.7 %collective-permute-done.9.above = bf16[72,8,128]{2,1,0:T(8,128)(2,1)S(1)} collective-permute-done((bf16[72,8,128]{2,1,0:T(8,128)(2,1)S(1)}, bf16[72,8,128]{2,1,0:T(8,128)(2,1)S(1)}, u32[]{:S(2)}, u32[]{:S(2)}) %collective-permute-start.9) | collective-permute-done | bytes 147488 | tf_op jit(solution)/shard_map/ppermute | solution.py:582
  73.6 0.0 copy-start.6
  73.6 0.0 copy-start.8
  73.6 0.3 source_pack.1
  73.9 2.3 %collective-permute-start.10 = (bf16[30,8,128]{2,1,0:T(8,128)(2,1)S(1)}, bf16[30,8,128]{2,1,0:T(8,128)(2,1)S(1)}, u32[]{:S(2)}, u32[]{:S(2)}) collective-permute-start(bf16[30,8,128]{2,1,0:T(8,128)(2,1)S(1)} %get-tuple-element.36), channel_id=1, source_target_pairs={{0,16},{16,32},{32,48},{48,64},{64,80},{80,96},{96,112},{112,128},... | collective-permute-start | bytes 184328 | tf_op jit(solution)/shard_map/ppermute | solution.py:581
  76.2 5.1 %collective-permute-start.11 = (bf16[30,8,128]{2,1,0:T(8,128)(2,1)S(1)}, bf16[30,8,128]{2,1,0:T(8,128)(2,1)S(1)}, u32[]{:S(2)}, u32[]{:S(2)}) collective-permute-start(bf16[30,8,128]{2,1,0:T(8,128)(2,1)S(1)} %get-tuple-element.37), channel_id=1, source_target_pairs={{16,0},{32,16},{48,32},{64,48},{80,64},{96,80},{112,96},{128,112},... | collective-permute-start | bytes 184328 | tf_op jit(solution)/shard_map/ppermute | solution.py:582
  81.3 0.0 collective-permute-done.10.from_left
  81.3 1.3 %collective-permute-done.11.from_right = bf16[30,8,128]{2,1,0:T(8,128)(2,1)S(1)} collective-permute-done((bf16[30,8,128]{2,1,0:T(8,128)(2,1)S(1)}, bf16[30,8,128]{2,1,0:T(8,128)(2,1)S(1)}, u32[]{:S(2)}, u32[]{:S(2)}) %collective-permute-start.11) | collective-permute-done | bytes 61472 | tf_op jit(solution)/shard_map/ppermute | solution.py:582
  82.6 0.0 copy-done.6
  82.6 0.0 copy-done.8
  82.6 9.3 %caa.1 = f32[4,128,128]{2,1,0:T(8,128)} custom-call(f32[4,128,128]{2,1,0:T(8,128)S(1)} %bitcast.17, f32[3,128,128]{2,1,0:T(8,128)S(1)} %bitcast.19, f32[2,3,16,8,128]{4,3,2,1,0:T(8,128)S(1)} %get-tuple-element.31.own, bf16[72,8,128]{2,1,0:T(8,128)(2,1)S(1)} %collective-permute-done.8.below, bf16[72,8,128]{2,1,0:T(8,128)(2,1)S(1)} %collective-permute-done.9.above, ...), custom_call_target="tpu_custom_call" | custom-call | tf_op jit(solution)/shard_map/caa/pallas_call | solution.py:567
Async XLA Ops:
  0.6 26.7 %copy-start = (s32[48,24,2]{0,2,1:T(2,128)S(1)}, s32[48,24,2]{0,2,1:T(2,128)}, u32[]{:S(2)}) copy-start(s32[48,24,2]{0,2,1:T(2,128)} %param.17) | copy-start | bytes 27652
  0.6 10.0 %copy-start.1 = (f32[3,8,16,128]{3,2,1,0:T(8,128)S(1)}, f32[3,8,16,128]{3,2,1,0:T(8,128)}, u32[]{:S(2)}) copy-start(f32[3,8,16,128]{3,2,1,0:T(8,128)} %param.12) | copy-start | bytes 589828
  0.7 9.9 %copy-start.2 = (f32[3,8,16,128]{3,2,1,0:T(8,128)S(1)}, f32[3,8,16,128]{3,2,1,0:T(8,128)}, u32[]{:S(2)}) copy-start(f32[3,8,16,128]{3,2,1,0:T(8,128)} %param.11) | copy-start | bytes 589828
  2.4 4.7 %collective-permute-start = (f32[15,8,128]{2,1,0:T(8,128)}, f32[15,8,128]{2,1,0:T(8,128)S(1)}, u32[]{:S(2)}, u32[]{:S(2)}) collective-permute-start(f32[15,8,128]{2,1,0:T(8,128)} %get-tuple-element.20), channel_id=1, source_target_pairs={{0,1},{1,2},{2,3},{3,4},{4,5},{5,6},{6,7},{7,8},{8,9},{9,10},{10,1... | collective-permute-start | bytes 184328 | tf_op jit(solution)/shard_map/ppermute | solution.py:581
  5.5 22.6 %copy-start.4 = (bf16[2,256,256]{2,1,0:T(8,128)(2,1)S(1)}, bf16[2,256,256]{2,1,0:T(8,128)(2,1)}, u32[]{:S(2)}) copy-start(bf16[2,256,256]{2,1,0:T(8,128)(2,1)} %constant.24.clone.weights) | copy-start | bytes 786436
  5.5 5.1 %collective-permute-start.1 = (f32[15,8,128]{2,1,0:T(8,128)}, f32[15,8,128]{2,1,0:T(8,128)S(1)}, u32[]{:S(2)}, u32[]{:S(2)}) collective-permute-start(f32[15,8,128]{2,1,0:T(8,128)} %get-tuple-element.21), channel_id=1, source_target_pairs={{1,0},{2,1},{3,2},{4,3},{5,4},{6,5},{7,6},{8,7},{9,8},{10,9},{11,1... | collective-permute-start | bytes 184328 | tf_op jit(solution)/shard_map/ppermute | solution.py:582
  10.9 17.2 %copy-start.7 = (f32[16,8,128]{2,1,0:T(8,128)S(1)}, f32[16,8,128]{2,1,0:T(8,128)}, u32[]{:S(2)}) copy-start(f32[16,8,128]{2,1,0:T(8,128)} %constant.26.clone.coef) | copy-start | bytes 196612
  10.9 17.0 %collective-permute-start.2 = (f32[4,8,128]{2,1,0:T(8,128)S(1)}, f32[4,8,128]{2,1,0:T(8,128)S(1)}, u32[]{:S(2)}, u32[]{:S(2)}) collective-permute-start(f32[4,8,128]{2,1,0:T(8,128)S(1)} %get-tuple-element.22), channel_id=1, source_target_pairs={{0,16},{16,32},{32,48},{48,64},{64,80},{80,96},{96,112},{112,128},... | collective-permute-start | bytes 49160 | tf_op jit(solution)/shard_map/ppermute | solution.py:581
  15.1 13.1 %collective-permute-start.3 = (f32[4,8,128]{2,1,0:T(8,128)S(1)}, f32[4,8,128]{2,1,0:T(8,128)S(1)}, u32[]{:S(2)}, u32[]{:S(2)}) collective-permute-start(f32[4,8,128]{2,1,0:T(8,128)S(1)} %get-tuple-element.23), channel_id=1, source_target_pairs={{16,0},{32,16},{48,32},{64,48},{80,64},{96,80},{112,96},{128,112},... | collective-permute-start | bytes 49160 | tf_op jit(solution)/shard_map/ppermute | solution.py:582
  32.2 7.6 %copy-start.3 = (f32[4,8,16,128]{3,2,1,0:T(8,128)S(1)}, f32[4,8,16,128]{3,2,1,0:T(8,128)}, u32[]{:S(2)}) copy-start(f32[4,8,16,128]{3,2,1,0:T(8,128)} %param.13) | copy-start | bytes 786436
  32.2 7.6 %copy-start.5 = (f32[3,8,16,128]{3,2,1,0:T(8,128)S(1)}, f32[3,8,16,128]{3,2,1,0:T(8,128)}, u32[]{:S(2)}) copy-start(f32[3,8,16,128]{3,2,1,0:T(8,128)} %param.14) | copy-start | bytes 589828
  32.2 32.6 %all-to-all-start = ((bf16[24,96,128]{2,1,0:T(8,128)(2,1)}), bf16[24,96,128]{2,1,0:T(8,128)(2,1)S(1)}, u32[]{:S(2)}, u32[]{:S(2)}) async-start(bf16[24,96,128]{2,1,0:T(8,128)(2,1)} %bitcast.2), calls=%async_computation | async-start | bytes 1179648 | tf_op jit(solution)/shard_map/all_to_all | solution.py:624
  40.0 4.8 %collective-permute-start.4 = (bf16[112,8,128]{2,1,0:T(8,128)(2,1)S(1)}, bf16[112,8,128]{2,1,0:T(8,128)(2,1)S(1)}, u32[]{:S(2)}, u32[]{:S(2)}) collective-permute-start(bf16[112,8,128]{2,1,0:T(8,128)(2,1)S(1)} %narrow.1.both), channel_id=1, source_target_pairs={{0,1},{1,2},{2,3},{3,4},{4,5},{5,6},{6,7},{7,8},{8,9},{9,10},{10,1... | collective-permute-start | bytes 688136 | tf_op jit(solution)/shard_map/ppermute | solution.py:581
  41.8 7.0 %collective-permute-start.5 = (bf16[112,8,128]{2,1,0:T(8,128)(2,1)S(1)}, bf16[112,8,128]{2,1,0:T(8,128)(2,1)S(1)}, u32[]{:S(2)}, u32[]{:S(2)}) collective-permute-start(bf16[112,8,128]{2,1,0:T(8,128)(2,1)S(1)} %narrow.1.both), channel_id=1, source_target_pairs={{1,0},{2,1},{3,2},{4,3},{5,4},{6,5},{7,6},{8,7},{9,8},{10,9},{11,1... | collective-permute-start | bytes 688136 | tf_op jit(solution)/shard_map/ppermute | solution.py:582
  49.1 7.4 %copy-start.10 = (s32[16,4]{0,1:T(4,128)S(1)}, s32[16,4]{0,1:T(4,128)}, u32[]{:S(2)}) copy-start(s32[16,4]{0,1:T(4,128)} %param.15) | copy-start | bytes 772
  49.1 13.7 %collective-permute-start.6 = (bf16[42,8,128]{2,1,0:T(8,128)(2,1)S(1)}, bf16[42,8,128]{2,1,0:T(8,128)(2,1)S(1)}, u32[]{:S(2)}, u32[]{:S(2)}) collective-permute-start(bf16[42,8,128]{2,1,0:T(8,128)(2,1)S(1)} %get-tuple-element.25), channel_id=1, source_target_pairs={{0,16},{16,32},{32,48},{48,64},{64,80},{80,96},{96,112},{112,128},... | collective-permute-start | bytes 258056 | tf_op jit(solution)/shard_map/ppermute | solution.py:581
  52.6 10.3 %collective-permute-start.7 = (bf16[42,8,128]{2,1,0:T(8,128)(2,1)S(1)}, bf16[42,8,128]{2,1,0:T(8,128)(2,1)S(1)}, u32[]{:S(2)}, u32[]{:S(2)}) collective-permute-start(bf16[42,8,128]{2,1,0:T(8,128)(2,1)S(1)} %get-tuple-element.26), channel_id=1, source_target_pairs={{16,0},{32,16},{48,32},{64,48},{80,64},{96,80},{112,96},{128,112},... | collective-permute-start | bytes 258056 | tf_op jit(solution)/shard_map/ppermute | solution.py:582
  58.3 6.4 %copy-start.9 = (s32[16]{0:T(128)S(1)}, s32[16]{0:T(128)}, u32[]{:S(2)}) copy-start(s32[16]{0:T(128)} %offsets.1) | copy-start | bytes 196
  66.2 3.7 %collective-permute-start.8 = (bf16[72,8,128]{2,1,0:T(8,128)(2,1)S(1)}, bf16[72,8,128]{2,1,0:T(8,128)(2,1)S(1)}, u32[]{:S(2)}, u32[]{:S(2)}) collective-permute-start(bf16[72,8,128]{2,1,0:T(8,128)(2,1)S(1)} %get-tuple-element.32), channel_id=1, source_target_pairs={{0,1},{1,2},{2,3},{3,4},{4,5},{5,6},{6,7},{7,8},{8,9},{9,10},{10,1... | collective-permute-start | bytes 442376 | tf_op jit(solution)/shard_map/ppermute | solution.py:581
  67.8 5.8 %collective-permute-start.9 = (bf16[72,8,128]{2,1,0:T(8,128)(2,1)S(1)}, bf16[72,8,128]{2,1,0:T(8,128)(2,1)S(1)}, u32[]{:S(2)}, u32[]{:S(2)}) collective-permute-start(bf16[72,8,128]{2,1,0:T(8,128)(2,1)S(1)} %get-tuple-element.33), channel_id=1, source_target_pairs={{1,0},{2,1},{3,2},{4,3},{5,4},{6,5},{7,6},{8,7},{9,8},{10,9},{11,1... | collective-permute-start | bytes 442376 | tf_op jit(solution)/shard_map/ppermute | solution.py:582
  73.6 9.0 %copy-start.6 = (bf16[2,256,256]{2,1,0:T(8,128)(2,1)S(1)}, bf16[2,256,256]{2,1,0:T(8,128)(2,1)}, u32[]{:S(2)}) copy-start(bf16[2,256,256]{2,1,0:T(8,128)(2,1)} %constant.25.clone.weights) | copy-start | bytes 786436
  73.6 9.0 %copy-start.8 = (f32[16,8,128]{2,1,0:T(8,128)S(1)}, f32[16,8,128]{2,1,0:T(8,128)}, u32[]{:S(2)}) copy-start(f32[16,8,128]{2,1,0:T(8,128)} %constant.27.clone.coef) | copy-start | bytes 196612
  73.9 7.4 %collective-permute-start.10 = (bf16[30,8,128]{2,1,0:T(8,128)(2,1)S(1)}, bf16[30,8,128]{2,1,0:T(8,128)(2,1)S(1)}, u32[]{:S(2)}, u32[]{:S(2)}) collective-permute-start(bf16[30,8,128]{2,1,0:T(8,128)(2,1)S(1)} %get-tuple-element.36), channel_id=1, source_target_pairs={{0,16},{16,32},{32,48},{48,64},{64,80},{80,96},{96,112},{112,128},... | collective-permute-start | bytes 184328 | tf_op jit(solution)/shard_map/ppermute | solution.py:581
  76.2 6.4 %collective-permute-start.11 = (bf16[30,8,128]{2,1,0:T(8,128)(2,1)S(1)}, bf16[30,8,128]{2,1,0:T(8,128)(2,1)S(1)}, u32[]{:S(2)}, u32[]{:S(2)}) collective-permute-start(bf16[30,8,128]{2,1,0:T(8,128)(2,1)S(1)} %get-tuple-element.37), channel_id=1, source_target_pairs={{16,0},{32,16},{48,32},{64,48},{80,64},{96,80},{112,96},{128,112},... | collective-permute-start | bytes 184328 | tf_op jit(solution)/shard_map/ppermute | solution.py:582

commit v3 on v2

--- a/solution.py
+++ b/solution.py
@@ -83,6 +83,55 @@
     return c
 
 
+WHOLE_T, WHOLE_P, WHOLE_N = 0, 6, 7
+
+
+def acoustic_coefficients():
+    c = np.zeros((10, 8, 128), np.float32)
+    for lane in range(128):
+        i = lane // 32
+        for n, k in enumerate(OFFSETS):
+            if 0 <= i + k <= 3:
+                c[WHOLE_T + n, :, lane] = DM[i, i + k]
+        if i == 0:
+            c[WHOLE_P, :, lane] = -3.0
+        if i == 3:
+            c[WHOLE_N, :, lane] = 3.0
+    c[8, :, 127], c[8, :, 0] = 3.0, -3.0
+    for i in range(4):
+        c[9, :, 32 * i + 15], c[9, :, 32 * i + 16] = -3.0, 3.0
+    return c
+
+
+def two_terms(full):
+    full = full.astype(np.float32)
+    high = full.astype(jnp.bfloat16)
+    return high, (full - high.astype(np.float32)).astype(jnp.bfloat16)
+
+
+def acoustic_weights():
+    natural = lane_matrix(16)
+    lane = np.arange(128)
+    reverse = 16 * (lane // 16) + 15 - lane % 16
+    return np.stack([np.concatenate(two_terms(full), axis=1) for full in (lane_matrix(128), natural[np.ix_(reverse, reverse)])])
+
+
+def radial_matrix(count):
+    block = np.zeros((8, 8))
+    block[:4, :4] = block[4:, 4:] = DM
+    block[3, 4], block[4, 3] = 3.0, -3.0
+    return np.concatenate(two_terms(np.kron(np.eye(count), block)), axis=0)
+
+
+def halo_order():
+    order = np.zeros((2, 128, 128), np.float32)
+    for lane in range(128):
+        i, half, k = lane // 32, (lane // 16) % 2, 15 - lane % 16
+        order[0, 64 * half + 16 * i + k, lane] = 1.0
+        order[1, 64 * (1 - half) + 16 * i + k, lane] = 1.0
+    return order.astype(jnp.bfloat16)
+
+
 def lanes_of():
     return lax.broadcasted_iota(jnp.int32, (8, 128), 1)
 
@@ -191,10 +240,15 @@
     shift = 4 * width * (n % count)
     left, right = lane_roll(left, 64 - shift), lane_roll(right, -shift)
     lane = lanes_of()
-    if width == 16:
-        return jnp.where(lane < 64, right, left)
     both = jnp.where(lane < 64, right, left)
     return jnp.where(lane % 64 < 4 * width, both, 0.0)
+
+
+def acoustic_tile(from_left, from_right, n):
+    left, right = from_left[n // 2].astype(F32), from_right[n // 2].astype(F32)
+    if n % 2:
+        left, right = lane_roll(left, 16), lane_roll(right, -16)
+    return jnp.where(lanes_of() % 32 < 16, right, left)
 
 
 def turn(tiles):
@@ -340,8 +394,7 @@
                     um1[c, k] = rows[c]
                     um1[c, 5 + sector + k] = rows[c]
 
-    @pl.loop(1, 5)
-    def _(e):
+    for e in range(1, 5):
         rows, tiles, fields, halos, slopes, fluxes = les_element(um, ut, mm, e, weights, coef, True)
         lamb_of(rows, slopes, lamb, e)
         for c in range(3):
@@ -369,8 +422,7 @@
 
     blocks(0)
 
-    @pl.loop(1, 5)
-    def _(e):
+    for e in range(1, 5):
         rows, _, _, _, slopes, _ = les_element(um1, Shifted(ut1), mm, e, weights, coef, False)
         lamb_of(rows, slopes, lamb, e)
 
@@ -402,11 +454,11 @@
                 out[c, pl.ds(4 * (e - 1) + i, 8, stride=sector), :] = rows[c][i] - les_change(rows, slopes, fluxes, c, i)
 
 
-def blend_kernel(sector, refs, offsets, got, own, up, down, mixed):
+def blend_kernel(sector, refs, got, own, up, down, mixed):
     for j in range(16):
         a = jnp.clip(refs[4 * j] * 2 + refs[4 * j + 1], 0, got.shape[0] - 1)
         b = jnp.clip(refs[4 * j + 2] * 2 + refs[4 * j + 3], 0, got.shape[0] - 1)
-        fraction = offsets[j].astype(F32)
+        fraction = refs[64 + j].astype(F32)
         for k in range(6):
             blend = (8.0 - fraction) * got[a, k].astype(F32) + fraction * got[b, k].astype(F32)
             mixed[k, j] = blend * 0.125
@@ -425,23 +477,28 @@
                     down[48 + c * 8 + az] = narrow
 
 
-def pack_entries(entries, first, last):
-    for n in range(len(entries) // 2):
-        rows = [ref[at].astype(F32) for ref, at in entries[2 * n] + entries[2 * n + 1]]
-        first[n] = pack(rows, False, CAA_WIDTH).astype(BF16)
-        last[n] = pack(rows, True, CAA_WIDTH).astype(BF16)
-
-
-def state_pack_kernel(sector, below, above, both, first, last):
+def pack_entries(entries, order, first, last):
+    for way, to in enumerate((first, last)):
+        tiles = []
+        for n in range(len(entries) // 2):
+            rows = [ref[at].astype(F32) for ref, at in entries[2 * n] + entries[2 * n + 1]]
+            tiles.append(pack(rows, way == 1, CAA_WIDTH))
+        x = jnp.concatenate(tiles, axis=0).astype(BF16)
+        y = jnp.dot(x, order[way], preferred_element_type=F32)
+        for n in range(len(tiles)):
+            to[n] = y[8 * n : 8 * n + 8].astype(BF16)
+
+
+def state_pack_kernel(sector, below, above, both, order, first, last):
     entries = []
     for f in range(7):
         for e in range(12):
             ref = (below, both, above)[e // 4]
             entries.append([(ref, f * sector + 4 * (e % 4) + i) for i in range(4)])
-    pack_entries(entries, first, last)
-
-
-def source_pack_kernel(sector, own, below, above, first, last):
+    pack_entries(entries, order, first, last)
+
+
+def source_pack_kernel(sector, own, below, above, order, first, last):
     entries = []
     for c in range(3):
         for e in range(12):
@@ -457,18 +514,16 @@
                 entries.append([(below, 48 + c * 8 + 4 * (e - 2) + i) for i in range(4)])
             else:
                 entries.append([(above, 48 + c * 8 + 4 * (e - 8) + i) for i in range(4)])
-    pack_entries(entries, first, last)
+    pack_entries(entries, order, first, last)
 
 
 CAA_RANGES = ((0, 12), (1, 11), (1, 11), (2, 10), (2, 10), (3, 9), (3, 9), (4, 8))
 
 
 def caa_kernel(
-    sector, w, m, own, below, above, caa_below, caa_above, state_left, state_right, from_left, from_right, weights, coef,
+    sector, w, m, own, below, above, caa_below, caa_above, state_left, state_right, from_left, from_right, weights, coef, upward,
     out, wm, wt, mm, mt, sm, st,
 ):
-    w_main, w_halo = weights[0], weights[1]
-
     for f in range(7):
         for az in range(3 * sector):
             if az < sector:
@@ -482,7 +537,7 @@
             else:
                 mm[f - 4, az] = value * caa_step
         for e in range(12):
-            value = halo_tile(state_left, state_right, 12 * f + e, CAA_WIDTH)
+            value = acoustic_tile(state_left, state_right, 12 * f + e)
             if f < 4:
                 wt[0, f, e] = value
             else:
@@ -497,31 +552,20 @@
             sm[1, c, 8 + az] = below[48 + c * 8 + az].astype(F32) * caa_step
             sm[1, c, 32 + az] = above[48 + c * 8 + az].astype(F32) * caa_step
         for e in range(12):
-            st[0, c, e] = halo_tile(from_left, from_right, 12 * c + e, CAA_WIDTH) * caa_step
+            st[0, c, e] = acoustic_tile(from_left, from_right, 12 * c + e) * caa_step
         for e in range(8):
-            st[1, c, 2 + e] = halo_tile(from_left, from_right, 36 + 8 * c + e, CAA_WIDTH) * caa_step
+            st[1, c, 2 + e] = acoustic_tile(from_left, from_right, 36 + 8 * c + e) * caa_step
+
+    def along(tiles, which):
+        x = jnp.concatenate(tiles, axis=0).astype(BF16)
+        y = jnp.dot(x, weights[which], preferred_element_type=F32)
+        y = y[:, :128] + y[:, 128:]
+        return [y[8 * n : 8 * n + 8] for n in range(len(tiles))]
 
     def pair(now, source, e, final):
         rows = [[wm[now, f, 4 * e + i] for i in range(8)] for f in range(4)]
         tiles = [[wt[now, f, e + n] for n in range(2)] for f in range(4)]
-        below, above = jnp.maximum(4 * e - 1, 0), jnp.minimum(4 * e + 8, 47)
-        tile_below, tile_above = jnp.maximum(e - 1, 0), jnp.minimum(e + 2, 11)
-
-        def rates(values, metric, sources, stream, around, up):
-            p, v0, v1, v2 = values
-            count = len(p)
-            azimuth_p, azimuth_v = around
-            radial_p, radial_v = up
-            for n in range(count):
-                m0, m1, m2 = metric[0](n), metric[1](n), metric[2](n)
-                half = mach_number * m0
-                yield (
-                    n,
-                    p[n] - m0 * stream[0][n] - m1 * azimuth_v[n] - m2 * radial_v[n],
-                    v0[n] - m0 * stream[1][n] + sources[0](n),
-                    v1[n] - half * stream[2][n] - m1 * azimuth_p[n] + sources[1](n),
-                    v2[n] - half * stream[3][n] - m2 * radial_p[n] + sources[2](n),
-                )
+        below, above, tile_below, tile_above = max(4 * e - 1, 0), min(4 * e + 8, 47), max(e - 1, 0), min(e + 2, 11)
 
         def mixed(values):
             p, v0, v1, v2 = values
@@ -532,33 +576,71 @@
                 v2,
             ]
 
+        def update(values, metric, sources, stream, around, up, store):
+            p, v0, v1, v2 = values
+            for n in range(len(p)):
+                m0, m1, m2 = metric(0, n), metric(1, n), metric(2, n)
+                half = mach_number * m0
+                store(0, n, p[n] - m0 * stream[0][n] - m1 * around[1][n] - m2 * up[1][n])
+                store(1, n, v0[n] - m0 * stream[1][n] + sources(0, n))
+                store(2, n, v1[n] - half * stream[2][n] - m1 * around[0][n] + sources(1, n))
+                store(3, n, v2[n] - half * stream[3][n] - m2 * up[0][n] + sources(2, n))
+
         fields, halos = mixed(rows), mixed(tiles)
-        stream = stream_main(fields, halos, w_main, coef, CAA_WIDTH)
+        x = [jnp.concatenate(rows[f] + tiles[f], axis=0).astype(BF16) for f in (0, 3)]
+        y = jnp.dot(upward[...], jnp.concatenate(x, axis=1), preferred_element_type=F32)
+        y = y[:80] + y[80:]
+        up = [[y[8 * n : 8 * n + 8, 128 * f : 128 * f + 128] for n in range(10)] for f in range(2)]
+
+        stream = along([row for values in fields for row in values], 0)
+        stream = [[stream[8 * f + n] for n in range(8)] for f in range(4)]
+        for f in range(4):
+            for n in range(8):
+                edge = lane_roll(halos[f][n // 4], -32 * (n % 4) - 16)
+                stream[f][n] = stream[f][n] + coef[8] * edge
         around = [azimuth_main(rows[f], wm[now, f, below], wm[now, f, above]) for f in (0, 2)]
-        up = [radial(rows[f], coef) for f in (0, 3)]
-        metric = [lambda n, c=c: mm[c, 4 * e + n] for c in range(3)]
-        sources = [lambda n, c=c: sm[source, c, 4 * e + n] for c in range(3)]
-        for n, *values in rates(rows, metric, sources, stream, around, up):
-            for f in range(4):
-                if final:
-                    out[f, pl.ds(4 * e + n - 16, 8, stride=sector), :] = values[f]
-                else:
-                    wm[1 - now, f, 4 * e + n] = values[f]
-        if not final:
-            stream = stream_halo(fields, halos, w_halo, coef, CAA_WIDTH)
-            around = [azimuth_halo(tiles[f], wt[now, f, tile_below], wt[now, f, tile_above], coef, CAA_WIDTH) for f in (0, 2)]
-            up = [radial(tiles[f], coef) for f in (0, 3)]
-            metric = [lambda n, c=c: mt[c, e + n] for c in range(3)]
-            sources = [lambda n, c=c: st[source, c, e + n] for c in range(3)]
-            for n, *values in rates(tiles, metric, sources, stream, around, up):
-                for f in range(4):
-                    wt[1 - now, f, e + n] = values[f]
+
+        def store(f, n, value):
+            if final:
+                out[f, pl.ds(4 * e + n - 16, 8, stride=sector), :] = value
+            else:
+                wm[1 - now, f, 4 * e + n] = value
+
+        update(rows, lambda c, n: mm[c, 4 * e + n], lambda c, n: sm[source, c, 4 * e + n], stream, around, up, store)
+        if final:
+            return
+
+        stream = along([tile for values in halos for tile in values], 1)
+        stream = [[stream[2 * f + n] for n in range(2)] for f in range(4)]
+        run = lanes_of() // 32
+        for f in range(4):
+            for n in range(2):
+                edge = None
+                for i in range(4):
+                    moved = lane_roll(fields[f][4 * n + i], 32 * i + 16)
+                    edge = moved if edge is None else jnp.where(run == i, moved, edge)
+                stream[f][n] = stream[f][n] + coef[9] * edge
+        around = []
+        for f in (0, 2):
+            values = []
+            for n in range(2):
+                before = wt[now, f, tile_below] if n == 0 else tiles[f][0]
+                after = wt[now, f, tile_above] if n == 1 else tiles[f][1]
+                total = coef[WHOLE_P] * lane_roll(before, -96) + coef[WHOLE_N] * lane_roll(after, 96)
+                for k, offset in enumerate(OFFSETS):
+                    total = total + coef[WHOLE_T + k] * lane_roll(tiles[f][n], -32 * offset)
+                values.append(total)
+            around.append(values)
+
+        def store(f, n, value):
+            wt[1 - now, f, e + n] = value
+
+        up = [values[8:] for values in up]
+        update(tiles, lambda c, n: mt[c, e + n], lambda c, n: st[source, c, e + n], stream, around, up, store)
 
     for step, (start, stop) in enumerate(CAA_RANGES):
-
-        @pl.loop(0, (stop - start) // 2)
-        def _(n):
-            pair(step % 2, step // 4, start + 2 * n, step == 7)
+        for e in range(start, stop, 2):
+            pair(step % 2, step // 4, e, step == 7)
 
 
 def call(kernel, name, outs, *args, smem=0, far=0, scratch=()):
@@ -590,8 +672,9 @@
     lines = radial_nodes * sector
     u, lm, w, m = (x.reshape(-1, lines, length) for x in (les_velocity, les_metric, caa_state, caa_metric))
     les_weights = jnp.asarray(np.stack([split_matrix(128), split_matrix(LES_WIDTH)]))
-    caa_weights = jnp.asarray(np.stack([split_matrix(128), split_matrix(CAA_WIDTH)]))
-    les_coef, caa_coef = jnp.asarray(coefficients(LES_WIDTH)), jnp.asarray(coefficients(CAA_WIDTH))
+    les_coef = jnp.asarray(coefficients(LES_WIDTH))
+    caa_weights, caa_coef = jnp.asarray(acoustic_weights()), jnp.asarray(acoustic_coefficients())
+    upward, order = jnp.asarray(radial_matrix(10)), jnp.asarray(halo_order())
     own_row = lax.axis_index("sec") * slabs + lax.axis_index("gx")
     sends = lax.dynamic_slice_in_dim(send_list, own_row, 1, axis=0).reshape(-1)
     tile = (8, 128)
@@ -636,17 +719,18 @@
         functools.partial(state_pack_kernel, sector),
         "state_pack",
         [((42, *tile), BF16)] * 2,
-        caa_below, caa_above, both,
+        caa_below, caa_above, both, order,
     )
     state_left, state_right = both_ways(first, last, STREAM, False)
-    got, state_left, state_right, les_out = lax.optimization_barrier((got, state_left, state_right, les_out))
+    table = jnp.concatenate([intersection_refs.reshape(-1), offsets])
+    got, table, state_left, state_right, les_out = lax.optimization_barrier((got, table, state_left, state_right, les_out))
 
     own, up, down = call(
         functools.partial(blend_kernel, sector),
         "blend",
         [((2, 3, sector, *tile), F32), ((72, *tile), BF16), ((72, *tile), BF16)],
-        intersection_refs.reshape(-1), offsets, got,
-        smem=2,
+        table, got,
+        smem=1,
         scratch=[vmem(6, 16)],
     )
     below, above = both_ways(down, up, "az", True)
@@ -654,14 +738,14 @@
         functools.partial(source_pack_kernel, sector),
         "source_pack",
         [((30, *tile), BF16)] * 2,
-        own, below, above,
+        own, below, above, order,
     )
     from_left, from_right = both_ways(first, last, STREAM, False)
     (caa_out,) = call(
         functools.partial(caa_kernel, sector),
         "caa",
         [((4, lines, length), F32)],
-        w, m, own, below, above, caa_below, caa_above, state_left, state_right, from_left, from_right, caa_weights, caa_coef,
+        w, m, own, below, above, caa_below, caa_above, state_left, state_right, from_left, from_right, caa_weights, caa_coef, upward,
         scratch=[vmem(2, 4, 48), vmem(2, 4, 12), vmem(3, 48), vmem(3, 12), vmem(2, 3, 48), vmem(2, 3, 12)],
     )
     return les_out.reshape(les_velocity.shape), caa_out.reshape(caa_state.shape)

time: 92.3 us -> 87.3 us (0.946)
  Pallas kernels: 19.3 us -> 14.4 us
    pallas_call x9, Pallas kernels: 19.3 us -> 14.4 us  [call(): pl.pallas_call(kernel, name=name, out_shape=[jax.ShapeDtypeStruct(shape,...]
  transfers between devices with their start and end apart: 13 -> 13, of which waited for: 10 -> 10; matrix products, arithmetic and copies ran while one was open for 1% -> 1% of each run, Pallas kernels for 2% -> 3%
where the time goes in v3:
time: 87.3 us; the launch traced here: 86.9 us
  starting transfers between devices  45.4 us (52%)
  waiting for transfers between devices  25.3 us (29%)
  Pallas kernels  14.4 us (16%)
  local copies, waits for them, and re-layouts  0.89 us (1%)
    ppermute x6, starting transfers between devices, both_ways(): above = lax.ppermute(low, axis, [((i + 1) % count, i) for i in range(ends)])  21.2 us
    ppermute x6, starting transfers between devices, both_ways(): lax.ppermute(high, axis, [(i, (i + 1) % count) for i in range(ends)])  16.6 us
    pallas_call x9, Pallas kernels, call(): pl.pallas_call(kernel, name=name, out_shape=[jax.ShapeDtypeStruct(shape,...  14.4 us
    ppermute x6, waiting for transfers between devices, both_ways(): above = lax.ppermute(low, axis, [((i + 1) % count, i) for i in range(ends)])  12.5 us
    ppermute x6, waiting for transfers between devices, both_ways(): lax.ppermute(high, axis, [(i, (i + 1) % count) for i in range(ends)])  10.9 us
    all_to_all x1, starting transfers between devices, body(): lax.all_to_all(sent.reshape(slabs, 96, 128), 'gx', 0, 0, tiled=True)  7.6 us
    all_to_all x1, waiting for transfers between devices, body(): lax.all_to_all(sent.reshape(slabs, 96, 128), 'gx', 0, 0, tiled=True)  1.85 us
  transfers between devices with their start and end apart: 13, of which 10 were waited for; matrix products, arithmetic and copies ran while one was open for 1% of the time, Pallas kernels for 3%

profile of v3, /device:TPU:29, one launch (start us, length us, event | category | flops | bytes accessed | tf_op | source)
XLA Modules:
  0.0 86.9 jit_solution(16128764015963831340)
XLA Ops:
  0.6 0.0 copy-start
  0.6 0.0 copy-start.1
  0.7 0.0 copy-start.2
  0.7 1.8 %first.1 = (f32[15,8,128]{2,1,0:T(8,128)}, f32[15,8,128]{2,1,0:T(8,128)}) custom-call(f32[3,128,128]{2,1,0:T(8,128)} %bitcast.13, f32[3,128,128]{2,1,0:T(8,128)} %bitcast.8), custom_call_target="tpu_custom_call" | custom-call | tf_op jit(solution)/shard_map/first/pallas_call | solution.py:649
  2.4 3.1 %collective-permute-start = (f32[15,8,128]{2,1,0:T(8,128)}, f32[15,8,128]{2,1,0:T(8,128)S(1)}, u32[]{:S(2)}, u32[]{:S(2)}) collective-permute-start(f32[15,8,128]{2,1,0:T(8,128)} %get-tuple-element.21), channel_id=1, source_target_pairs={{0,1},{1,2},{2,3},{3,4},{4,5},{5,6},{6,7},{7,8},{8,9},{9,10},{10,1... | collective-permute-start | bytes 184328 | tf_op jit(solution)/shard_map/ppermute | solution.py:663
  5.5 0.0 copy-start.4
  5.5 0.0 collective-permute-start.1
  5.5 1.6 %collective-permute-done.before = f32[15,8,128]{2,1,0:T(8,128)S(1)} collective-permute-done((f32[15,8,128]{2,1,0:T(8,128)}, f32[15,8,128]{2,1,0:T(8,128)S(1)}, u32[]{:S(2)}, u32[]{:S(2)}) %collective-permute-start) | collective-permute-done | bytes 61472 | tf_op jit(solution)/shard_map/ppermute | solution.py:663
  7.1 3.5 %collective-permute-done.1.after = f32[15,8,128]{2,1,0:T(8,128)S(1)} collective-permute-done((f32[15,8,128]{2,1,0:T(8,128)}, f32[15,8,128]{2,1,0:T(8,128)S(1)}, u32[]{:S(2)}, u32[]{:S(2)}) %collective-permute-start.1) | collective-permute-done | bytes 61472 | tf_op jit(solution)/shard_map/ppermute | solution.py:664
  10.6 0.0 copy-done.1
  10.6 0.0 copy-done.2
  10.6 0.3 les_pack.1
  10.9 0.0 copy-start.7
  10.9 4.1 %collective-permute-start.2 = (f32[4,8,128]{2,1,0:T(8,128)S(1)}, f32[4,8,128]{2,1,0:T(8,128)S(1)}, u32[]{:S(2)}, u32[]{:S(2)}) collective-permute-start(f32[4,8,128]{2,1,0:T(8,128)S(1)} %get-tuple-element.23), channel_id=1, source_target_pairs={{0,16},{16,32},{32,48},{48,64},{64,80},{80,96},{96,112},{112,128},... | collective-permute-start | bytes 49160 | tf_op jit(solution)/shard_map/ppermute | solution.py:663
  15.1 12.2 %collective-permute-start.3 = (f32[4,8,128]{2,1,0:T(8,128)S(1)}, f32[4,8,128]{2,1,0:T(8,128)S(1)}, u32[]{:S(2)}, u32[]{:S(2)}) collective-permute-start(f32[4,8,128]{2,1,0:T(8,128)S(1)} %get-tuple-element.24), channel_id=1, source_target_pairs={{16,0},{32,16},{48,32},{64,48},{80,64},{96,80},{112,96},{128,112},... | collective-permute-start | bytes 49160 | tf_op jit(solution)/shard_map/ppermute | solution.py:664
  27.3 0.0 copy-done
  27.3 0.6 dynamic-slice_reduce_fusion
  27.9 0.1 reshape.34.sends
  28.0 0.0 collective-permute-done.2.from_left
  28.0 0.2 collective-permute-done.3.from_right
  28.1 0.0 copy-done.4
  28.1 0.0 copy-done.7
  28.1 3.8 %les.1 = (bf16[48,6,8,128]{3,2,1,0:T(8,128)(2,1)}, f32[3,24,8,128]{3,2,1,0:T(8,128)S(1)}, f32[3,4,8,128]{3,2,1,0:T(8,128)S(1)}) custom-call(s32[48]{0:T(128)S(1)} %reshape.34.sends, f32[3,128,128]{2,1,0:T(8,128)S(1)} %bitcast.15, f32[3,128,128]{2,1,0:T(8,128)S(1)} %bitcast.10, f32[15,8,128]{2,1,0:T(8,128)S(1)} %collective-permute-done.before, ...), custom_call_target="tpu_custom_call" | custom-call | tf_op jit(solution)/shard_map/les/pallas_call | solution.py:649
  31.9 0.0 copy-start.3
  31.9 0.0 copy-start.5
  31.9 7.6 %all-to-all-start = ((bf16[24,96,128]{2,1,0:T(8,128)(2,1)}), bf16[24,96,128]{2,1,0:T(8,128)(2,1)S(1)}, u32[]{:S(2)}, u32[]{:S(2)}) async-start(bf16[24,96,128]{2,1,0:T(8,128)(2,1)} %bitcast.2), calls=%async_computation | async-start | bytes 1179648 | tf_op jit(solution)/shard_map/all_to_all | solution.py:707
  39.5 0.0 copy-done.3
  39.5 0.0 copy-done.5
  39.5 0.0 copy-start.11
  39.5 0.0 copy-start.6
  39.6 0.2 narrow.1.both
  39.7 1.8 %collective-permute-start.4 = (bf16[112,8,128]{2,1,0:T(8,128)(2,1)S(1)}, bf16[112,8,128]{2,1,0:T(8,128)(2,1)S(1)}, u32[]{:S(2)}, u32[]{:S(2)}) collective-permute-start(bf16[112,8,128]{2,1,0:T(8,128)(2,1)S(1)} %narrow.1.both), channel_id=1, source_target_pairs={{0,1},{1,2},{2,3},{3,4},{4,5},{5,6},{6,7},{7,8},{8,9},{9,10},{10,1... | collective-permute-start | bytes 688136 | tf_op jit(solution)/shard_map/ppermute | solution.py:663
  41.5 0.0 collective-permute-start.5
  41.5 0.0 copy-done.11
  41.5 0.1 copy.16
  41.6 0.1 reshape.39
  41.7 2.8 %collective-permute-done.4.below.caa_below = bf16[112,8,128]{2,1,0:T(8,128)(2,1)S(1)} collective-permute-done((bf16[112,8,128]{2,1,0:T(8,128)(2,1)S(1)}, bf16[112,8,128]{2,1,0:T(8,128)(2,1)S(1)}, u32[]{:S(2)}, u32[]{:S(2)}) %collective-permute-start.4) | collective-permute-done | bytes 229408 | tf_op jit(solution)/shard_map/ppermute | solution.py:663
  44.5 4.0 %collective-permute-done.5.above.caa_above = bf16[112,8,128]{2,1,0:T(8,128)(2,1)S(1)} collective-permute-done((bf16[112,8,128]{2,1,0:T(8,128)(2,1)S(1)}, bf16[112,8,128]{2,1,0:T(8,128)(2,1)S(1)}, u32[]{:S(2)}, u32[]{:S(2)}) %collective-permute-start.5) | collective-permute-done | bytes 229408 | tf_op jit(solution)/shard_map/ppermute | solution.py:664
  48.5 0.0 copy-done.6
  48.5 0.5 state_pack.1
  49.0 0.0 copy-start.12
  49.0 3.6 %collective-permute-start.6 = (bf16[42,8,128]{2,1,0:T(8,128)(2,1)S(1)}, bf16[42,8,128]{2,1,0:T(8,128)(2,1)S(1)}, u32[]{:S(2)}, u32[]{:S(2)}) collective-permute-start(bf16[42,8,128]{2,1,0:T(8,128)(2,1)S(1)} %get-tuple-element.26), channel_id=1, source_target_pairs={{0,16},{16,32},{32,48},{48,64},{64,80},{80,96},{96,112},{112,128},... | collective-permute-start | bytes 258056 | tf_op jit(solution)/shard_map/ppermute | solution.py:663
  52.6 3.9 %collective-permute-start.7 = (bf16[42,8,128]{2,1,0:T(8,128)(2,1)S(1)}, bf16[42,8,128]{2,1,0:T(8,128)(2,1)S(1)}, u32[]{:S(2)}, u32[]{:S(2)}) collective-permute-start(bf16[42,8,128]{2,1,0:T(8,128)(2,1)S(1)} %get-tuple-element.27), channel_id=1, source_target_pairs={{16,0},{32,16},{48,32},{64,48},{80,64},{96,80},{112,96},{128,112},... | collective-permute-start | bytes 258056 | tf_op jit(solution)/shard_map/ppermute | solution.py:664
  56.5 0.0 copy-done.12
  56.5 0.1 pad_add_fusion.refs
  56.6 1.6 %les_out.1 = f32[3,128,128]{2,1,0:T(8,128)} custom-call(f32[3,128,128]{2,1,0:T(8,128)S(1)} %bitcast.11, f32[3,24,8,128]{3,2,1,0:T(8,128)S(1)} %get-tuple-element.28.um1, f32[3,4,8,128]{3,2,1,0:T(8,128)S(1)} %get-tuple-element.29.ut1, bf16[2,256,256]{2,1,0:T(8,128)(2,1)S(1)} %copy-done.4, f32[16,8,128]{2,1,0:T(8,128)S(1)} %copy-done.7), custom_call_target="tpu_custom_call" | custom-call | tf_op jit(solution)/shard_map/les_out/pallas_call | solution.py:649
  58.2 4.4 %collective-permute-done.6.state_left = bf16[42,8,128]{2,1,0:T(8,128)(2,1)S(1)} collective-permute-done((bf16[42,8,128]{2,1,0:T(8,128)(2,1)S(1)}, bf16[42,8,128]{2,1,0:T(8,128)(2,1)S(1)}, u32[]{:S(2)}, u32[]{:S(2)}) %collective-permute-start.6) | collective-permute-done | bytes 86048 | tf_op jit(solution)/shard_map/ppermute | solution.py:663
  62.6 0.0 collective-permute-done.7.state_right
  62.6 1.8 %all-to-all-done = bf16[24,96,128]{2,1,0:T(8,128)(2,1)S(1)} async-done(((bf16[24,96,128]{2,1,0:T(8,128)(2,1)}), bf16[24,96,128]{2,1,0:T(8,128)(2,1)S(1)}, u32[]{:S(2)}, u32[]{:S(2)}) %all-to-all-start) | async-done | bytes 589856 | tf_op jit(solution)/shard_map/all_to_all | solution.py:707
  64.4 1.4 %blend.1 = (f32[2,3,16,8,128]{4,3,2,1,0:T(8,128)S(1)}, bf16[72,8,128]{2,1,0:T(8,128)(2,1)S(1)}, bf16[72,8,128]{2,1,0:T(8,128)(2,1)S(1)}) custom-call(s32[80]{0:T(128)S(1)} %pad_add_fusion.refs, bf16[48,6,8,128]{3,2,1,0:T(8,128)(2,1)S(1)} %bitcast.12), custom_call_target="tpu_custom_call" | custom-call | tf_op jit(solution)/shard_map/blend/pallas_call | solution.py:649
  65.9 1.7 %collective-permute-start.8 = (bf16[72,8,128]{2,1,0:T(8,128)(2,1)S(1)}, bf16[72,8,128]{2,1,0:T(8,128)(2,1)S(1)}, u32[]{:S(2)}, u32[]{:S(2)}) collective-permute-start(bf16[72,8,128]{2,1,0:T(8,128)(2,1)S(1)} %get-tuple-element.34), channel_id=1, source_target_pairs={{0,1},{1,2},{2,3},{3,4},{4,5},{5,6},{6,7},{7,8},{8,9},{9,10},{10,1... | collective-permute-start | bytes 442376 | tf_op jit(solution)/shard_map/ppermute | solution.py:663
  67.5 0.0 collective-permute-start.9
  67.5 2.1 %collective-permute-done.8.below = bf16[72,8,128]{2,1,0:T(8,128)(2,1)S(1)} collective-permute-done((bf16[72,8,128]{2,1,0:T(8,128)(2,1)S(1)}, bf16[72,8,128]{2,1,0:T(8,128)(2,1)S(1)}, u32[]{:S(2)}, u32[]{:S(2)}) %collective-permute-start.8) | collective-permute-done | bytes 147488 | tf_op jit(solution)/shard_map/ppermute | solution.py:663
  69.6 3.7 %collective-permute-done.9.above = bf16[72,8,128]{2,1,0:T(8,128)(2,1)S(1)} collective-permute-done((bf16[72,8,128]{2,1,0:T(8,128)(2,1)S(1)}, bf16[72,8,128]{2,1,0:T(8,128)(2,1)S(1)}, u32[]{:S(2)}, u32[]{:S(2)}) %collective-permute-start.9) | collective-permute-done | bytes 147488 | tf_op jit(solution)/shard_map/ppermute | solution.py:664
  73.3 0.0 copy-start.8
  73.3 0.4 source_pack.1
  73.7 2.3 %collective-permute-start.10 = (bf16[30,8,128]{2,1,0:T(8,128)(2,1)S(1)}, bf16[30,8,128]{2,1,0:T(8,128)(2,1)S(1)}, u32[]{:S(2)}, u32[]{:S(2)}) collective-permute-start(bf16[30,8,128]{2,1,0:T(8,128)(2,1)S(1)} %get-tuple-element.38), channel_id=1, source_target_pairs={{0,16},{16,32},{32,48},{48,64},{64,80},{80,96},{96,112},{112,128},... | collective-permute-start | bytes 184328 | tf_op jit(solution)/shard_map/ppermute | solution.py:663
  76.0 5.1 %collective-permute-start.11 = (bf16[30,8,128]{2,1,0:T(8,128)(2,1)S(1)}, bf16[30,8,128]{2,1,0:T(8,128)(2,1)S(1)}, u32[]{:S(2)}, u32[]{:S(2)}) collective-permute-start(bf16[30,8,128]{2,1,0:T(8,128)(2,1)S(1)} %get-tuple-element.39), channel_id=1, source_target_pairs={{16,0},{32,16},{48,32},{64,48},{80,64},{96,80},{112,96},{128,112},... | collective-permute-start | bytes 184328 | tf_op jit(solution)/shard_map/ppermute | solution.py:664
  81.1 0.0 collective-permute-done.10.from_left
  81.1 1.3 %collective-permute-done.11.from_right = bf16[30,8,128]{2,1,0:T(8,128)(2,1)S(1)} collective-permute-done((bf16[30,8,128]{2,1,0:T(8,128)(2,1)S(1)}, bf16[30,8,128]{2,1,0:T(8,128)(2,1)S(1)}, u32[]{:S(2)}, u32[]{:S(2)}) %collective-permute-start.11) | collective-permute-done | bytes 61472 | tf_op jit(solution)/shard_map/ppermute | solution.py:664
  82.4 0.0 copy-done.8
  82.4 0.0 copy-done.9
  82.4 0.0 copy-done.10
  82.4 4.5 %caa.1 = f32[4,128,128]{2,1,0:T(8,128)} custom-call(f32[4,128,128]{2,1,0:T(8,128)S(1)} %bitcast.17, f32[3,128,128]{2,1,0:T(8,128)S(1)} %bitcast.19, f32[2,3,16,8,128]{4,3,2,1,0:T(8,128)S(1)} %get-tuple-element.33.own, bf16[72,8,128]{2,1,0:T(8,128)(2,1)S(1)} %collective-permute-done.8.below, bf16[72,8,128]{2,1,0:T(8,128)(2,1)S(1)} %collective-permute-done.9.above, ...), custom_call_target="tpu_custom_call" | custom-call | tf_op jit(solution)/shard_map/caa/pallas_call | solution.py:649
  (2 shorter events, 0.0 us)
Async XLA Ops:
  0.6 26.7 %copy-start = (s32[48,24,2]{0,2,1:T(2,128)S(1)}, s32[48,24,2]{0,2,1:T(2,128)}, u32[]{:S(2)}) copy-start(s32[48,24,2]{0,2,1:T(2,128)} %param.19) | copy-start | bytes 27652
  0.6 10.0 %copy-start.1 = (f32[3,8,16,128]{3,2,1,0:T(8,128)S(1)}, f32[3,8,16,128]{3,2,1,0:T(8,128)}, u32[]{:S(2)}) copy-start(f32[3,8,16,128]{3,2,1,0:T(8,128)} %param.14) | copy-start | bytes 589828
  0.7 9.9 %copy-start.2 = (f32[3,8,16,128]{3,2,1,0:T(8,128)S(1)}, f32[3,8,16,128]{3,2,1,0:T(8,128)}, u32[]{:S(2)}) copy-start(f32[3,8,16,128]{3,2,1,0:T(8,128)} %param.13) | copy-start | bytes 589828
  2.4 4.7 %collective-permute-start = (f32[15,8,128]{2,1,0:T(8,128)}, f32[15,8,128]{2,1,0:T(8,128)S(1)}, u32[]{:S(2)}, u32[]{:S(2)}) collective-permute-start(f32[15,8,128]{2,1,0:T(8,128)} %get-tuple-element.21), channel_id=1, source_target_pairs={{0,1},{1,2},{2,3},{3,4},{4,5},{5,6},{6,7},{7,8},{8,9},{9,10},{10,1... | collective-permute-start | bytes 184328 | tf_op jit(solution)/shard_map/ppermute | solution.py:663
  5.5 22.6 %copy-start.4 = (bf16[2,256,256]{2,1,0:T(8,128)(2,1)S(1)}, bf16[2,256,256]{2,1,0:T(8,128)(2,1)}, u32[]{:S(2)}) copy-start(bf16[2,256,256]{2,1,0:T(8,128)(2,1)} %constant.28.clone.weights) | copy-start | bytes 786436
  5.5 5.1 %collective-permute-start.1 = (f32[15,8,128]{2,1,0:T(8,128)}, f32[15,8,128]{2,1,0:T(8,128)S(1)}, u32[]{:S(2)}, u32[]{:S(2)}) collective-permute-start(f32[15,8,128]{2,1,0:T(8,128)} %get-tuple-element.22), channel_id=1, source_target_pairs={{1,0},{2,1},{3,2},{4,3},{5,4},{6,5},{7,6},{8,7},{9,8},{10,9},{11,1... | collective-permute-start | bytes 184328 | tf_op jit(solution)/shard_map/ppermute | solution.py:664
  10.9 17.2 %copy-start.7 = (f32[16,8,128]{2,1,0:T(8,128)S(1)}, f32[16,8,128]{2,1,0:T(8,128)}, u32[]{:S(2)}) copy-start(f32[16,8,128]{2,1,0:T(8,128)} %constant.29.clone.coef) | copy-start | bytes 196612
  10.9 17.0 %collective-permute-start.2 = (f32[4,8,128]{2,1,0:T(8,128)S(1)}, f32[4,8,128]{2,1,0:T(8,128)S(1)}, u32[]{:S(2)}, u32[]{:S(2)}) collective-permute-start(f32[4,8,128]{2,1,0:T(8,128)S(1)} %get-tuple-element.23), channel_id=1, source_target_pairs={{0,16},{16,32},{32,48},{48,64},{64,80},{80,96},{96,112},{112,128},... | collective-permute-start | bytes 49160 | tf_op jit(solution)/shard_map/ppermute | solution.py:663
  15.1 13.1 %collective-permute-start.3 = (f32[4,8,128]{2,1,0:T(8,128)S(1)}, f32[4,8,128]{2,1,0:T(8,128)S(1)}, u32[]{:S(2)}, u32[]{:S(2)}) collective-permute-start(f32[4,8,128]{2,1,0:T(8,128)S(1)} %get-tuple-element.24), channel_id=1, source_target_pairs={{16,0},{32,16},{48,32},{64,48},{80,64},{96,80},{112,96},{128,112},... | collective-permute-start | bytes 49160 | tf_op jit(solution)/shard_map/ppermute | solution.py:664
  31.9 7.6 %copy-start.3 = (f32[4,8,16,128]{3,2,1,0:T(8,128)S(1)}, f32[4,8,16,128]{3,2,1,0:T(8,128)}, u32[]{:S(2)}) copy-start(f32[4,8,16,128]{3,2,1,0:T(8,128)} %param.15) | copy-start | bytes 786436
  31.9 7.6 %copy-start.5 = (f32[3,8,16,128]{3,2,1,0:T(8,128)S(1)}, f32[3,8,16,128]{3,2,1,0:T(8,128)}, u32[]{:S(2)}) copy-start(f32[3,8,16,128]{3,2,1,0:T(8,128)} %param.16) | copy-start | bytes 589828
  31.9 32.5 %all-to-all-start = ((bf16[24,96,128]{2,1,0:T(8,128)(2,1)}), bf16[24,96,128]{2,1,0:T(8,128)(2,1)S(1)}, u32[]{:S(2)}, u32[]{:S(2)}) async-start(bf16[24,96,128]{2,1,0:T(8,128)(2,1)} %bitcast.2), calls=%async_computation | async-start | bytes 1179648 | tf_op jit(solution)/shard_map/all_to_all | solution.py:707
  39.5 2.0 %copy-start.11 = (s32[16,4]{0,1:T(4,128)S(1)}, s32[16,4]{0,1:T(4,128)}, u32[]{:S(2)}) copy-start(s32[16,4]{0,1:T(4,128)} %param.17) | copy-start | bytes 772
  39.5 8.9 %copy-start.6 = (bf16[2,128,128]{2,1,0:T(8,128)(2,1)S(1)}, bf16[2,128,128]{2,1,0:T(8,128)(2,1)}, u32[]{:S(2)}) copy-start(bf16[2,128,128]{2,1,0:T(8,128)(2,1)} %constant.33.clone.order) | copy-start | bytes 196612
  39.7 4.8 %collective-permute-start.4 = (bf16[112,8,128]{2,1,0:T(8,128)(2,1)S(1)}, bf16[112,8,128]{2,1,0:T(8,128)(2,1)S(1)}, u32[]{:S(2)}, u32[]{:S(2)}) collective-permute-start(bf16[112,8,128]{2,1,0:T(8,128)(2,1)S(1)} %narrow.1.both), channel_id=1, source_target_pairs={{0,1},{1,2},{2,3},{3,4},{4,5},{5,6},{6,7},{7,8},{8,9},{9,10},{10,1... | collective-permute-start | bytes 688136 | tf_op jit(solution)/shard_map/ppermute | solution.py:663
  41.5 7.0 %collective-permute-start.5 = (bf16[112,8,128]{2,1,0:T(8,128)(2,1)S(1)}, bf16[112,8,128]{2,1,0:T(8,128)(2,1)S(1)}, u32[]{:S(2)}, u32[]{:S(2)}) collective-permute-start(bf16[112,8,128]{2,1,0:T(8,128)(2,1)S(1)} %narrow.1.both), channel_id=1, source_target_pairs={{1,0},{2,1},{3,2},{4,3},{5,4},{6,5},{7,6},{8,7},{9,8},{10,9},{11,1... | collective-permute-start | bytes 688136 | tf_op jit(solution)/shard_map/ppermute | solution.py:664
  49.0 7.6 %copy-start.12 = (s32[16]{0:T(128)S(1)}, s32[16]{0:T(128)}, u32[]{:S(2)}) copy-start(s32[16]{0:T(128)} %param.18) | copy-start | bytes 196
  49.0 13.6 %collective-permute-start.6 = (bf16[42,8,128]{2,1,0:T(8,128)(2,1)S(1)}, bf16[42,8,128]{2,1,0:T(8,128)(2,1)S(1)}, u32[]{:S(2)}, u32[]{:S(2)}) collective-permute-start(bf16[42,8,128]{2,1,0:T(8,128)(2,1)S(1)} %get-tuple-element.26), channel_id=1, source_target_pairs={{0,16},{16,32},{32,48},{48,64},{64,80},{80,96},{96,112},{112,128},... | collective-permute-start | bytes 258056 | tf_op jit(solution)/shard_map/ppermute | solution.py:663
  52.6 10.0 %collective-permute-start.7 = (bf16[42,8,128]{2,1,0:T(8,128)(2,1)S(1)}, bf16[42,8,128]{2,1,0:T(8,128)(2,1)S(1)}, u32[]{:S(2)}, u32[]{:S(2)}) collective-permute-start(bf16[42,8,128]{2,1,0:T(8,128)(2,1)S(1)} %get-tuple-element.27), channel_id=1, source_target_pairs={{16,0},{32,16},{48,32},{64,48},{80,64},{96,80},{112,96},{128,112},... | collective-permute-start | bytes 258056 | tf_op jit(solution)/shard_map/ppermute | solution.py:664
  65.9 3.8 %collective-permute-start.8 = (bf16[72,8,128]{2,1,0:T(8,128)(2,1)S(1)}, bf16[72,8,128]{2,1,0:T(8,128)(2,1)S(1)}, u32[]{:S(2)}, u32[]{:S(2)}) collective-permute-start(bf16[72,8,128]{2,1,0:T(8,128)(2,1)S(1)} %get-tuple-element.34), channel_id=1, source_target_pairs={{0,1},{1,2},{2,3},{3,4},{4,5},{5,6},{6,7},{7,8},{8,9},{9,10},{10,1... | collective-permute-start | bytes 442376 | tf_op jit(solution)/shard_map/ppermute | solution.py:663
  67.5 5.8 %collective-permute-start.9 = (bf16[72,8,128]{2,1,0:T(8,128)(2,1)S(1)}, bf16[72,8,128]{2,1,0:T(8,128)(2,1)S(1)}, u32[]{:S(2)}, u32[]{:S(2)}) collective-permute-start(bf16[72,8,128]{2,1,0:T(8,128)(2,1)S(1)} %get-tuple-element.35), channel_id=1, source_target_pairs={{1,0},{2,1},{3,2},{4,3},{5,4},{6,5},{7,6},{8,7},{9,8},{10,9},{11,1... | collective-permute-start | bytes 442376 | tf_op jit(solution)/shard_map/ppermute | solution.py:664
  73.3 9.1 %copy-start.8 = (bf16[2,128,256]{2,1,0:T(8,128)(2,1)S(1)}, bf16[2,128,256]{2,1,0:T(8,128)(2,1)}, u32[]{:S(2)}) copy-start(bf16[2,128,256]{2,1,0:T(8,128)(2,1)} %constant.30.clone.weights) | copy-start | bytes 393220
  73.3 9.1 %copy-start.9 = (f32[10,8,128]{2,1,0:T(8,128)S(1)}, f32[10,8,128]{2,1,0:T(8,128)}, u32[]{:S(2)}) copy-start(f32[10,8,128]{2,1,0:T(8,128)} %constant.31.clone.coef) | copy-start | bytes 122884
  73.3 9.1 %copy-start.10 = (bf16[160,80]{1,0:T(8,128)(2,1)S(1)}, bf16[160,80]{1,0:T(8,128)(2,1)}, u32[]{:S(2)}) copy-start(bf16[160,80]{1,0:T(8,128)(2,1)} %constant.32.clone.upward) | copy-start | bytes 76804
  73.7 7.4 %collective-permute-start.10 = (bf16[30,8,128]{2,1,0:T(8,128)(2,1)S(1)}, bf16[30,8,128]{2,1,0:T(8,128)(2,1)S(1)}, u32[]{:S(2)}, u32[]{:S(2)}) collective-permute-start(bf16[30,8,128]{2,1,0:T(8,128)(2,1)S(1)} %get-tuple-element.38), channel_id=1, source_target_pairs={{0,16},{16,32},{32,48},{48,64},{64,80},{80,96},{96,112},{112,128},... | collective-permute-start | bytes 184328 | tf_op jit(solution)/shard_map/ppermute | solution.py:663
  76.0 6.4 %collective-permute-start.11 = (bf16[30,8,128]{2,1,0:T(8,128)(2,1)S(1)}, bf16[30,8,128]{2,1,0:T(8,128)(2,1)S(1)}, u32[]{:S(2)}, u32[]{:S(2)}) collective-permute-start(bf16[30,8,128]{2,1,0:T(8,128)(2,1)S(1)} %get-tuple-element.39), channel_id=1, source_target_pairs={{16,0},{32,16},{48,32},{64,48},{80,64},{96,80},{112,96},{128,112},... | collective-permute-start | bytes 184328 | tf_op jit(solution)/shard_map/ppermute | solution.py:664

commit v4 on v3

--- a/solution.py
+++ b/solution.py
@@ -234,6 +234,18 @@
     return out
 
 
+class Side:
+    def __init__(self, mask, first, second):
+        self.mask, self.first, self.second = mask[...] > 0.5, first, second
+
+    def __getitem__(self, at):
+        return jnp.where(self.mask, self.first[at].astype(F32), self.second[at].astype(F32))
+
+
+def sides(mask, even, odd):
+    return Side(mask, odd, even), Side(mask, even, odd)
+
+
 def halo_tile(from_left, from_right, n, width):
     count = 32 // width
     left, right = from_left[n // count].astype(F32), from_right[n // count].astype(F32)
@@ -291,7 +303,8 @@
             both[f * sector + az] = value.astype(BF16)
 
 
-def les_pack_kernel(sector, u, lm, before, after, first, last):
+def les_pack_kernel(sector, u, lm, before, after, mask, even, odd):
+    right = mask[...] > 0.5
     entries = []
     for c in range(3):
         for e in range(-1, 5):
@@ -306,8 +319,9 @@
             entries.append([(lm, (c, pl.ds(4 * e + i, 8, stride=sector), slice(None))) for i in range(4)])
     for n in range(4):
         rows = [ref[at] for entry in entries[8 * n : 8 * n + 8] for ref, at in entry]
-        first[n] = pack(rows, False, LES_WIDTH)
-        last[n] = pack(rows, True, LES_WIDTH)
+        first, last = pack(rows, False, LES_WIDTH), pack(rows, True, LES_WIDTH)
+        even[n] = jnp.where(right, last, first)
+        odd[n] = jnp.where(right, first, last)
 
 
 def les_element(um, ut, mm, e, weights, coef, with_flux):
@@ -352,7 +366,12 @@
         lamb[2, 4 * e + i] = first * rows[1][i] - second * rows[0][i]
 
 
-def les_kernel(sector, sends, u, lm, before, after, from_left, from_right, weights, coef, sent, um1, ut1, um, ut, mm, mt, lamb, blk):
+def les_kernel(
+    sector, sends_far, u, lm, before, after, odd, even, mask, weights, coef, sent, um1, ut1, um, ut, mm, mt, lamb, blk, sends, arrived, gone,
+):
+    fetch = pltpu.make_async_copy(sends_far, sends, arrived)
+    fetch.start()
+    from_left, from_right = sides(mask, even, odd)
     for c in range(3):
         for i in range(4):
             um[c, i] = before[4 * c + i]
@@ -420,17 +439,26 @@
             for j in range(16):
                 blk[j, 3 * step + c] = tiles[j].astype(BF16)
 
+    def send(step):
+        part = pl.ds(3 * step, 3)
+        copies = []
+        for n in range(sends.shape[0]):
+            index = jnp.clip(sends[n], 0, 15)
+            copies.append(pltpu.make_async_copy(blk.at[index, part], sent.at[n, part], gone.at[step, n]))
+            copies[-1].start()
+        return copies
+
     blocks(0)
+    fetch.wait()
+    copies = send(0)
 
     for e in range(1, 5):
         rows, _, _, _, slopes, _ = les_element(um1, Shifted(ut1), mm, e, weights, coef, False)
         lamb_of(rows, slopes, lamb, e)
 
     blocks(1)
-    for n in range(sends.shape[0]):
-        index = jnp.maximum(sends[n], 0)
-        for k in range(6):
-            sent[n, k] = blk[index, k]
+    for copy in copies + send(1):
+        copy.wait()
 
 
 class Shifted:
@@ -477,28 +505,32 @@
                     down[48 + c * 8 + az] = narrow
 
 
-def pack_entries(entries, order, first, last):
-    for way, to in enumerate((first, last)):
+def pack_entries(entries, order, mask, even, odd):
+    right = mask[...] > 0.5
+    results = []
+    for way in range(2):
         tiles = []
         for n in range(len(entries) // 2):
             rows = [ref[at].astype(F32) for ref, at in entries[2 * n] + entries[2 * n + 1]]
             tiles.append(pack(rows, way == 1, CAA_WIDTH))
         x = jnp.concatenate(tiles, axis=0).astype(BF16)
         y = jnp.dot(x, order[way], preferred_element_type=F32)
-        for n in range(len(tiles)):
-            to[n] = y[8 * n : 8 * n + 8].astype(BF16)
-
-
-def state_pack_kernel(sector, below, above, both, order, first, last):
+        results.append([y[8 * n : 8 * n + 8] for n in range(len(tiles))])
+    for n, (first, last) in enumerate(zip(*results)):
+        even[n] = jnp.where(right, last, first).astype(BF16)
+        odd[n] = jnp.where(right, first, last).astype(BF16)
+
+
+def state_pack_kernel(sector, below, above, both, order, mask, even, odd):
     entries = []
     for f in range(7):
         for e in range(12):
             ref = (below, both, above)[e // 4]
             entries.append([(ref, f * sector + 4 * (e % 4) + i) for i in range(4)])
-    pack_entries(entries, order, first, last)
-
-
-def source_pack_kernel(sector, own, below, above, order, first, last):
+    pack_entries(entries, order, mask, even, odd)
+
+
+def source_pack_kernel(sector, own, below, above, order, mask, even, odd):
     entries = []
     for c in range(3):
         for e in range(12):
@@ -514,16 +546,18 @@
                 entries.append([(below, 48 + c * 8 + 4 * (e - 2) + i) for i in range(4)])
             else:
                 entries.append([(above, 48 + c * 8 + 4 * (e - 8) + i) for i in range(4)])
-    pack_entries(entries, order, first, last)
+    pack_entries(entries, order, mask, even, odd)
 
 
 CAA_RANGES = ((0, 12), (1, 11), (1, 11), (2, 10), (2, 10), (3, 9), (3, 9), (4, 8))
 
 
 def caa_kernel(
-    sector, w, m, own, below, above, caa_below, caa_above, state_left, state_right, from_left, from_right, weights, coef, upward,
+    sector, w, m, own, below, above, caa_below, caa_above, state_odd, state_even, odd, even, mask, weights, coef, upward,
     out, wm, wt, mm, mt, sm, st,
 ):
+    state_left, state_right = sides(mask, state_even, state_odd)
+    from_left, from_right = sides(mask, even, odd)
     for f in range(7):
         for az in range(3 * sector):
             if az < sector:
@@ -643,18 +677,27 @@
             pair(step % 2, step // 4, e, step == 7)
 
 
-def call(kernel, name, outs, *args, smem=0, far=0, scratch=()):
-    whole = pl.BlockSpec(memory_space=pltpu.VMEM)
-    specs = [pl.BlockSpec(memory_space=pltpu.SMEM)] * smem + [pl.BlockSpec(memory_space=pltpu.HBM)] * far
+def call(kernel, name, outs, *args, smem=0, far=0, far_outs=0, scratch=()):
+    whole, hbm = pl.BlockSpec(memory_space=pltpu.VMEM), pl.BlockSpec(memory_space=pltpu.HBM)
+    args = [pltpu.with_memory_space_constraint(x, pltpu.HBM) if smem <= n < smem + far else x for n, x in enumerate(args)]
+    specs = [pl.BlockSpec(memory_space=pltpu.SMEM)] * smem + [hbm] * far
     return pl.pallas_call(
         kernel,
         name=name,
         out_shape=[jax.ShapeDtypeStruct(shape, dtype) for shape, dtype in outs],
         in_specs=specs + [whole] * (len(args) - smem - far),
-        out_specs=[whole] * len(outs),
+        out_specs=[hbm] * far_outs + [whole] * (len(outs) - far_outs),
         scratch_shapes=list(scratch),
-        compiler_params=pltpu.CompilerParams(vmem_limit_bytes=None if far else VMEM_LIMIT),
+        compiler_params=pltpu.CompilerParams(vmem_limit_bytes=VMEM_LIMIT),
     )(*args)
+
+
+def swap_pairs(ours, theirs, axis):
+    count = lax.axis_size(axis)
+    edges = lambda start: [pair for a in range(start, count - 1, 2) for pair in ((a, a + 1), (a + 1, a))]
+    odd = lax.ppermute(theirs, axis, edges(1))
+    even = lax.ppermute(ours, axis, edges(0))
+    return even, odd
 
 
 def both_ways(low, high, axis, closed):
@@ -678,6 +721,7 @@
     own_row = lax.axis_index("sec") * slabs + lax.axis_index("gx")
     sends = lax.dynamic_slice_in_dim(send_list, own_row, 1, axis=0).reshape(-1)
     tile = (8, 128)
+    mask = jnp.broadcast_to(((own_row + 1) % 2).astype(F32), tile)
     vmem = lambda *shape, dtype=F32: pltpu.VMEM((*shape, *tile), dtype)
 
     low, high = call(
@@ -689,20 +733,24 @@
         scratch=[pltpu.VMEM(u.shape, F32), pltpu.VMEM(lm.shape, F32), pltpu.SemaphoreType.DMA((2,))],
     )
     before, after = both_ways(low, high, "az", True)
-    first, last = call(
+    even, odd = call(
         functools.partial(les_pack_kernel, sector),
         "les_pack",
         [((4, *tile), F32)] * 2,
-        u, lm, before, after,
+        u, lm, before, after, mask,
     )
-    from_left, from_right = both_ways(first, last, STREAM, False)
+    even, odd = swap_pairs(even, odd, STREAM)
     sent, um1, ut1 = call(
         functools.partial(les_kernel, sector),
         "les",
         [((slabs * 2, 6, *tile), BF16), ((3, 24, *tile), F32), ((3, 4, *tile), F32)],
-        sends, u, lm, before, after, from_left, from_right, les_weights, les_coef,
-        smem=1,
-        scratch=[vmem(3, 24), vmem(3, 6), vmem(3, 24), vmem(3, 6), vmem(3, 24), vmem(16, 6, dtype=BF16)],
+        sends, u, lm, before, after, odd, even, mask, les_weights, les_coef,
+        far=1,
+        far_outs=1,
+        scratch=[
+            vmem(3, 24), vmem(3, 6), vmem(3, 24), vmem(3, 6), vmem(3, 24), vmem(16, 6, dtype=BF16),
+            pltpu.SMEM(sends.shape, jnp.int32), pltpu.SemaphoreType.DMA, pltpu.SemaphoreType.DMA((2, *sends.shape)),
+        ],
     )
     got = lax.all_to_all(sent.reshape(slabs, 96, 128), "gx", 0, 0, tiled=True).reshape(slabs * 2, 6, *tile)
 
@@ -715,15 +763,15 @@
         lm, um1, ut1, les_weights, les_coef,
         scratch=[vmem(3, 24)],
     )
-    first, last = call(
+    even, odd = call(
         functools.partial(state_pack_kernel, sector),
         "state_pack",
         [((42, *tile), BF16)] * 2,
-        caa_below, caa_above, both, order,
+        caa_below, caa_above, both, order, mask,
     )
-    state_left, state_right = both_ways(first, last, STREAM, False)
+    state_even, state_odd = swap_pairs(even, odd, STREAM)
     table = jnp.concatenate([intersection_refs.reshape(-1), offsets])
-    got, table, state_left, state_right, les_out = lax.optimization_barrier((got, table, state_left, state_right, les_out))
+    got, table, state_odd, state_even, les_out = lax.optimization_barrier((got, table, state_odd, state_even, les_out))
 
     own, up, down = call(
         functools.partial(blend_kernel, sector),
@@ -734,18 +782,18 @@
         scratch=[vmem(6, 16)],
     )
     below, above = both_ways(down, up, "az", True)
-    first, last = call(
+    even, odd = call(
         functools.partial(source_pack_kernel, sector),
         "source_pack",
         [((30, *tile), BF16)] * 2,
-        own, below, above, order,
+        own, below, above, order, mask,
     )
-    from_left, from_right = both_ways(first, last, STREAM, False)
+    even, odd = swap_pairs(even, odd, STREAM)
     (caa_out,) = call(
         functools.partial(caa_kernel, sector),
         "caa",
         [((4, lines, length), F32)],
-        w, m, own, below, above, caa_below, caa_above, state_left, state_right, from_left, from_right, caa_weights, caa_coef, upward,
+        w, m, own, below, above, caa_below, caa_above, state_odd, state_even, odd, even, mask, caa_weights, caa_coef, upward,
         scratch=[vmem(2, 4, 48), vmem(2, 4, 12), vmem(3, 48), vmem(3, 12), vmem(2, 3, 48), vmem(2, 3, 12)],
     )
     return les_out.reshape(les_velocity.shape), caa_out.reshape(caa_state.shape)

time: 87.3 us -> 85.1 us (0.975)
  the two profiles are of different devices: /device:TPU:29 before, /device:TPU:27 now
where the time goes in v4:
time: 85.1 us; the launch traced here: 84.7 us
  starting transfers between devices  40.5 us (48%)
  waiting for transfers between devices  27.8 us (33%)
  Pallas kernels  14 us (16%)
  local copies, waits for them, and re-layouts  1.41 us (2%)
  between operations  0.86 us (1%)
    ppermute x3, starting transfers between devices, swap_pairs(): odd = lax.ppermute(theirs, axis, edges(1))  22.5 us
    pallas_call x9, Pallas kernels, call(): pl.pallas_call(kernel, name=name, out_shape=[jax.ShapeDtypeStruct(shape,...  14 us
    ppermute x3, waiting for transfers between devices, both_ways(): above = lax.ppermute(low, axis, [((i + 1) % count, i) for i in range(ends)])  11.2 us
    ppermute x3, starting transfers between devices, both_ways(): lax.ppermute(high, axis, [(i, (i + 1) % count) for i in range(ends)])  6.53 us
    ppermute x3, starting transfers between devices, swap_pairs(): even = lax.ppermute(ours, axis, edges(0))  6.39 us
    ppermute x3, waiting for transfers between devices, both_ways(): lax.ppermute(high, axis, [(i, (i + 1) % count) for i in range(ends)])  6.18 us
    ppermute x3, waiting for transfers between devices, swap_pairs(): odd = lax.ppermute(theirs, axis, edges(1))  5.59 us
    all_to_all x1, starting transfers between devices, body(): lax.all_to_all(sent.reshape(slabs, 96, 128), 'gx', 0, 0, tiled=True)  5.07 us
  transfers between devices with their start and end apart: 13, of which 11 were waited for; matrix products, arithmetic and copies ran while one was open for 2% of the time, Pallas kernels for 3%

profile of v4, /device:TPU:27, one launch (start us, length us, event | category | flops | bytes accessed | tf_op | source)
XLA Modules:
  0.0 84.7 jit_solution(15808648919442752534)
XLA Ops:
  0.6 0.0 copy-start
  0.6 0.0 copy-start.1
  0.7 0.0 copy-start.2
  0.7 1.1 %first.1 = (f32[15,8,128]{2,1,0:T(8,128)S(1)}, f32[15,8,128]{2,1,0:T(8,128)S(1)}) custom-call(f32[3,128,128]{2,1,0:T(8,128)} %bitcast.13, f32[3,128,128]{2,1,0:T(8,128)} %bitcast.8), custom_call_target="tpu_custom_call" | custom-call | tf_op jit(solution)/shard_map/first/pallas_call | solution.py:684
  1.8 3.1 %collective-permute-start = (f32[15,8,128]{2,1,0:T(8,128)S(1)}, f32[15,8,128]{2,1,0:T(8,128)S(1)}, u32[]{:S(2)}, u32[]{:S(2)}) collective-permute-start(f32[15,8,128]{2,1,0:T(8,128)S(1)} %get-tuple-element.21), channel_id=1, source_target_pairs={{0,1},{1,2},{2,3},{3,4},{4,5},{5,6},{6,7},{7,8},{8,9},{9,10},{10,1... | collective-permute-start | bytes 184328 | tf_op jit(solution)/shard_map/ppermute | solution.py:706
  4.9 0.0 collective-permute-start.1
  4.9 1.3 %collective-permute-done.before = f32[15,8,128]{2,1,0:T(8,128)S(1)} collective-permute-done((f32[15,8,128]{2,1,0:T(8,128)S(1)}, f32[15,8,128]{2,1,0:T(8,128)S(1)}, u32[]{:S(2)}, u32[]{:S(2)}) %collective-permute-start) | collective-permute-done | bytes 61472 | tf_op jit(solution)/shard_map/ppermute | solution.py:706
  6.2 3.6 %collective-permute-done.1.after = f32[15,8,128]{2,1,0:T(8,128)S(1)} collective-permute-done((f32[15,8,128]{2,1,0:T(8,128)S(1)}, f32[15,8,128]{2,1,0:T(8,128)S(1)}, u32[]{:S(2)}, u32[]{:S(2)}) %collective-permute-start.1) | collective-permute-done | bytes 61472 | tf_op jit(solution)/shard_map/ppermute | solution.py:707
  9.7 0.0 copy-done.1
  9.7 0.0 copy-done.2
  9.7 0.0 copy-start.4
  9.8 0.0 copy-start.7
  9.8 0.3 les_pack.1
  10.1 14.3 %collective-permute-start.2 = (f32[4,8,128]{2,1,0:T(8,128)S(1)}, f32[4,8,128]{2,1,0:T(8,128)S(1)}, u32[]{:S(2)}, u32[]{:S(2)}) collective-permute-start(f32[4,8,128]{2,1,0:T(8,128)S(1)} %get-tuple-element.23), channel_id=1, source_target_pairs={{16,32},{32,16},{48,64},{64,48},{80,96},{96,80},{112,128},{128,112... | collective-permute-start | bytes 49160 | tf_op jit(solution)/shard_map/ppermute | solution.py:698
  24.4 1.9 %collective-permute-start.3 = (f32[4,8,128]{2,1,0:T(8,128)S(1)}, f32[4,8,128]{2,1,0:T(8,128)S(1)}, u32[]{:S(2)}, u32[]{:S(2)}) collective-permute-start(f32[4,8,128]{2,1,0:T(8,128)S(1)} %get-tuple-element.24), channel_id=1, source_target_pairs={{0,16},{16,0},{32,48},{48,32},{64,80},{80,64},{96,112},{112,96},{1... | collective-permute-start | bytes 49160 | tf_op jit(solution)/shard_map/ppermute | solution.py:699
  26.3 0.0 copy-done
  26.3 0.6 dynamic-slice_reduce_fusion
  26.9 0.6 reshape.34.sends_far
  27.5 0.0 collective-permute-done.2.odd
  27.5 1.4 %collective-permute-done.3.even = f32[4,8,128]{2,1,0:T(8,128)S(1)} collective-permute-done((f32[4,8,128]{2,1,0:T(8,128)S(1)}, f32[4,8,128]{2,1,0:T(8,128)S(1)}, u32[]{:S(2)}, u32[]{:S(2)}) %collective-permute-start.3) | collective-permute-done | bytes 16416 | tf_op jit(solution)/shard_map/ppermute | solution.py:699
  28.9 0.0 copy-done.4
  28.9 0.0 copy-done.7
  28.9 3.8 %les.1 = (bf16[48,6,8,128]{3,2,1,0:T(8,128)(2,1)}, f32[3,24,8,128]{3,2,1,0:T(8,128)S(1)}, f32[3,4,8,128]{3,2,1,0:T(8,128)S(1)}) custom-call(s32[48]{0:T(128)} %reshape.34.sends_far, f32[3,128,128]{2,1,0:T(8,128)S(1)} %bitcast.15, f32[3,128,128]{2,1,0:T(8,128)S(1)} %bitcast.10, f32[15,8,128]{2,1,0:T(8,128)S(1)} %collective-permute-done.before, ...), custom_call_target="tpu_custom_call" | custom-call | tf_op jit(solution)/shard_map/les/pallas_call | solution.py:684
  32.6 0.0 copy-start.3
  32.7 0.0 copy-start.5
  32.7 5.1 %all-to-all-start = ((bf16[24,96,128]{2,1,0:T(8,128)(2,1)}), bf16[24,96,128]{2,1,0:T(8,128)(2,1)S(1)}, u32[]{:S(2)}, u32[]{:S(2)}) async-start(bf16[24,96,128]{2,1,0:T(8,128)(2,1)} %bitcast.2), calls=%async_computation | async-start | bytes 1179648 | tf_op jit(solution)/shard_map/all_to_all | solution.py:755
  37.7 0.0 copy-done.3
  37.7 0.0 copy-done.5
  37.8 0.0 copy-start.11
  37.8 0.0 copy-start.6
  37.8 0.2 narrow.1.both
  37.9 2.0 %collective-permute-start.4 = (bf16[112,8,128]{2,1,0:T(8,128)(2,1)S(1)}, bf16[112,8,128]{2,1,0:T(8,128)(2,1)S(1)}, u32[]{:S(2)}, u32[]{:S(2)}) collective-permute-start(bf16[112,8,128]{2,1,0:T(8,128)(2,1)S(1)} %narrow.1.both), channel_id=1, source_target_pairs={{0,1},{1,2},{2,3},{3,4},{4,5},{5,6},{6,7},{7,8},{8,9},{9,10},{10,1... | collective-permute-start | bytes 688136 | tf_op jit(solution)/shard_map/ppermute | solution.py:706
  40.0 0.0 collective-permute-start.5
  40.0 0.0 copy-done.11
  40.0 0.1 copy.16
  40.0 0.1 reshape.39
  40.1 2.8 %collective-permute-done.4.below.caa_below = bf16[112,8,128]{2,1,0:T(8,128)(2,1)S(1)} collective-permute-done((bf16[112,8,128]{2,1,0:T(8,128)(2,1)S(1)}, bf16[112,8,128]{2,1,0:T(8,128)(2,1)S(1)}, u32[]{:S(2)}, u32[]{:S(2)}) %collective-permute-start.4) | collective-permute-done | bytes 229408 | tf_op jit(solution)/shard_map/ppermute | solution.py:706
  42.9 4.0 %collective-permute-done.5.above.caa_above = bf16[112,8,128]{2,1,0:T(8,128)(2,1)S(1)} collective-permute-done((bf16[112,8,128]{2,1,0:T(8,128)(2,1)S(1)}, bf16[112,8,128]{2,1,0:T(8,128)(2,1)S(1)}, u32[]{:S(2)}, u32[]{:S(2)}) %collective-permute-start.5) | collective-permute-done | bytes 229408 | tf_op jit(solution)/shard_map/ppermute | solution.py:707
  46.9 0.0 copy-done.6
  46.9 0.5 state_pack.1
  47.4 0.0 copy-start.12
  47.4 4.4 %collective-permute-start.6 = (bf16[42,8,128]{2,1,0:T(8,128)(2,1)S(1)}, bf16[42,8,128]{2,1,0:T(8,128)(2,1)S(1)}, u32[]{:S(2)}, u32[]{:S(2)}) collective-permute-start(bf16[42,8,128]{2,1,0:T(8,128)(2,1)S(1)} %get-tuple-element.26), channel_id=1, source_target_pairs={{16,32},{32,16},{48,64},{64,48},{80,96},{96,80},{112,128},{128,112... | collective-permute-start | bytes 258056 | tf_op jit(solution)/shard_map/ppermute | solution.py:698
  51.9 1.9 %collective-permute-start.7 = (bf16[42,8,128]{2,1,0:T(8,128)(2,1)S(1)}, bf16[42,8,128]{2,1,0:T(8,128)(2,1)S(1)}, u32[]{:S(2)}, u32[]{:S(2)}) collective-permute-start(bf16[42,8,128]{2,1,0:T(8,128)(2,1)S(1)} %get-tuple-element.27), channel_id=1, source_target_pairs={{0,16},{16,0},{32,48},{48,32},{64,80},{80,64},{96,112},{112,96},{1... | collective-permute-start | bytes 258056 | tf_op jit(solution)/shard_map/ppermute | solution.py:699
  53.8 0.0 copy-done.12
  53.8 0.1 pad_add_fusion.refs
  53.9 1.6 %les_out.1 = f32[3,128,128]{2,1,0:T(8,128)} custom-call(f32[3,128,128]{2,1,0:T(8,128)S(1)} %bitcast.11, f32[3,24,8,128]{3,2,1,0:T(8,128)S(1)} %get-tuple-element.28.um1, f32[3,4,8,128]{3,2,1,0:T(8,128)S(1)} %get-tuple-element.29.ut1, bf16[2,256,256]{2,1,0:T(8,128)(2,1)S(1)} %copy-done.4, f32[16,8,128]{2,1,0:T(8,128)S(1)} %copy-done.7), custom_call_target="tpu_custom_call" | custom-call | tf_op jit(solution)/shard_map/les_out/pallas_call | solution.py:684
  55.5 4.9 %collective-permute-done.6.state_odd = bf16[42,8,128]{2,1,0:T(8,128)(2,1)S(1)} collective-permute-done((bf16[42,8,128]{2,1,0:T(8,128)(2,1)S(1)}, bf16[42,8,128]{2,1,0:T(8,128)(2,1)S(1)}, u32[]{:S(2)}, u32[]{:S(2)}) %collective-permute-start.6) | collective-permute-done | bytes 86048 | tf_op jit(solution)/shard_map/ppermute | solution.py:698
  60.4 0.0 collective-permute-done.7.state_even
  60.4 1.7 %all-to-all-done = bf16[24,96,128]{2,1,0:T(8,128)(2,1)S(1)} async-done(((bf16[24,96,128]{2,1,0:T(8,128)(2,1)}), bf16[24,96,128]{2,1,0:T(8,128)(2,1)S(1)}, u32[]{:S(2)}, u32[]{:S(2)}) %all-to-all-start) | async-done | bytes 589856 | tf_op jit(solution)/shard_map/all_to_all | solution.py:755
  62.1 1.4 %blend.1 = (f32[2,3,16,8,128]{4,3,2,1,0:T(8,128)S(1)}, bf16[72,8,128]{2,1,0:T(8,128)(2,1)S(1)}, bf16[72,8,128]{2,1,0:T(8,128)(2,1)S(1)}) custom-call(s32[80]{0:T(128)S(1)} %pad_add_fusion.refs, bf16[48,6,8,128]{3,2,1,0:T(8,128)(2,1)S(1)} %bitcast.12), custom_call_target="tpu_custom_call" | custom-call | tf_op jit(solution)/shard_map/blend/pallas_call | solution.py:684
  63.5 1.4 %collective-permute-start.8 = (bf16[72,8,128]{2,1,0:T(8,128)(2,1)S(1)}, bf16[72,8,128]{2,1,0:T(8,128)(2,1)S(1)}, u32[]{:S(2)}, u32[]{:S(2)}) collective-permute-start(bf16[72,8,128]{2,1,0:T(8,128)(2,1)S(1)} %get-tuple-element.34), channel_id=1, source_target_pairs={{0,1},{1,2},{2,3},{3,4},{4,5},{5,6},{6,7},{7,8},{8,9},{9,10},{10,1... | collective-permute-start | bytes 442376 | tf_op jit(solution)/shard_map/ppermute | solution.py:706
  64.9 0.0 collective-permute-start.9
  64.9 2.1 %collective-permute-done.8.below = bf16[72,8,128]{2,1,0:T(8,128)(2,1)S(1)} collective-permute-done((bf16[72,8,128]{2,1,0:T(8,128)(2,1)S(1)}, bf16[72,8,128]{2,1,0:T(8,128)(2,1)S(1)}, u32[]{:S(2)}, u32[]{:S(2)}) %collective-permute-start.8) | collective-permute-done | bytes 147488 | tf_op jit(solution)/shard_map/ppermute | solution.py:706
  67.0 3.7 %collective-permute-done.9.above = bf16[72,8,128]{2,1,0:T(8,128)(2,1)S(1)} collective-permute-done((bf16[72,8,128]{2,1,0:T(8,128)(2,1)S(1)}, bf16[72,8,128]{2,1,0:T(8,128)(2,1)S(1)}, u32[]{:S(2)}, u32[]{:S(2)}) %collective-permute-start.9) | collective-permute-done | bytes 147488 | tf_op jit(solution)/shard_map/ppermute | solution.py:707
  70.7 0.0 copy-start.8
  70.7 0.4 source_pack.1
  71.1 3.8 %collective-permute-start.10 = (bf16[30,8,128]{2,1,0:T(8,128)(2,1)S(1)}, bf16[30,8,128]{2,1,0:T(8,128)(2,1)S(1)}, u32[]{:S(2)}, u32[]{:S(2)}) collective-permute-start(bf16[30,8,128]{2,1,0:T(8,128)(2,1)S(1)} %get-tuple-element.38), channel_id=1, source_target_pairs={{16,32},{32,16},{48,64},{64,48},{80,96},{96,80},{112,128},{128,112... | collective-permute-start | bytes 184328 | tf_op jit(solution)/shard_map/ppermute | solution.py:698
  75.0 2.6 %collective-permute-start.11 = (bf16[30,8,128]{2,1,0:T(8,128)(2,1)S(1)}, bf16[30,8,128]{2,1,0:T(8,128)(2,1)S(1)}, u32[]{:S(2)}, u32[]{:S(2)}) collective-permute-start(bf16[30,8,128]{2,1,0:T(8,128)(2,1)S(1)} %get-tuple-element.39), channel_id=1, source_target_pairs={{0,16},{16,0},{32,48},{48,32},{64,80},{80,64},{96,112},{112,96},{1... | collective-permute-start | bytes 184328 | tf_op jit(solution)/shard_map/ppermute | solution.py:699
  77.5 0.7 collective-permute-done.10.odd
  78.2 1.7 %collective-permute-done.11.even = bf16[30,8,128]{2,1,0:T(8,128)(2,1)S(1)} collective-permute-done((bf16[30,8,128]{2,1,0:T(8,128)(2,1)S(1)}, bf16[30,8,128]{2,1,0:T(8,128)(2,1)S(1)}, u32[]{:S(2)}, u32[]{:S(2)}) %collective-permute-start.11) | collective-permute-done | bytes 61472 | tf_op jit(solution)/shard_map/ppermute | solution.py:699
  79.9 0.0 copy-done.8
  79.9 0.0 copy-done.9
  79.9 0.0 copy-done.10
  79.9 4.7 %caa.1 = f32[4,128,128]{2,1,0:T(8,128)} custom-call(f32[4,128,128]{2,1,0:T(8,128)S(1)} %bitcast.17, f32[3,128,128]{2,1,0:T(8,128)S(1)} %bitcast.19, f32[2,3,16,8,128]{4,3,2,1,0:T(8,128)S(1)} %get-tuple-element.33.own, bf16[72,8,128]{2,1,0:T(8,128)(2,1)S(1)} %collective-permute-done.8.below, bf16[72,8,128]{2,1,0:T(8,128)(2,1)S(1)} %collective-permute-done.9.above, ...), custom_call_target="tpu_custom_call" | custom-call | tf_op jit(solution)/shard_map/caa/pallas_call | solution.py:684
  (3 shorter events, 0.0 us)
Async XLA Ops:
  0.6 25.7 %copy-start = (s32[48,24,2]{0,2,1:T(2,128)S(1)}, s32[48,24,2]{0,2,1:T(2,128)}, u32[]{:S(2)}) copy-start(s32[48,24,2]{0,2,1:T(2,128)} %param.19) | copy-start | bytes 27652
  0.6 9.1 %copy-start.1 = (f32[3,8,16,128]{3,2,1,0:T(8,128)S(1)}, f32[3,8,16,128]{3,2,1,0:T(8,128)}, u32[]{:S(2)}) copy-start(f32[3,8,16,128]{3,2,1,0:T(8,128)} %param.14) | copy-start | bytes 589828
  0.7 9.1 %copy-start.2 = (f32[3,8,16,128]{3,2,1,0:T(8,128)S(1)}, f32[3,8,16,128]{3,2,1,0:T(8,128)}, u32[]{:S(2)}) copy-start(f32[3,8,16,128]{3,2,1,0:T(8,128)} %param.13) | copy-start | bytes 589828
  1.8 4.4 %collective-permute-start = (f32[15,8,128]{2,1,0:T(8,128)S(1)}, f32[15,8,128]{2,1,0:T(8,128)S(1)}, u32[]{:S(2)}, u32[]{:S(2)}) collective-permute-start(f32[15,8,128]{2,1,0:T(8,128)S(1)} %get-tuple-element.21), channel_id=1, source_target_pairs={{0,1},{1,2},{2,3},{3,4},{4,5},{5,6},{6,7},{7,8},{8,9},{9,10},{10,1... | collective-permute-start | bytes 184328 | tf_op jit(solution)/shard_map/ppermute | solution.py:706
  4.9 4.9 %collective-permute-start.1 = (f32[15,8,128]{2,1,0:T(8,128)S(1)}, f32[15,8,128]{2,1,0:T(8,128)S(1)}, u32[]{:S(2)}, u32[]{:S(2)}) collective-permute-start(f32[15,8,128]{2,1,0:T(8,128)S(1)} %get-tuple-element.22), channel_id=1, source_target_pairs={{1,0},{2,1},{3,2},{4,3},{5,4},{6,5},{7,6},{8,7},{9,8},{10,9},{11,1... | collective-permute-start | bytes 184328 | tf_op jit(solution)/shard_map/ppermute | solution.py:707
  9.7 19.1 %copy-start.4 = (bf16[2,256,256]{2,1,0:T(8,128)(2,1)S(1)}, bf16[2,256,256]{2,1,0:T(8,128)(2,1)}, u32[]{:S(2)}) copy-start(bf16[2,256,256]{2,1,0:T(8,128)(2,1)} %constant.41.clone.weights) | copy-start | bytes 786436
  9.8 19.1 %copy-start.7 = (f32[16,8,128]{2,1,0:T(8,128)S(1)}, f32[16,8,128]{2,1,0:T(8,128)}, u32[]{:S(2)}) copy-start(f32[16,8,128]{2,1,0:T(8,128)} %constant.42.clone.coef) | copy-start | bytes 196612
  10.1 17.4 %collective-permute-start.2 = (f32[4,8,128]{2,1,0:T(8,128)S(1)}, f32[4,8,128]{2,1,0:T(8,128)S(1)}, u32[]{:S(2)}, u32[]{:S(2)}) collective-permute-start(f32[4,8,128]{2,1,0:T(8,128)S(1)} %get-tuple-element.23), channel_id=1, source_target_pairs={{16,32},{32,16},{48,64},{64,48},{80,96},{96,80},{112,128},{128,112... | collective-permute-start | bytes 49160 | tf_op jit(solution)/shard_map/ppermute | solution.py:698
  24.4 4.5 %collective-permute-start.3 = (f32[4,8,128]{2,1,0:T(8,128)S(1)}, f32[4,8,128]{2,1,0:T(8,128)S(1)}, u32[]{:S(2)}, u32[]{:S(2)}) collective-permute-start(f32[4,8,128]{2,1,0:T(8,128)S(1)} %get-tuple-element.24), channel_id=1, source_target_pairs={{0,16},{16,0},{32,48},{48,32},{64,80},{80,64},{96,112},{112,96},{1... | collective-permute-start | bytes 49160 | tf_op jit(solution)/shard_map/ppermute | solution.py:699
  32.6 5.1 %copy-start.3 = (f32[4,8,16,128]{3,2,1,0:T(8,128)S(1)}, f32[4,8,16,128]{3,2,1,0:T(8,128)}, u32[]{:S(2)}) copy-start(f32[4,8,16,128]{3,2,1,0:T(8,128)} %param.15) | copy-start | bytes 786436
  32.7 5.1 %copy-start.5 = (f32[3,8,16,128]{3,2,1,0:T(8,128)S(1)}, f32[3,8,16,128]{3,2,1,0:T(8,128)}, u32[]{:S(2)}) copy-start(f32[3,8,16,128]{3,2,1,0:T(8,128)} %param.16) | copy-start | bytes 589828
  32.7 29.4 %all-to-all-start = ((bf16[24,96,128]{2,1,0:T(8,128)(2,1)}), bf16[24,96,128]{2,1,0:T(8,128)(2,1)S(1)}, u32[]{:S(2)}, u32[]{:S(2)}) async-start(bf16[24,96,128]{2,1,0:T(8,128)(2,1)} %bitcast.2), calls=%async_computation | async-start | bytes 1179648 | tf_op jit(solution)/shard_map/all_to_all | solution.py:755
  37.8 2.2 %copy-start.11 = (s32[16,4]{0,1:T(4,128)S(1)}, s32[16,4]{0,1:T(4,128)}, u32[]{:S(2)}) copy-start(s32[16,4]{0,1:T(4,128)} %param.17) | copy-start | bytes 772
  37.8 9.1 %copy-start.6 = (bf16[2,128,128]{2,1,0:T(8,128)(2,1)S(1)}, bf16[2,128,128]{2,1,0:T(8,128)(2,1)}, u32[]{:S(2)}) copy-start(bf16[2,128,128]{2,1,0:T(8,128)(2,1)} %constant.46.clone.order) | copy-start | bytes 196612
  37.9 5.0 %collective-permute-start.4 = (bf16[112,8,128]{2,1,0:T(8,128)(2,1)S(1)}, bf16[112,8,128]{2,1,0:T(8,128)(2,1)S(1)}, u32[]{:S(2)}, u32[]{:S(2)}) collective-permute-start(bf16[112,8,128]{2,1,0:T(8,128)(2,1)S(1)} %narrow.1.both), channel_id=1, source_target_pairs={{0,1},{1,2},{2,3},{3,4},{4,5},{5,6},{6,7},{7,8},{8,9},{9,10},{10,1... | collective-permute-start | bytes 688136 | tf_op jit(solution)/shard_map/ppermute | solution.py:706
  40.0 7.0 %collective-permute-start.5 = (bf16[112,8,128]{2,1,0:T(8,128)(2,1)S(1)}, bf16[112,8,128]{2,1,0:T(8,128)(2,1)S(1)}, u32[]{:S(2)}, u32[]{:S(2)}) collective-permute-start(bf16[112,8,128]{2,1,0:T(8,128)(2,1)S(1)} %narrow.1.both), channel_id=1, source_target_pairs={{1,0},{2,1},{3,2},{4,3},{5,4},{6,5},{7,6},{8,7},{9,8},{10,9},{11,1... | collective-permute-start | bytes 688136 | tf_op jit(solution)/shard_map/ppermute | solution.py:707
  47.4 6.4 %copy-start.12 = (s32[16]{0:T(128)S(1)}, s32[16]{0:T(128)}, u32[]{:S(2)}) copy-start(s32[16]{0:T(128)} %param.18) | copy-start | bytes 196
  47.4 12.9 %collective-permute-start.6 = (bf16[42,8,128]{2,1,0:T(8,128)(2,1)S(1)}, bf16[42,8,128]{2,1,0:T(8,128)(2,1)S(1)}, u32[]{:S(2)}, u32[]{:S(2)}) collective-permute-start(bf16[42,8,128]{2,1,0:T(8,128)(2,1)S(1)} %get-tuple-element.26), channel_id=1, source_target_pairs={{16,32},{32,16},{48,64},{64,48},{80,96},{96,80},{112,128},{128,112... | collective-permute-start | bytes 258056 | tf_op jit(solution)/shard_map/ppermute | solution.py:698
  51.9 8.5 %collective-permute-start.7 = (bf16[42,8,128]{2,1,0:T(8,128)(2,1)S(1)}, bf16[42,8,128]{2,1,0:T(8,128)(2,1)S(1)}, u32[]{:S(2)}, u32[]{:S(2)}) collective-permute-start(bf16[42,8,128]{2,1,0:T(8,128)(2,1)S(1)} %get-tuple-element.27), channel_id=1, source_target_pairs={{0,16},{16,0},{32,48},{48,32},{64,80},{80,64},{96,112},{112,96},{1... | collective-permute-start | bytes 258056 | tf_op jit(solution)/shard_map/ppermute | solution.py:699
  63.5 3.5 %collective-permute-start.8 = (bf16[72,8,128]{2,1,0:T(8,128)(2,1)S(1)}, bf16[72,8,128]{2,1,0:T(8,128)(2,1)S(1)}, u32[]{:S(2)}, u32[]{:S(2)}) collective-permute-start(bf16[72,8,128]{2,1,0:T(8,128)(2,1)S(1)} %get-tuple-element.34), channel_id=1, source_target_pairs={{0,1},{1,2},{2,3},{3,4},{4,5},{5,6},{6,7},{7,8},{8,9},{9,10},{10,1... | collective-permute-start | bytes 442376 | tf_op jit(solution)/shard_map/ppermute | solution.py:706
  64.9 5.8 %collective-permute-start.9 = (bf16[72,8,128]{2,1,0:T(8,128)(2,1)S(1)}, bf16[72,8,128]{2,1,0:T(8,128)(2,1)S(1)}, u32[]{:S(2)}, u32[]{:S(2)}) collective-permute-start(bf16[72,8,128]{2,1,0:T(8,128)(2,1)S(1)} %get-tuple-element.35), channel_id=1, source_target_pairs={{1,0},{2,1},{3,2},{4,3},{5,4},{6,5},{7,6},{8,7},{9,8},{10,9},{11,1... | collective-permute-start | bytes 442376 | tf_op jit(solution)/shard_map/ppermute | solution.py:707
  70.7 9.2 %copy-start.8 = (bf16[2,128,256]{2,1,0:T(8,128)(2,1)S(1)}, bf16[2,128,256]{2,1,0:T(8,128)(2,1)}, u32[]{:S(2)}) copy-start(bf16[2,128,256]{2,1,0:T(8,128)(2,1)} %constant.43.clone.weights) | copy-start | bytes 393220
  70.7 9.2 %copy-start.9 = (f32[10,8,128]{2,1,0:T(8,128)S(1)}, f32[10,8,128]{2,1,0:T(8,128)}, u32[]{:S(2)}) copy-start(f32[10,8,128]{2,1,0:T(8,128)} %constant.44.clone.coef) | copy-start | bytes 122884
  70.7 9.2 %copy-start.10 = (bf16[160,80]{1,0:T(8,128)(2,1)S(1)}, bf16[160,80]{1,0:T(8,128)(2,1)}, u32[]{:S(2)}) copy-start(bf16[160,80]{1,0:T(8,128)(2,1)} %constant.45.clone.upward) | copy-start | bytes 76804
  71.1 7.1 %collective-permute-start.10 = (bf16[30,8,128]{2,1,0:T(8,128)(2,1)S(1)}, bf16[30,8,128]{2,1,0:T(8,128)(2,1)S(1)}, u32[]{:S(2)}, u32[]{:S(2)}) collective-permute-start(bf16[30,8,128]{2,1,0:T(8,128)(2,1)S(1)} %get-tuple-element.38), channel_id=1, source_target_pairs={{16,32},{32,16},{48,64},{64,48},{80,96},{96,80},{112,128},{128,112... | collective-permute-start | bytes 184328 | tf_op jit(solution)/shard_map/ppermute | solution.py:698
  75.0 5.0 %collective-permute-start.11 = (bf16[30,8,128]{2,1,0:T(8,128)(2,1)S(1)}, bf16[30,8,128]{2,1,0:T(8,128)(2,1)S(1)}, u32[]{:S(2)}, u32[]{:S(2)}) collective-permute-start(bf16[30,8,128]{2,1,0:T(8,128)(2,1)S(1)} %get-tuple-element.39), channel_id=1, source_target_pairs={{0,16},{16,0},{32,48},{48,32},{64,80},{80,64},{96,112},{112,96},{1... | collective-permute-start | bytes 184328 | tf_op jit(solution)/shard_map/ppermute | solution.py:699

commit v5 on v4

--- a/solution.py
+++ b/solution.py
@@ -282,18 +282,18 @@
     return ref[c, pl.ds(az, 8, stride=sector), :]
 
 
-def first_kernel(sector, u_far, lm_far, low, high, u, lm, arrived):
+def first_kernel(sector, u_far, lm_far, mask, even, odd, u, lm, arrived):
+    upper = mask[...] > 0.5
     copies = [pltpu.make_async_copy(a, b, arrived.at[n]) for n, (a, b) in enumerate([(u_far, u), (lm_far, lm)])]
     for copy in copies:
         copy.start()
     for copy in copies:
         copy.wait()
     for c in range(3):
-        for i in range(4):
-            low[4 * c + i] = column(u, c, i, sector)
-            high[4 * c + i] = column(u, c, sector - 4 + i, sector)
-        low[12 + c] = column(lm, c, 0, sector)
-        high[12 + c] = column(lm, c, sector - 1, sector)
+        for n, low, high in [(4 * c + i, (u, i), (u, sector - 4 + i)) for i in range(4)] + [(12 + c, (lm, 0), (lm, sector - 1))]:
+            low, high = column(low[0], c, low[1], sector), column(high[0], c, high[1], sector)
+            even[n] = jnp.where(upper, high, low)
+            odd[n] = jnp.where(upper, low, high)
 
 
 def narrow_kernel(sector, w, m, both):
@@ -303,7 +303,8 @@
             both[f * sector + az] = value.astype(BF16)
 
 
-def les_pack_kernel(sector, u, lm, before, after, mask, even, odd):
+def les_pack_kernel(sector, u, lm, near_odd, near_even, mask_az, mask, even, odd):
+    before, after = sides(mask_az, near_even, near_odd)
     right = mask[...] > 0.5
     entries = []
     for c in range(3):
@@ -367,10 +368,11 @@
 
 
 def les_kernel(
-    sector, sends_far, u, lm, before, after, odd, even, mask, weights, coef, sent, um1, ut1, um, ut, mm, mt, lamb, blk, sends, arrived, gone,
+    sector, sends_far, u, lm, near_odd, near_even, odd, even, mask_az, mask, weights, coef, sent, um1, ut1, um, ut, mm, mt, lamb, blk, sends, arrived,
 ):
     fetch = pltpu.make_async_copy(sends_far, sends, arrived)
     fetch.start()
+    before, after = sides(mask_az, near_even, near_odd)
     from_left, from_right = sides(mask, even, odd)
     for c in range(3):
         for i in range(4):
@@ -439,26 +441,18 @@
             for j in range(16):
                 blk[j, 3 * step + c] = tiles[j].astype(BF16)
 
-    def send(step):
-        part = pl.ds(3 * step, 3)
-        copies = []
-        for n in range(sends.shape[0]):
-            index = jnp.clip(sends[n], 0, 15)
-            copies.append(pltpu.make_async_copy(blk.at[index, part], sent.at[n, part], gone.at[step, n]))
-            copies[-1].start()
-        return copies
-
     blocks(0)
     fetch.wait()
-    copies = send(0)
 
     for e in range(1, 5):
         rows, _, _, _, slopes, _ = les_element(um1, Shifted(ut1), mm, e, weights, coef, False)
         lamb_of(rows, slopes, lamb, e)
 
     blocks(1)
-    for copy in copies + send(1):
-        copy.wait()
+    for n in range(sends.shape[0]):
+        index = jnp.clip(sends[n], 0, 15)
+        for k in range(6):
+            sent[n, k] = blk[index, k]
 
 
 class Shifted:
@@ -482,7 +476,7 @@
                 out[c, pl.ds(4 * (e - 1) + i, 8, stride=sector), :] = rows[c][i] - les_change(rows, slopes, fluxes, c, i)
 
 
-def blend_kernel(sector, refs, got, own, up, down, mixed):
+def blend_kernel(sector, refs, got, mask_az, own, even, odd, mixed):
     for j in range(16):
         a = jnp.clip(refs[4 * j] * 2 + refs[4 * j + 1], 0, got.shape[0] - 1)
         b = jnp.clip(refs[4 * j + 2] * 2 + refs[4 * j + 3], 0, got.shape[0] - 1)
@@ -490,19 +484,32 @@
         for k in range(6):
             blend = (8.0 - fraction) * got[a, k].astype(F32) + fraction * got[b, k].astype(F32)
             mixed[k, j] = blend * 0.125
+    upper = mask_az[...] > 0.5
     for step in range(2):
         for c in range(3):
             tiles = turn([mixed[3 * step + c, j] for j in range(16)])
             for az in range(sector):
                 own[step, c, az] = tiles[az]
-                narrow = tiles[az].astype(BF16)
-                if step == 0:
-                    up[c * 16 + az] = narrow
-                    down[c * 16 + az] = narrow
-                elif az >= 8:
-                    up[48 + c * 8 + az - 8] = narrow
-                else:
-                    down[48 + c * 8 + az] = narrow
+            depth = DEPTHS[step]
+            for n in range(depth):
+                down, up = tiles[n], tiles[sector - depth + n]
+                at = first_of(step, c) + n
+                even[at] = jnp.where(upper, up, down).astype(BF16)
+                odd[at] = jnp.where(upper, down, up).astype(BF16)
+
+
+DEPTHS = (13, 5)
+
+
+def first_of(step, c):
+    return DEPTHS[step] * c + (3 * DEPTHS[0] if step else 0)
+
+
+def source_row(below, above, step, c, az):
+    depth = DEPTHS[step]
+    if az < 0:
+        return below, first_of(step, c) + max(az + depth, 0)
+    return above, first_of(step, c) + min(az - 16, depth - 1)
 
 
 def pack_entries(entries, order, mask, even, odd):
@@ -530,22 +537,16 @@
     pack_entries(entries, order, mask, even, odd)
 
 
-def source_pack_kernel(sector, own, below, above, order, mask, even, odd):
+def source_pack_kernel(sector, own, near_odd, near_even, order, mask_az, mask, even, odd):
+    below, above = sides(mask_az, near_even, near_odd)
     entries = []
-    for c in range(3):
-        for e in range(12):
-            if 4 <= e < 8:
-                entries.append([(own, (0, c, 4 * (e - 4) + i)) for i in range(4)])
-            else:
-                entries.append([(below if e < 4 else above, c * 16 + 4 * (e % 4) + i) for i in range(4)])
-    for c in range(3):
-        for e in range(2, 10):
-            if 4 <= e < 8:
-                entries.append([(own, (1, c, 4 * (e - 4) + i)) for i in range(4)])
-            elif e < 4:
-                entries.append([(below, 48 + c * 8 + 4 * (e - 2) + i) for i in range(4)])
-            else:
-                entries.append([(above, 48 + c * 8 + 4 * (e - 8) + i) for i in range(4)])
+    for step, (start, stop) in enumerate(((0, 12), (2, 10))):
+        for c in range(3):
+            for e in range(start, stop):
+                if 4 <= e < 8:
+                    entries.append([(own, (step, c, 4 * (e - 4) + i)) for i in range(4)])
+                else:
+                    entries.append([source_row(below, above, step, c, 4 * (e - 4) + i) for i in range(4)])
     pack_entries(entries, order, mask, even, odd)
 
 
@@ -553,9 +554,10 @@
 
 
 def caa_kernel(
-    sector, w, m, own, below, above, caa_below, caa_above, state_odd, state_even, odd, even, mask, weights, coef, upward,
+    sector, w, m, own, near_odd, near_even, mask_az, caa_below, caa_above, state_odd, state_even, odd, even, mask, weights, coef, upward,
     out, wm, wt, mm, mt, sm, st,
 ):
+    below, above = sides(mask_az, near_even, near_odd)
     state_left, state_right = sides(mask, state_even, state_odd)
     from_left, from_right = sides(mask, even, odd)
     for f in range(7):
@@ -578,13 +580,12 @@
                 mt[f - 4, e] = value * caa_step
     for c in range(3):
         for az in range(16):
-            sm[0, c, az] = below[c * 16 + az].astype(F32) * caa_step
             sm[0, c, 16 + az] = own[0, c, az] * caa_step
-            sm[0, c, 32 + az] = above[c * 16 + az].astype(F32) * caa_step
             sm[1, c, 16 + az] = own[1, c, az] * caa_step
-        for az in range(8):
-            sm[1, c, 8 + az] = below[48 + c * 8 + az].astype(F32) * caa_step
-            sm[1, c, 32 + az] = above[48 + c * 8 + az].astype(F32) * caa_step
+        for step, depth in enumerate((16, 8)):
+            for az in [*range(-depth, 0), *range(16, 16 + depth)]:
+                ref, at = source_row(below, above, step, c, az)
+                sm[step, c, 16 + az] = ref[at] * caa_step
         for e in range(12):
             st[0, c, e] = acoustic_tile(from_left, from_right, 12 * c + e) * caa_step
         for e in range(8):
@@ -677,24 +678,25 @@
             pair(step % 2, step // 4, e, step == 7)
 
 
-def call(kernel, name, outs, *args, smem=0, far=0, far_outs=0, scratch=()):
+def call(kernel, name, outs, *args, smem=0, far=0, free=0, scratch=()):
     whole, hbm = pl.BlockSpec(memory_space=pltpu.VMEM), pl.BlockSpec(memory_space=pltpu.HBM)
     args = [pltpu.with_memory_space_constraint(x, pltpu.HBM) if smem <= n < smem + far else x for n, x in enumerate(args)]
-    specs = [pl.BlockSpec(memory_space=pltpu.SMEM)] * smem + [hbm] * far
+    specs = [pl.BlockSpec(memory_space=pltpu.SMEM)] * smem + [hbm] * far + [pl.BlockSpec(memory_space=pl.ANY)] * free
     return pl.pallas_call(
         kernel,
         name=name,
         out_shape=[jax.ShapeDtypeStruct(shape, dtype) for shape, dtype in outs],
-        in_specs=specs + [whole] * (len(args) - smem - far),
-        out_specs=[hbm] * far_outs + [whole] * (len(outs) - far_outs),
+        in_specs=specs + [whole] * (len(args) - smem - far - free),
+        out_specs=[whole] * len(outs),
         scratch_shapes=list(scratch),
         compiler_params=pltpu.CompilerParams(vmem_limit_bytes=VMEM_LIMIT),
     )(*args)
 
 
-def swap_pairs(ours, theirs, axis):
+def swap_pairs(ours, theirs, axis, closed):
     count = lax.axis_size(axis)
-    edges = lambda start: [pair for a in range(start, count - 1, 2) for pair in ((a, a + 1), (a + 1, a))]
+    ends = count if closed else count - 1
+    edges = lambda start: [pair for a in range(start, ends, 2) for pair in ((a, (a + 1) % count), ((a + 1) % count, a))]
     odd = lax.ppermute(theirs, axis, edges(1))
     even = lax.ppermute(ours, axis, edges(0))
     return even, odd
@@ -722,34 +724,34 @@
     sends = lax.dynamic_slice_in_dim(send_list, own_row, 1, axis=0).reshape(-1)
     tile = (8, 128)
     mask = jnp.broadcast_to(((own_row + 1) % 2).astype(F32), tile)
+    mask_az = jnp.broadcast_to(((lax.axis_index("az") + 1) % 2).astype(F32), tile)
     vmem = lambda *shape, dtype=F32: pltpu.VMEM((*shape, *tile), dtype)
 
-    low, high = call(
+    even, odd = call(
         functools.partial(first_kernel, sector),
         "first",
         [((15, *tile), F32)] * 2,
-        u, lm,
+        u, lm, mask_az,
         far=2,
         scratch=[pltpu.VMEM(u.shape, F32), pltpu.VMEM(lm.shape, F32), pltpu.SemaphoreType.DMA((2,))],
     )
-    before, after = both_ways(low, high, "az", True)
+    near_even, near_odd = swap_pairs(even, odd, "az", True)
     even, odd = call(
         functools.partial(les_pack_kernel, sector),
         "les_pack",
         [((4, *tile), F32)] * 2,
-        u, lm, before, after, mask,
+        u, lm, near_odd, near_even, mask_az, mask,
     )
-    even, odd = swap_pairs(even, odd, STREAM)
+    even, odd = swap_pairs(even, odd, STREAM, False)
     sent, um1, ut1 = call(
         functools.partial(les_kernel, sector),
         "les",
         [((slabs * 2, 6, *tile), BF16), ((3, 24, *tile), F32), ((3, 4, *tile), F32)],
-        sends, u, lm, before, after, odd, even, mask, les_weights, les_coef,
-        far=1,
-        far_outs=1,
+        sends, u, lm, near_odd, near_even, odd, even, mask_az, mask, les_weights, les_coef,
+        free=1,
         scratch=[
             vmem(3, 24), vmem(3, 6), vmem(3, 24), vmem(3, 6), vmem(3, 24), vmem(16, 6, dtype=BF16),
-            pltpu.SMEM(sends.shape, jnp.int32), pltpu.SemaphoreType.DMA, pltpu.SemaphoreType.DMA((2, *sends.shape)),
+            pltpu.SMEM(sends.shape, jnp.int32), pltpu.SemaphoreType.DMA,
         ],
     )
     got = lax.all_to_all(sent.reshape(slabs, 96, 128), "gx", 0, 0, tiled=True).reshape(slabs * 2, 6, *tile)
@@ -769,31 +771,31 @@
         [((42, *tile), BF16)] * 2,
         caa_below, caa_above, both, order, mask,
     )
-    state_even, state_odd = swap_pairs(even, odd, STREAM)
+    state_even, state_odd = swap_pairs(even, odd, STREAM, False)
     table = jnp.concatenate([intersection_refs.reshape(-1), offsets])
     got, table, state_odd, state_even, les_out = lax.optimization_barrier((got, table, state_odd, state_even, les_out))
 
-    own, up, down = call(
+    own, even, odd = call(
         functools.partial(blend_kernel, sector),
         "blend",
-        [((2, 3, sector, *tile), F32), ((72, *tile), BF16), ((72, *tile), BF16)],
-        table, got,
+        [((2, 3, sector, *tile), F32), ((54, *tile), BF16), ((54, *tile), BF16)],
+        table, got, mask_az,
         smem=1,
         scratch=[vmem(6, 16)],
     )
-    below, above = both_ways(down, up, "az", True)
+    near_even, near_odd = swap_pairs(even, odd, "az", True)
     even, odd = call(
         functools.partial(source_pack_kernel, sector),
         "source_pack",
         [((30, *tile), BF16)] * 2,
-        own, below, above, order, mask,
+        own, near_odd, near_even, order, mask_az, mask,
     )
-    even, odd = swap_pairs(even, odd, STREAM)
+    even, odd = swap_pairs(even, odd, STREAM, False)
     (caa_out,) = call(
         functools.partial(caa_kernel, sector),
         "caa",
         [((4, lines, length), F32)],
-        w, m, own, below, above, caa_below, caa_above, state_odd, state_even, odd, even, mask, caa_weights, caa_coef, upward,
+        w, m, own, near_odd, near_even, mask_az, caa_below, caa_above, state_odd, state_even, odd, even, mask, caa_weights, caa_coef, upward,
         scratch=[vmem(2, 4, 48), vmem(2, 4, 12), vmem(3, 48), vmem(3, 12), vmem(2, 3, 48), vmem(2, 3, 12)],
     )
     return les_out.reshape(les_velocity.shape), caa_out.reshape(caa_state.shape)

time: 85.1 us -> 87.5 us (1.028)
  the two profiles are of different devices: /device:TPU:27 before, /device:TPU:2 now
where the time goes in v5:
time: 87.5 us; the launch traced here: 87 us
  starting transfers between devices  49.2 us (56%)
  waiting for transfers between devices  22.9 us (26%)
  Pallas kernels  13 us (15%)
  between operations  0.95 us (1%)
  local copies, waits for them, and re-layouts  0.9 us (1%)
    ppermute x5, starting transfers between devices, swap_pairs(): odd = lax.ppermute(theirs, axis, edges(1))  30 us
    pallas_call x9, Pallas kernels, call(): pl.pallas_call(kernel, name=name, out_shape=[jax.ShapeDtypeStruct(shape,...  13 us
    ppermute x5, waiting for transfers between devices, swap_pairs(): odd = lax.ppermute(theirs, axis, edges(1))  11.3 us
    ppermute x5, starting transfers between devices, swap_pairs(): even = lax.ppermute(ours, axis, edges(0))  10.6 us
    ppermute x5, waiting for transfers between devices, swap_pairs(): even = lax.ppermute(ours, axis, edges(0))  6.06 us
    all_to_all x1, starting transfers between devices, body(): lax.all_to_all(sent.reshape(slabs, 96, 128), 'gx', 0, 0, tiled=True)  5.62 us
    ppermute x1, waiting for transfers between devices, both_ways(): lax.ppermute(high, axis, [(i, (i + 1) % count) for i in range(ends)])  3.52 us
    ppermute x1, starting transfers between devices, both_ways(): above = lax.ppermute(low, axis, [((i + 1) % count, i) for i in range(ends)])  2.94 us
  transfers between devices with their start and end apart: 13, of which 8 were waited for; matrix products, arithmetic and copies ran while one was open for 1% of the time, Pallas kernels for 3%

profile of v5, /device:TPU:2, one launch (start us, length us, event | category | flops | bytes accessed | tf_op | source)
XLA Modules:
  0.0 87.0 jit_solution(16997049918824044947)
XLA Ops:
  0.6 0.0 copy-start
  0.7 0.0 copy-start.1
  0.7 0.0 copy-start.2
  0.7 1.1 %first.1 = (f32[15,8,128]{2,1,0:T(8,128)S(1)}, f32[15,8,128]{2,1,0:T(8,128)S(1)}) custom-call(f32[3,128,128]{2,1,0:T(8,128)} %bitcast.13, f32[3,128,128]{2,1,0:T(8,128)} %bitcast.8, f32[8,128]{1,0:T(8,128)S(1)} %broadcast_in_dim.6.mask.mask_az), custom_call_target="tpu_custom_call" | custom-call | tf_op jit(solution)/shard_map/first/pallas_call | solution.py:685
  1.8 4.8 %collective-permute-start = (f32[15,8,128]{2,1,0:T(8,128)S(1)}, f32[15,8,128]{2,1,0:T(8,128)S(1)}, u32[]{:S(2)}, u32[]{:S(2)}) collective-permute-start(f32[15,8,128]{2,1,0:T(8,128)S(1)} %get-tuple-element.21), channel_id=1, source_target_pairs={{1,2},{2,1},{3,4},{4,3},{5,6},{6,5},{7,8},{8,7},{9,10},{10,9},{11,... | collective-permute-start | bytes 184328 | tf_op jit(solution)/shard_map/ppermute | solution.py:700
  6.7 1.9 %collective-permute-start.1 = (f32[15,8,128]{2,1,0:T(8,128)S(1)}, f32[15,8,128]{2,1,0:T(8,128)S(1)}, u32[]{:S(2)}, u32[]{:S(2)}) collective-permute-start(f32[15,8,128]{2,1,0:T(8,128)S(1)} %get-tuple-element.22), channel_id=1, source_target_pairs={{0,1},{1,0},{2,3},{3,2},{4,5},{5,4},{6,7},{7,6},{8,9},{9,8},{10,11... | collective-permute-start | bytes 184328 | tf_op jit(solution)/shard_map/ppermute | solution.py:701
  8.6 0.0 collective-permute-done.near_odd
  8.6 1.2 %collective-permute-done.1.near_even = f32[15,8,128]{2,1,0:T(8,128)S(1)} collective-permute-done((f32[15,8,128]{2,1,0:T(8,128)S(1)}, f32[15,8,128]{2,1,0:T(8,128)S(1)}, u32[]{:S(2)}, u32[]{:S(2)}) %collective-permute-start.1) | collective-permute-done | bytes 61472 | tf_op jit(solution)/shard_map/ppermute | solution.py:701
  9.8 0.0 copy-done.1
  9.8 0.0 copy-done.2
  9.8 0.0 copy-start.4
  9.8 0.0 copy-start.6
  9.8 0.3 les_pack.1
  10.1 14.6 %collective-permute-start.2 = (f32[4,8,128]{2,1,0:T(8,128)S(1)}, f32[4,8,128]{2,1,0:T(8,128)S(1)}, u32[]{:S(2)}, u32[]{:S(2)}) collective-permute-start(f32[4,8,128]{2,1,0:T(8,128)S(1)} %get-tuple-element.23), channel_id=1, source_target_pairs={{16,32},{32,16},{48,64},{64,48},{80,96},{96,80},{112,128},{128,112... | collective-permute-start | bytes 49160 | tf_op jit(solution)/shard_map/ppermute | solution.py:700
  24.7 1.9 %collective-permute-start.3 = (f32[4,8,128]{2,1,0:T(8,128)S(1)}, f32[4,8,128]{2,1,0:T(8,128)S(1)}, u32[]{:S(2)}, u32[]{:S(2)}) collective-permute-start(f32[4,8,128]{2,1,0:T(8,128)S(1)} %get-tuple-element.24), channel_id=1, source_target_pairs={{0,16},{16,0},{32,48},{48,32},{64,80},{80,64},{96,112},{112,96},{1... | collective-permute-start | bytes 49160 | tf_op jit(solution)/shard_map/ppermute | solution.py:701
  26.6 0.0 copy-done
  26.6 0.6 dynamic-slice_reduce_fusion
  27.2 0.1 reshape.34.sends_far
  27.3 0.0 collective-permute-done.2.odd
  27.3 3.0 %collective-permute-done.3.even = f32[4,8,128]{2,1,0:T(8,128)S(1)} collective-permute-done((f32[4,8,128]{2,1,0:T(8,128)S(1)}, f32[4,8,128]{2,1,0:T(8,128)S(1)}, u32[]{:S(2)}, u32[]{:S(2)}) %collective-permute-start.3) | collective-permute-done | bytes 16416 | tf_op jit(solution)/shard_map/ppermute | solution.py:701
  30.3 0.0 copy-done.4
  30.3 0.0 copy-done.6
  30.3 2.9 %les.1 = (bf16[48,6,8,128]{3,2,1,0:T(8,128)(2,1)}, f32[3,24,8,128]{3,2,1,0:T(8,128)S(1)}, f32[3,4,8,128]{3,2,1,0:T(8,128)S(1)}) custom-call(s32[48]{0:T(128)S(1)} %reshape.34.sends_far, f32[3,128,128]{2,1,0:T(8,128)S(1)} %bitcast.15, f32[3,128,128]{2,1,0:T(8,128)S(1)} %bitcast.10, f32[15,8,128]{2,1,0:T(8,128)S(1)} %collective-permute-done.near_odd, ...), custom_call_target="tpu_custom_call" | custom-call | tf_op jit(solution)/shard_map/les/pallas_call | solution.py:685
  33.3 0.0 copy-start.3
  33.3 0.0 copy-start.5
  33.3 5.6 %all-to-all-start = ((bf16[24,96,128]{2,1,0:T(8,128)(2,1)}), bf16[24,96,128]{2,1,0:T(8,128)(2,1)S(1)}, u32[]{:S(2)}, u32[]{:S(2)}) async-start(bf16[24,96,128]{2,1,0:T(8,128)(2,1)} %bitcast.2), calls=%async_computation | async-start | bytes 1179648 | tf_op jit(solution)/shard_map/all_to_all | solution.py:757
  39.0 0.0 copy-done.3
  39.0 0.0 copy-done.5
  39.0 0.0 copy-start.11
  39.0 0.0 copy-start.7
  39.0 0.2 narrow.1.both
  39.2 0.0 collective-permute-start.4
  39.2 2.9 %collective-permute-start.5 = (bf16[112,8,128]{2,1,0:T(8,128)(2,1)S(1)}, bf16[112,8,128]{2,1,0:T(8,128)(2,1)S(1)}, u32[]{:S(2)}, u32[]{:S(2)}) collective-permute-start(bf16[112,8,128]{2,1,0:T(8,128)(2,1)S(1)} %narrow.1.both), channel_id=1, source_target_pairs={{1,0},{2,1},{3,2},{4,3},{5,4},{6,5},{7,6},{8,7},{9,8},{10,9},{11,1... | collective-permute-start | bytes 688136 | tf_op jit(solution)/shard_map/ppermute | solution.py:709
  42.1 0.0 copy-done.11
  42.1 0.1 copy.16
  42.2 0.1 reshape.39
  42.3 3.5 %collective-permute-done.4.below.caa_below = bf16[112,8,128]{2,1,0:T(8,128)(2,1)S(1)} collective-permute-done((bf16[112,8,128]{2,1,0:T(8,128)(2,1)S(1)}, bf16[112,8,128]{2,1,0:T(8,128)(2,1)S(1)}, u32[]{:S(2)}, u32[]{:S(2)}) %collective-permute-start.4) | collective-permute-done | bytes 229408 | tf_op jit(solution)/shard_map/ppermute | solution.py:708
  45.8 0.0 collective-permute-done.5.above.caa_above
  45.8 0.0 copy-done.7
  45.8 0.5 state_pack.1
  46.3 0.0 copy-start.12
  46.3 4.7 %collective-permute-start.6 = (bf16[42,8,128]{2,1,0:T(8,128)(2,1)S(1)}, bf16[42,8,128]{2,1,0:T(8,128)(2,1)S(1)}, u32[]{:S(2)}, u32[]{:S(2)}) collective-permute-start(bf16[42,8,128]{2,1,0:T(8,128)(2,1)S(1)} %get-tuple-element.26), channel_id=1, source_target_pairs={{16,32},{32,16},{48,64},{64,48},{80,96},{96,80},{112,128},{128,112... | collective-permute-start | bytes 258056 | tf_op jit(solution)/shard_map/ppermute | solution.py:700
  51.1 2.2 %collective-permute-start.7 = (bf16[42,8,128]{2,1,0:T(8,128)(2,1)S(1)}, bf16[42,8,128]{2,1,0:T(8,128)(2,1)S(1)}, u32[]{:S(2)}, u32[]{:S(2)}) collective-permute-start(bf16[42,8,128]{2,1,0:T(8,128)(2,1)S(1)} %get-tuple-element.27), channel_id=1, source_target_pairs={{0,16},{16,0},{32,48},{48,32},{64,80},{80,64},{96,112},{112,96},{1... | collective-permute-start | bytes 258056 | tf_op jit(solution)/shard_map/ppermute | solution.py:701
  53.2 0.0 copy-done.12
  53.2 0.1 pad_add_fusion.refs
  53.3 1.6 %les_out.1 = f32[3,128,128]{2,1,0:T(8,128)} custom-call(f32[3,128,128]{2,1,0:T(8,128)S(1)} %bitcast.11, f32[3,24,8,128]{3,2,1,0:T(8,128)S(1)} %get-tuple-element.28.um1, f32[3,4,8,128]{3,2,1,0:T(8,128)S(1)} %get-tuple-element.29.ut1, bf16[2,256,256]{2,1,0:T(8,128)(2,1)S(1)} %copy-done.4, f32[16,8,128]{2,1,0:T(8,128)S(1)} %copy-done.6), custom_call_target="tpu_custom_call" | custom-call | tf_op jit(solution)/shard_map/les_out/pallas_call | solution.py:685
  54.9 6.4 %collective-permute-done.6.state_odd = bf16[42,8,128]{2,1,0:T(8,128)(2,1)S(1)} collective-permute-done((bf16[42,8,128]{2,1,0:T(8,128)(2,1)S(1)}, bf16[42,8,128]{2,1,0:T(8,128)(2,1)S(1)}, u32[]{:S(2)}, u32[]{:S(2)}) %collective-permute-start.6) | collective-permute-done | bytes 86048 | tf_op jit(solution)/shard_map/ppermute | solution.py:700
  61.3 0.0 collective-permute-done.7.state_even
  61.3 2.0 %all-to-all-done = bf16[24,96,128]{2,1,0:T(8,128)(2,1)S(1)} async-done(((bf16[24,96,128]{2,1,0:T(8,128)(2,1)}), bf16[24,96,128]{2,1,0:T(8,128)(2,1)S(1)}, u32[]{:S(2)}, u32[]{:S(2)}) %all-to-all-start) | async-done | bytes 589856 | tf_op jit(solution)/shard_map/all_to_all | solution.py:757
  63.3 1.4 %blend.1 = (f32[2,3,16,8,128]{4,3,2,1,0:T(8,128)S(1)}, bf16[54,8,128]{2,1,0:T(8,128)(2,1)S(1)}, bf16[54,8,128]{2,1,0:T(8,128)(2,1)S(1)}) custom-call(s32[80]{0:T(128)S(1)} %pad_add_fusion.refs, bf16[48,6,8,128]{3,2,1,0:T(8,128)(2,1)S(1)} %bitcast.12, f32[8,128]{1,0:T(8,128)S(1)} %broadcast_in_dim.6.mask.mask_az), custom_call_target="tpu_custom_call" | custom-call | tf_op jit(solution)/shard_map/blend/pallas_call | solution.py:685
  64.7 1.9 %collective-permute-start.8 = (bf16[54,8,128]{2,1,0:T(8,128)(2,1)S(1)}, bf16[54,8,128]{2,1,0:T(8,128)(2,1)S(1)}, u32[]{:S(2)}, u32[]{:S(2)}) collective-permute-start(bf16[54,8,128]{2,1,0:T(8,128)(2,1)S(1)} %get-tuple-element.34), channel_id=1, source_target_pairs={{1,2},{2,1},{3,4},{4,3},{5,6},{6,5},{7,8},{8,7},{9,10},{10,9},{11,... | collective-permute-start | bytes 331784 | tf_op jit(solution)/shard_map/ppermute | solution.py:700
  66.6 2.3 %collective-permute-start.9 = (bf16[54,8,128]{2,1,0:T(8,128)(2,1)S(1)}, bf16[54,8,128]{2,1,0:T(8,128)(2,1)S(1)}, u32[]{:S(2)}, u32[]{:S(2)}) collective-permute-start(bf16[54,8,128]{2,1,0:T(8,128)(2,1)S(1)} %get-tuple-element.35), channel_id=1, source_target_pairs={{0,1},{1,0},{2,3},{3,2},{4,5},{5,4},{6,7},{7,6},{8,9},{9,8},{10,11... | collective-permute-start | bytes 331784 | tf_op jit(solution)/shard_map/ppermute | solution.py:701
  68.9 3.1 %collective-permute-done.8.near_odd = bf16[54,8,128]{2,1,0:T(8,128)(2,1)S(1)} collective-permute-done((bf16[54,8,128]{2,1,0:T(8,128)(2,1)S(1)}, bf16[54,8,128]{2,1,0:T(8,128)(2,1)S(1)}, u32[]{:S(2)}, u32[]{:S(2)}) %collective-permute-start.8) | collective-permute-done | bytes 110624 | tf_op jit(solution)/shard_map/ppermute | solution.py:700
  72.0 0.0 collective-permute-done.9.near_even
  72.0 0.0 copy-start.8
  72.0 0.4 source_pack.1
  72.4 4.0 %collective-permute-start.10 = (bf16[30,8,128]{2,1,0:T(8,128)(2,1)S(1)}, bf16[30,8,128]{2,1,0:T(8,128)(2,1)S(1)}, u32[]{:S(2)}, u32[]{:S(2)}) collective-permute-start(bf16[30,8,128]{2,1,0:T(8,128)(2,1)S(1)} %get-tuple-element.38), channel_id=1, source_target_pairs={{16,32},{32,16},{48,64},{64,48},{80,96},{96,80},{112,128},{128,112... | collective-permute-start | bytes 184328 | tf_op jit(solution)/shard_map/ppermute | solution.py:700
  76.4 2.3 %collective-permute-start.11 = (bf16[30,8,128]{2,1,0:T(8,128)(2,1)S(1)}, bf16[30,8,128]{2,1,0:T(8,128)(2,1)S(1)}, u32[]{:S(2)}, u32[]{:S(2)}) collective-permute-start(bf16[30,8,128]{2,1,0:T(8,128)(2,1)S(1)} %get-tuple-element.39), channel_id=1, source_target_pairs={{0,16},{16,0},{32,48},{48,32},{64,80},{80,64},{96,112},{112,96},{1... | collective-permute-start | bytes 184328 | tf_op jit(solution)/shard_map/ppermute | solution.py:701
  78.7 1.9 %collective-permute-done.10.odd = bf16[30,8,128]{2,1,0:T(8,128)(2,1)S(1)} collective-permute-done((bf16[30,8,128]{2,1,0:T(8,128)(2,1)S(1)}, bf16[30,8,128]{2,1,0:T(8,128)(2,1)S(1)}, u32[]{:S(2)}, u32[]{:S(2)}) %collective-permute-start.10) | collective-permute-done | bytes 61472 | tf_op jit(solution)/shard_map/ppermute | solution.py:700
  80.6 1.9 %collective-permute-done.11.even = bf16[30,8,128]{2,1,0:T(8,128)(2,1)S(1)} collective-permute-done((bf16[30,8,128]{2,1,0:T(8,128)(2,1)S(1)}, bf16[30,8,128]{2,1,0:T(8,128)(2,1)S(1)}, u32[]{:S(2)}, u32[]{:S(2)}) %collective-permute-start.11) | collective-permute-done | bytes 61472 | tf_op jit(solution)/shard_map/ppermute | solution.py:701
  82.5 0.0 copy-done.8
  82.5 0.0 copy-done.9
  82.5 0.0 copy-done.10
  82.5 4.5 %caa.1 = f32[4,128,128]{2,1,0:T(8,128)} custom-call(f32[4,128,128]{2,1,0:T(8,128)S(1)} %bitcast.17, f32[3,128,128]{2,1,0:T(8,128)S(1)} %bitcast.19, f32[2,3,16,8,128]{4,3,2,1,0:T(8,128)S(1)} %get-tuple-element.33.own, bf16[54,8,128]{2,1,0:T(8,128)(2,1)S(1)} %collective-permute-done.8.near_odd, bf16[54,8,128]{2,1,0:T(8,128)(2,1)S(1)} %collective-permute-done.9.near_even, ...), custom_call_target="tpu_custom_call" | custom-call | tf_op jit(solution)/shard_map/caa/pallas_call | solution.py:685
  (4 shorter events, 0.0 us)
Async XLA Ops:
  0.6 26.0 %copy-start = (s32[48,24,2]{0,2,1:T(2,128)S(1)}, s32[48,24,2]{0,2,1:T(2,128)}, u32[]{:S(2)}) copy-start(s32[48,24,2]{0,2,1:T(2,128)} %param.19) | copy-start | bytes 27652
  0.7 9.1 %copy-start.1 = (f32[3,8,16,128]{3,2,1,0:T(8,128)S(1)}, f32[3,8,16,128]{3,2,1,0:T(8,128)}, u32[]{:S(2)}) copy-start(f32[3,8,16,128]{3,2,1,0:T(8,128)} %param.14) | copy-start | bytes 589828
  0.7 9.1 %copy-start.2 = (f32[3,8,16,128]{3,2,1,0:T(8,128)S(1)}, f32[3,8,16,128]{3,2,1,0:T(8,128)}, u32[]{:S(2)}) copy-start(f32[3,8,16,128]{3,2,1,0:T(8,128)} %param.13) | copy-start | bytes 589828
  1.8 6.8 %collective-permute-start = (f32[15,8,128]{2,1,0:T(8,128)S(1)}, f32[15,8,128]{2,1,0:T(8,128)S(1)}, u32[]{:S(2)}, u32[]{:S(2)}) collective-permute-start(f32[15,8,128]{2,1,0:T(8,128)S(1)} %get-tuple-element.21), channel_id=1, source_target_pairs={{1,2},{2,1},{3,4},{4,3},{5,6},{6,5},{7,8},{8,7},{9,10},{10,9},{11,... | collective-permute-start | bytes 184328 | tf_op jit(solution)/shard_map/ppermute | solution.py:700
  6.7 3.1 %collective-permute-start.1 = (f32[15,8,128]{2,1,0:T(8,128)S(1)}, f32[15,8,128]{2,1,0:T(8,128)S(1)}, u32[]{:S(2)}, u32[]{:S(2)}) collective-permute-start(f32[15,8,128]{2,1,0:T(8,128)S(1)} %get-tuple-element.22), channel_id=1, source_target_pairs={{0,1},{1,0},{2,3},{3,2},{4,5},{5,4},{6,7},{7,6},{8,9},{9,8},{10,11... | collective-permute-start | bytes 184328 | tf_op jit(solution)/shard_map/ppermute | solution.py:701
  9.8 20.5 %copy-start.4 = (bf16[2,256,256]{2,1,0:T(8,128)(2,1)S(1)}, bf16[2,256,256]{2,1,0:T(8,128)(2,1)}, u32[]{:S(2)}) copy-start(bf16[2,256,256]{2,1,0:T(8,128)(2,1)} %constant.48.clone.weights) | copy-start | bytes 786436
  9.8 20.5 %copy-start.6 = (f32[16,8,128]{2,1,0:T(8,128)S(1)}, f32[16,8,128]{2,1,0:T(8,128)}, u32[]{:S(2)}) copy-start(f32[16,8,128]{2,1,0:T(8,128)} %constant.49.clone.coef) | copy-start | bytes 196612
  10.1 17.2 %collective-permute-start.2 = (f32[4,8,128]{2,1,0:T(8,128)S(1)}, f32[4,8,128]{2,1,0:T(8,128)S(1)}, u32[]{:S(2)}, u32[]{:S(2)}) collective-permute-start(f32[4,8,128]{2,1,0:T(8,128)S(1)} %get-tuple-element.23), channel_id=1, source_target_pairs={{16,32},{32,16},{48,64},{64,48},{80,96},{96,80},{112,128},{128,112... | collective-permute-start | bytes 49160 | tf_op jit(solution)/shard_map/ppermute | solution.py:700
  24.7 5.6 %collective-permute-start.3 = (f32[4,8,128]{2,1,0:T(8,128)S(1)}, f32[4,8,128]{2,1,0:T(8,128)S(1)}, u32[]{:S(2)}, u32[]{:S(2)}) collective-permute-start(f32[4,8,128]{2,1,0:T(8,128)S(1)} %get-tuple-element.24), channel_id=1, source_target_pairs={{0,16},{16,0},{32,48},{48,32},{64,80},{80,64},{96,112},{112,96},{1... | collective-permute-start | bytes 49160 | tf_op jit(solution)/shard_map/ppermute | solution.py:701
  33.3 5.7 %copy-start.3 = (f32[4,8,16,128]{3,2,1,0:T(8,128)S(1)}, f32[4,8,16,128]{3,2,1,0:T(8,128)}, u32[]{:S(2)}) copy-start(f32[4,8,16,128]{3,2,1,0:T(8,128)} %param.15) | copy-start | bytes 786436
  33.3 5.7 %copy-start.5 = (f32[3,8,16,128]{3,2,1,0:T(8,128)S(1)}, f32[3,8,16,128]{3,2,1,0:T(8,128)}, u32[]{:S(2)}) copy-start(f32[3,8,16,128]{3,2,1,0:T(8,128)} %param.16) | copy-start | bytes 589828
  33.3 29.9 %all-to-all-start = ((bf16[24,96,128]{2,1,0:T(8,128)(2,1)}), bf16[24,96,128]{2,1,0:T(8,128)(2,1)S(1)}, u32[]{:S(2)}, u32[]{:S(2)}) async-start(bf16[24,96,128]{2,1,0:T(8,128)(2,1)} %bitcast.2), calls=%async_computation | async-start | bytes 1179648 | tf_op jit(solution)/shard_map/all_to_all | solution.py:757
  39.0 3.2 %copy-start.11 = (s32[16,4]{0,1:T(4,128)S(1)}, s32[16,4]{0,1:T(4,128)}, u32[]{:S(2)}) copy-start(s32[16,4]{0,1:T(4,128)} %param.17) | copy-start | bytes 772
  39.0 6.8 %copy-start.7 = (bf16[2,128,128]{2,1,0:T(8,128)(2,1)S(1)}, bf16[2,128,128]{2,1,0:T(8,128)(2,1)}, u32[]{:S(2)}) copy-start(bf16[2,128,128]{2,1,0:T(8,128)(2,1)} %constant.53.clone.order) | copy-start | bytes 196612
  39.2 6.7 %collective-permute-start.4 = (bf16[112,8,128]{2,1,0:T(8,128)(2,1)S(1)}, bf16[112,8,128]{2,1,0:T(8,128)(2,1)S(1)}, u32[]{:S(2)}, u32[]{:S(2)}) collective-permute-start(bf16[112,8,128]{2,1,0:T(8,128)(2,1)S(1)} %narrow.1.both), channel_id=1, source_target_pairs={{0,1},{1,2},{2,3},{3,4},{4,5},{5,6},{6,7},{7,8},{8,9},{9,10},{10,1... | collective-permute-start | bytes 688136 | tf_op jit(solution)/shard_map/ppermute | solution.py:708
  39.2 6.6 %collective-permute-start.5 = (bf16[112,8,128]{2,1,0:T(8,128)(2,1)S(1)}, bf16[112,8,128]{2,1,0:T(8,128)(2,1)S(1)}, u32[]{:S(2)}, u32[]{:S(2)}) collective-permute-start(bf16[112,8,128]{2,1,0:T(8,128)(2,1)S(1)} %narrow.1.both), channel_id=1, source_target_pairs={{1,0},{2,1},{3,2},{4,3},{5,4},{6,5},{7,6},{8,7},{9,8},{10,9},{11,1... | collective-permute-start | bytes 688136 | tf_op jit(solution)/shard_map/ppermute | solution.py:709
  46.3 6.9 %copy-start.12 = (s32[16]{0:T(128)S(1)}, s32[16]{0:T(128)}, u32[]{:S(2)}) copy-start(s32[16]{0:T(128)} %param.18) | copy-start | bytes 196
  46.3 14.9 %collective-permute-start.6 = (bf16[42,8,128]{2,1,0:T(8,128)(2,1)S(1)}, bf16[42,8,128]{2,1,0:T(8,128)(2,1)S(1)}, u32[]{:S(2)}, u32[]{:S(2)}) collective-permute-start(bf16[42,8,128]{2,1,0:T(8,128)(2,1)S(1)} %get-tuple-element.26), channel_id=1, source_target_pairs={{16,32},{32,16},{48,64},{64,48},{80,96},{96,80},{112,128},{128,112... | collective-permute-start | bytes 258056 | tf_op jit(solution)/shard_map/ppermute | solution.py:700
  51.1 10.2 %collective-permute-start.7 = (bf16[42,8,128]{2,1,0:T(8,128)(2,1)S(1)}, bf16[42,8,128]{2,1,0:T(8,128)(2,1)S(1)}, u32[]{:S(2)}, u32[]{:S(2)}) collective-permute-start(bf16[42,8,128]{2,1,0:T(8,128)(2,1)S(1)} %get-tuple-element.27), channel_id=1, source_target_pairs={{0,16},{16,0},{32,48},{48,32},{64,80},{80,64},{96,112},{112,96},{1... | collective-permute-start | bytes 258056 | tf_op jit(solution)/shard_map/ppermute | solution.py:701
  64.7 7.3 %collective-permute-start.8 = (bf16[54,8,128]{2,1,0:T(8,128)(2,1)S(1)}, bf16[54,8,128]{2,1,0:T(8,128)(2,1)S(1)}, u32[]{:S(2)}, u32[]{:S(2)}) collective-permute-start(bf16[54,8,128]{2,1,0:T(8,128)(2,1)S(1)} %get-tuple-element.34), channel_id=1, source_target_pairs={{1,2},{2,1},{3,4},{4,3},{5,6},{6,5},{7,8},{8,7},{9,10},{10,9},{11,... | collective-permute-start | bytes 331784 | tf_op jit(solution)/shard_map/ppermute | solution.py:700
  66.6 5.4 %collective-permute-start.9 = (bf16[54,8,128]{2,1,0:T(8,128)(2,1)S(1)}, bf16[54,8,128]{2,1,0:T(8,128)(2,1)S(1)}, u32[]{:S(2)}, u32[]{:S(2)}) collective-permute-start(bf16[54,8,128]{2,1,0:T(8,128)(2,1)S(1)} %get-tuple-element.35), channel_id=1, source_target_pairs={{0,1},{1,0},{2,3},{3,2},{4,5},{5,4},{6,7},{7,6},{8,9},{9,8},{10,11... | collective-permute-start | bytes 331784 | tf_op jit(solution)/shard_map/ppermute | solution.py:701
  72.0 10.5 %copy-start.8 = (bf16[2,128,256]{2,1,0:T(8,128)(2,1)S(1)}, bf16[2,128,256]{2,1,0:T(8,128)(2,1)}, u32[]{:S(2)}) copy-start(bf16[2,128,256]{2,1,0:T(8,128)(2,1)} %constant.50.clone.weights) | copy-start | bytes 393220
  72.0 10.5 %copy-start.9 = (f32[10,8,128]{2,1,0:T(8,128)S(1)}, f32[10,8,128]{2,1,0:T(8,128)}, u32[]{:S(2)}) copy-start(f32[10,8,128]{2,1,0:T(8,128)} %constant.51.clone.coef) | copy-start | bytes 122884
  72.0 10.5 %copy-start.10 = (bf16[160,80]{1,0:T(8,128)(2,1)S(1)}, bf16[160,80]{1,0:T(8,128)(2,1)}, u32[]{:S(2)}) copy-start(bf16[160,80]{1,0:T(8,128)(2,1)} %constant.52.clone.upward) | copy-start | bytes 76804
  72.4 8.2 %collective-permute-start.10 = (bf16[30,8,128]{2,1,0:T(8,128)(2,1)S(1)}, bf16[30,8,128]{2,1,0:T(8,128)(2,1)S(1)}, u32[]{:S(2)}, u32[]{:S(2)}) collective-permute-start(bf16[30,8,128]{2,1,0:T(8,128)(2,1)S(1)} %get-tuple-element.38), channel_id=1, source_target_pairs={{16,32},{32,16},{48,64},{64,48},{80,96},{96,80},{112,128},{128,112... | collective-permute-start | bytes 184328 | tf_op jit(solution)/shard_map/ppermute | solution.py:700
  76.4 6.1 %collective-permute-start.11 = (bf16[30,8,128]{2,1,0:T(8,128)(2,1)S(1)}, bf16[30,8,128]{2,1,0:T(8,128)(2,1)S(1)}, u32[]{:S(2)}, u32[]{:S(2)}) collective-permute-start(bf16[30,8,128]{2,1,0:T(8,128)(2,1)S(1)} %get-tuple-element.39), channel_id=1, source_target_pairs={{0,16},{16,0},{32,48},{48,32},{64,80},{80,64},{96,112},{112,96},{1... | collective-permute-start | bytes 184328 | tf_op jit(solution)/shard_map/ppermute | solution.py:701

commit v6 on v4

--- a/solution.py
+++ b/solution.py
@@ -367,7 +367,7 @@
 
 
 def les_kernel(
-    sector, sends_far, u, lm, before, after, odd, even, mask, weights, coef, sent, um1, ut1, um, ut, mm, mt, lamb, blk, sends, arrived, gone,
+    sector, sends_far, u, lm, before, after, odd, even, mask, weights, coef, sent, um1, ut1, um, ut, mm, mt, lamb, blk, sends, arrived,
 ):
     fetch = pltpu.make_async_copy(sends_far, sends, arrived)
     fetch.start()
@@ -439,26 +439,18 @@
             for j in range(16):
                 blk[j, 3 * step + c] = tiles[j].astype(BF16)
 
-    def send(step):
-        part = pl.ds(3 * step, 3)
-        copies = []
-        for n in range(sends.shape[0]):
-            index = jnp.clip(sends[n], 0, 15)
-            copies.append(pltpu.make_async_copy(blk.at[index, part], sent.at[n, part], gone.at[step, n]))
-            copies[-1].start()
-        return copies
-
     blocks(0)
     fetch.wait()
-    copies = send(0)
 
     for e in range(1, 5):
         rows, _, _, _, slopes, _ = les_element(um1, Shifted(ut1), mm, e, weights, coef, False)
         lamb_of(rows, slopes, lamb, e)
 
     blocks(1)
-    for copy in copies + send(1):
-        copy.wait()
+    for n in range(sends.shape[0]):
+        index = jnp.clip(sends[n], 0, 15)
+        for k in range(6):
+            sent[n, k] = blk[index, k]
 
 
 class Shifted:
@@ -549,6 +541,7 @@
     pack_entries(entries, order, mask, even, odd)
 
 
+CAA_DEPTHS = (13, 12, 9, 8, 5, 4, 1, 0)
 CAA_RANGES = ((0, 12), (1, 11), (1, 11), (2, 10), (2, 10), (3, 9), (3, 9), (4, 8))
 
 
@@ -596,7 +589,7 @@
         y = y[:, :128] + y[:, 128:]
         return [y[8 * n : 8 * n + 8] for n in range(len(tiles))]
 
-    def pair(now, source, e, final):
+    def pair(now, source, e, final, depth):
         rows = [[wm[now, f, 4 * e + i] for i in range(8)] for f in range(4)]
         tiles = [[wt[now, f, e + n] for n in range(2)] for f in range(4)]
         below, above, tile_below, tile_above = max(4 * e - 1, 0), min(4 * e + 8, 47), max(e - 1, 0), min(e + 2, 11)
@@ -610,9 +603,9 @@
                 v2,
             ]
 
-        def update(values, metric, sources, stream, around, up, store):
+        def update(needed, values, metric, sources, stream, around, up, store):
             p, v0, v1, v2 = values
-            for n in range(len(p)):
+            for n in needed:
                 m0, m1, m2 = metric(0, n), metric(1, n), metric(2, n)
                 half = mach_number * m0
                 store(0, n, p[n] - m0 * stream[0][n] - m1 * around[1][n] - m2 * up[1][n])
@@ -640,7 +633,12 @@
             else:
                 wm[1 - now, f, 4 * e + n] = value
 
-        update(rows, lambda c, n: mm[c, 4 * e + n], lambda c, n: sm[source, c, 4 * e + n], stream, around, up, store)
+        for n in range(8):
+            if not 16 - depth <= 4 * e + n < 32 + depth:
+                for f in range(4):
+                    wm[1 - now, f, 4 * e + n] = rows[f][n]
+        needed = [n for n in range(8) if 16 - depth <= 4 * e + n < 32 + depth]
+        update(needed, rows, lambda c, n: mm[c, 4 * e + n], lambda c, n: sm[source, c, 4 * e + n], stream, around, up, store)
         if final:
             return
 
@@ -670,23 +668,23 @@
             wt[1 - now, f, e + n] = value
 
         up = [values[8:] for values in up]
-        update(tiles, lambda c, n: mt[c, e + n], lambda c, n: st[source, c, e + n], stream, around, up, store)
+        update(range(2), tiles, lambda c, n: mt[c, e + n], lambda c, n: st[source, c, e + n], stream, around, up, store)
 
     for step, (start, stop) in enumerate(CAA_RANGES):
         for e in range(start, stop, 2):
-            pair(step % 2, step // 4, e, step == 7)
-
-
-def call(kernel, name, outs, *args, smem=0, far=0, far_outs=0, scratch=()):
+            pair(step % 2, step // 4, e, step == 7, CAA_DEPTHS[step])
+
+
+def call(kernel, name, outs, *args, smem=0, far=0, free=0, scratch=()):
     whole, hbm = pl.BlockSpec(memory_space=pltpu.VMEM), pl.BlockSpec(memory_space=pltpu.HBM)
     args = [pltpu.with_memory_space_constraint(x, pltpu.HBM) if smem <= n < smem + far else x for n, x in enumerate(args)]
-    specs = [pl.BlockSpec(memory_space=pltpu.SMEM)] * smem + [hbm] * far
+    specs = [pl.BlockSpec(memory_space=pltpu.SMEM)] * smem + [hbm] * far + [pl.BlockSpec(memory_space=pl.ANY)] * free
     return pl.pallas_call(
         kernel,
         name=name,
         out_shape=[jax.ShapeDtypeStruct(shape, dtype) for shape, dtype in outs],
-        in_specs=specs + [whole] * (len(args) - smem - far),
-        out_specs=[hbm] * far_outs + [whole] * (len(outs) - far_outs),
+        in_specs=specs + [whole] * (len(args) - smem - far - free),
+        out_specs=[whole] * len(outs),
         scratch_shapes=list(scratch),
         compiler_params=pltpu.CompilerParams(vmem_limit_bytes=VMEM_LIMIT),
     )(*args)
@@ -745,11 +743,10 @@
         "les",
         [((slabs * 2, 6, *tile), BF16), ((3, 24, *tile), F32), ((3, 4, *tile), F32)],
         sends, u, lm, before, after, odd, even, mask, les_weights, les_coef,
-        far=1,
-        far_outs=1,
+        free=1,
         scratch=[
             vmem(3, 24), vmem(3, 6), vmem(3, 24), vmem(3, 6), vmem(3, 24), vmem(16, 6, dtype=BF16),
-            pltpu.SMEM(sends.shape, jnp.int32), pltpu.SemaphoreType.DMA, pltpu.SemaphoreType.DMA((2, *sends.shape)),
+            pltpu.SMEM(sends.shape, jnp.int32), pltpu.SemaphoreType.DMA,
         ],
     )
     got = lax.all_to_all(sent.reshape(slabs, 96, 128), "gx", 0, 0, tiled=True).reshape(slabs * 2, 6, *tile)

time: 85.1 us -> 84.2 us (0.989)
  transfers between devices with their start and end apart: 13 -> 13, of which waited for: 11 -> 11; matrix products, arithmetic and copies ran while one was open for 2% -> 1% of each run, Pallas kernels for 3% -> 3%
where the time goes in v6:
time: 84.2 us; the launch traced here: 83.8 us
  starting transfers between devices  40.5 us (48%)
  waiting for transfers between devices  28.3 us (34%)
  Pallas kernels  13.2 us (16%)
  local copies, waits for them, and re-layouts  0.89 us (1%)
  between operations  0.87 us (1%)
    ppermute x3, starting transfers between devices, swap_pairs(): odd = lax.ppermute(theirs, axis, edges(1))  22.5 us
    pallas_call x9, Pallas kernels, call(): pl.pallas_call(kernel, name=name, out_shape=[jax.ShapeDtypeStruct(shape,...  13.2 us
    ppermute x3, waiting for transfers between devices, both_ways(): above = lax.ppermute(low, axis, [((i + 1) % count, i) for i in range(ends)])  11.2 us
    ppermute x3, starting transfers between devices, both_ways(): lax.ppermute(high, axis, [(i, (i + 1) % count) for i in range(ends)])  6.53 us
    ppermute x3, starting transfers between devices, swap_pairs(): even = lax.ppermute(ours, axis, edges(0))  6.39 us
    ppermute x3, waiting for transfers between devices, both_ways(): lax.ppermute(high, axis, [(i, (i + 1) % count) for i in range(ends)])  6.18 us
    ppermute x3, waiting for transfers between devices, swap_pairs(): odd = lax.ppermute(theirs, axis, edges(1))  5.59 us
    all_to_all x1, starting transfers between devices, body(): lax.all_to_all(sent.reshape(slabs, 96, 128), 'gx', 0, 0, tiled=True)  5.07 us
  transfers between devices with their start and end apart: 13, of which 11 were waited for; matrix products, arithmetic and copies ran while one was open for 1% of the time, Pallas kernels for 3%

profile of v6, /device:TPU:27, one launch (start us, length us, event | category | flops | bytes accessed | tf_op | source)
XLA Modules:
  0.0 83.8 jit_solution(11951307020512259305)
XLA Ops:
  0.6 0.0 copy-start
  0.6 0.0 copy-start.1
  0.7 0.0 copy-start.2
  0.7 1.1 %first.1 = (f32[15,8,128]{2,1,0:T(8,128)S(1)}, f32[15,8,128]{2,1,0:T(8,128)S(1)}) custom-call(f32[3,128,128]{2,1,0:T(8,128)} %bitcast.13, f32[3,128,128]{2,1,0:T(8,128)} %bitcast.8), custom_call_target="tpu_custom_call" | custom-call | tf_op jit(solution)/shard_map/first/pallas_call | solution.py:682
  1.8 3.1 %collective-permute-start = (f32[15,8,128]{2,1,0:T(8,128)S(1)}, f32[15,8,128]{2,1,0:T(8,128)S(1)}, u32[]{:S(2)}, u32[]{:S(2)}) collective-permute-start(f32[15,8,128]{2,1,0:T(8,128)S(1)} %get-tuple-element.21), channel_id=1, source_target_pairs={{0,1},{1,2},{2,3},{3,4},{4,5},{5,6},{6,7},{7,8},{8,9},{9,10},{10,1... | collective-permute-start | bytes 184328 | tf_op jit(solution)/shard_map/ppermute | solution.py:704
  4.9 0.0 collective-permute-start.1
  4.9 1.3 %collective-permute-done.before = f32[15,8,128]{2,1,0:T(8,128)S(1)} collective-permute-done((f32[15,8,128]{2,1,0:T(8,128)S(1)}, f32[15,8,128]{2,1,0:T(8,128)S(1)}, u32[]{:S(2)}, u32[]{:S(2)}) %collective-permute-start) | collective-permute-done | bytes 61472 | tf_op jit(solution)/shard_map/ppermute | solution.py:704
  6.2 3.6 %collective-permute-done.1.after = f32[15,8,128]{2,1,0:T(8,128)S(1)} collective-permute-done((f32[15,8,128]{2,1,0:T(8,128)S(1)}, f32[15,8,128]{2,1,0:T(8,128)S(1)}, u32[]{:S(2)}, u32[]{:S(2)}) %collective-permute-start.1) | collective-permute-done | bytes 61472 | tf_op jit(solution)/shard_map/ppermute | solution.py:705
  9.7 0.0 copy-done.1
  9.7 0.0 copy-done.2
  9.7 0.0 copy-start.4
  9.8 0.0 copy-start.7
  9.8 0.3 les_pack.1
  10.1 14.3 %collective-permute-start.2 = (f32[4,8,128]{2,1,0:T(8,128)S(1)}, f32[4,8,128]{2,1,0:T(8,128)S(1)}, u32[]{:S(2)}, u32[]{:S(2)}) collective-permute-start(f32[4,8,128]{2,1,0:T(8,128)S(1)} %get-tuple-element.23), channel_id=1, source_target_pairs={{16,32},{32,16},{48,64},{64,48},{80,96},{96,80},{112,128},{128,112... | collective-permute-start | bytes 49160 | tf_op jit(solution)/shard_map/ppermute | solution.py:696
  24.4 1.9 %collective-permute-start.3 = (f32[4,8,128]{2,1,0:T(8,128)S(1)}, f32[4,8,128]{2,1,0:T(8,128)S(1)}, u32[]{:S(2)}, u32[]{:S(2)}) collective-permute-start(f32[4,8,128]{2,1,0:T(8,128)S(1)} %get-tuple-element.24), channel_id=1, source_target_pairs={{0,16},{16,0},{32,48},{48,32},{64,80},{80,64},{96,112},{112,96},{1... | collective-permute-start | bytes 49160 | tf_op jit(solution)/shard_map/ppermute | solution.py:697
  26.3 0.0 copy-done
  26.3 0.6 dynamic-slice_reduce_fusion
  26.9 0.1 reshape.34.sends_far
  27.0 0.0 collective-permute-done.2.odd
  27.0 1.9 %collective-permute-done.3.even = f32[4,8,128]{2,1,0:T(8,128)S(1)} collective-permute-done((f32[4,8,128]{2,1,0:T(8,128)S(1)}, f32[4,8,128]{2,1,0:T(8,128)S(1)}, u32[]{:S(2)}, u32[]{:S(2)}) %collective-permute-start.3) | collective-permute-done | bytes 16416 | tf_op jit(solution)/shard_map/ppermute | solution.py:697
  28.9 0.0 copy-done.4
  28.9 0.0 copy-done.7
  28.9 2.9 %les.1 = (bf16[48,6,8,128]{3,2,1,0:T(8,128)(2,1)}, f32[3,24,8,128]{3,2,1,0:T(8,128)S(1)}, f32[3,4,8,128]{3,2,1,0:T(8,128)S(1)}) custom-call(s32[48]{0:T(128)S(1)} %reshape.34.sends_far, f32[3,128,128]{2,1,0:T(8,128)S(1)} %bitcast.15, f32[3,128,128]{2,1,0:T(8,128)S(1)} %bitcast.10, f32[15,8,128]{2,1,0:T(8,128)S(1)} %collective-permute-done.before, ...), custom_call_target="tpu_custom_call" | custom-call | tf_op jit(solution)/shard_map/les/pallas_call | solution.py:682
  31.8 0.0 copy-start.3
  31.8 0.0 copy-start.5
  31.8 5.1 %all-to-all-start = ((bf16[24,96,128]{2,1,0:T(8,128)(2,1)}), bf16[24,96,128]{2,1,0:T(8,128)(2,1)S(1)}, u32[]{:S(2)}, u32[]{:S(2)}) async-start(bf16[24,96,128]{2,1,0:T(8,128)(2,1)} %bitcast.2), calls=%async_computation | async-start | bytes 1179648 | tf_op jit(solution)/shard_map/all_to_all | solution.py:752
  36.9 0.0 copy-done.3
  36.9 0.0 copy-done.5
  36.9 0.0 copy-start.11
  36.9 0.0 copy-start.6
  36.9 0.2 narrow.1.both
  37.1 2.0 %collective-permute-start.4 = (bf16[112,8,128]{2,1,0:T(8,128)(2,1)S(1)}, bf16[112,8,128]{2,1,0:T(8,128)(2,1)S(1)}, u32[]{:S(2)}, u32[]{:S(2)}) collective-permute-start(bf16[112,8,128]{2,1,0:T(8,128)(2,1)S(1)} %narrow.1.both), channel_id=1, source_target_pairs={{0,1},{1,2},{2,3},{3,4},{4,5},{5,6},{6,7},{7,8},{8,9},{9,10},{10,1... | collective-permute-start | bytes 688136 | tf_op jit(solution)/shard_map/ppermute | solution.py:704
  39.1 0.0 collective-permute-start.5
  39.1 0.0 copy-done.11
  39.1 0.1 copy.16
  39.2 0.1 reshape.39
  39.3 2.8 %collective-permute-done.4.below.caa_below = bf16[112,8,128]{2,1,0:T(8,128)(2,1)S(1)} collective-permute-done((bf16[112,8,128]{2,1,0:T(8,128)(2,1)S(1)}, bf16[112,8,128]{2,1,0:T(8,128)(2,1)S(1)}, u32[]{:S(2)}, u32[]{:S(2)}) %collective-permute-start.4) | collective-permute-done | bytes 229408 | tf_op jit(solution)/shard_map/ppermute | solution.py:704
  42.1 4.0 %collective-permute-done.5.above.caa_above = bf16[112,8,128]{2,1,0:T(8,128)(2,1)S(1)} collective-permute-done((bf16[112,8,128]{2,1,0:T(8,128)(2,1)S(1)}, bf16[112,8,128]{2,1,0:T(8,128)(2,1)S(1)}, u32[]{:S(2)}, u32[]{:S(2)}) %collective-permute-start.5) | collective-permute-done | bytes 229408 | tf_op jit(solution)/shard_map/ppermute | solution.py:705
  46.1 0.0 copy-done.6
  46.1 0.5 state_pack.1
  46.6 0.0 copy-start.12
  46.6 4.4 %collective-permute-start.6 = (bf16[42,8,128]{2,1,0:T(8,128)(2,1)S(1)}, bf16[42,8,128]{2,1,0:T(8,128)(2,1)S(1)}, u32[]{:S(2)}, u32[]{:S(2)}) collective-permute-start(bf16[42,8,128]{2,1,0:T(8,128)(2,1)S(1)} %get-tuple-element.26), channel_id=1, source_target_pairs={{16,32},{32,16},{48,64},{64,48},{80,96},{96,80},{112,128},{128,112... | collective-permute-start | bytes 258056 | tf_op jit(solution)/shard_map/ppermute | solution.py:696
  51.0 1.9 %collective-permute-start.7 = (bf16[42,8,128]{2,1,0:T(8,128)(2,1)S(1)}, bf16[42,8,128]{2,1,0:T(8,128)(2,1)S(1)}, u32[]{:S(2)}, u32[]{:S(2)}) collective-permute-start(bf16[42,8,128]{2,1,0:T(8,128)(2,1)S(1)} %get-tuple-element.27), channel_id=1, source_target_pairs={{0,16},{16,0},{32,48},{48,32},{64,80},{80,64},{96,112},{112,96},{1... | collective-permute-start | bytes 258056 | tf_op jit(solution)/shard_map/ppermute | solution.py:697
  53.0 0.0 copy-done.12
  53.0 0.1 pad_add_fusion.refs
  53.0 1.6 %les_out.1 = f32[3,128,128]{2,1,0:T(8,128)} custom-call(f32[3,128,128]{2,1,0:T(8,128)S(1)} %bitcast.11, f32[3,24,8,128]{3,2,1,0:T(8,128)S(1)} %get-tuple-element.28.um1, f32[3,4,8,128]{3,2,1,0:T(8,128)S(1)} %get-tuple-element.29.ut1, bf16[2,256,256]{2,1,0:T(8,128)(2,1)S(1)} %copy-done.4, f32[16,8,128]{2,1,0:T(8,128)S(1)} %copy-done.7), custom_call_target="tpu_custom_call" | custom-call | tf_op jit(solution)/shard_map/les_out/pallas_call | solution.py:682
  54.6 4.9 %collective-permute-done.6.state_odd = bf16[42,8,128]{2,1,0:T(8,128)(2,1)S(1)} collective-permute-done((bf16[42,8,128]{2,1,0:T(8,128)(2,1)S(1)}, bf16[42,8,128]{2,1,0:T(8,128)(2,1)S(1)}, u32[]{:S(2)}, u32[]{:S(2)}) %collective-permute-start.6) | collective-permute-done | bytes 86048 | tf_op jit(solution)/shard_map/ppermute | solution.py:696
  59.5 0.0 collective-permute-done.7.state_even
  59.5 1.7 %all-to-all-done = bf16[24,96,128]{2,1,0:T(8,128)(2,1)S(1)} async-done(((bf16[24,96,128]{2,1,0:T(8,128)(2,1)}), bf16[24,96,128]{2,1,0:T(8,128)(2,1)S(1)}, u32[]{:S(2)}, u32[]{:S(2)}) %all-to-all-start) | async-done | bytes 589856 | tf_op jit(solution)/shard_map/all_to_all | solution.py:752
  61.2 1.4 %blend.1 = (f32[2,3,16,8,128]{4,3,2,1,0:T(8,128)S(1)}, bf16[72,8,128]{2,1,0:T(8,128)(2,1)S(1)}, bf16[72,8,128]{2,1,0:T(8,128)(2,1)S(1)}) custom-call(s32[80]{0:T(128)S(1)} %pad_add_fusion.refs, bf16[48,6,8,128]{3,2,1,0:T(8,128)(2,1)S(1)} %bitcast.12), custom_call_target="tpu_custom_call" | custom-call | tf_op jit(solution)/shard_map/blend/pallas_call | solution.py:682
  62.7 1.4 %collective-permute-start.8 = (bf16[72,8,128]{2,1,0:T(8,128)(2,1)S(1)}, bf16[72,8,128]{2,1,0:T(8,128)(2,1)S(1)}, u32[]{:S(2)}, u32[]{:S(2)}) collective-permute-start(bf16[72,8,128]{2,1,0:T(8,128)(2,1)S(1)} %get-tuple-element.34), channel_id=1, source_target_pairs={{0,1},{1,2},{2,3},{3,4},{4,5},{5,6},{6,7},{7,8},{8,9},{9,10},{10,1... | collective-permute-start | bytes 442376 | tf_op jit(solution)/shard_map/ppermute | solution.py:704
  64.1 0.0 collective-permute-start.9
  64.1 2.1 %collective-permute-done.8.below = bf16[72,8,128]{2,1,0:T(8,128)(2,1)S(1)} collective-permute-done((bf16[72,8,128]{2,1,0:T(8,128)(2,1)S(1)}, bf16[72,8,128]{2,1,0:T(8,128)(2,1)S(1)}, u32[]{:S(2)}, u32[]{:S(2)}) %collective-permute-start.8) | collective-permute-done | bytes 147488 | tf_op jit(solution)/shard_map/ppermute | solution.py:704
  66.2 3.7 %collective-permute-done.9.above = bf16[72,8,128]{2,1,0:T(8,128)(2,1)S(1)} collective-permute-done((bf16[72,8,128]{2,1,0:T(8,128)(2,1)S(1)}, bf16[72,8,128]{2,1,0:T(8,128)(2,1)S(1)}, u32[]{:S(2)}, u32[]{:S(2)}) %collective-permute-start.9) | collective-permute-done | bytes 147488 | tf_op jit(solution)/shard_map/ppermute | solution.py:705
  69.9 0.0 copy-start.8
  69.9 0.4 source_pack.1
  70.3 3.8 %collective-permute-start.10 = (bf16[30,8,128]{2,1,0:T(8,128)(2,1)S(1)}, bf16[30,8,128]{2,1,0:T(8,128)(2,1)S(1)}, u32[]{:S(2)}, u32[]{:S(2)}) collective-permute-start(bf16[30,8,128]{2,1,0:T(8,128)(2,1)S(1)} %get-tuple-element.38), channel_id=1, source_target_pairs={{16,32},{32,16},{48,64},{64,48},{80,96},{96,80},{112,128},{128,112... | collective-permute-start | bytes 184328 | tf_op jit(solution)/shard_map/ppermute | solution.py:696
  74.1 2.6 %collective-permute-start.11 = (bf16[30,8,128]{2,1,0:T(8,128)(2,1)S(1)}, bf16[30,8,128]{2,1,0:T(8,128)(2,1)S(1)}, u32[]{:S(2)}, u32[]{:S(2)}) collective-permute-start(bf16[30,8,128]{2,1,0:T(8,128)(2,1)S(1)} %get-tuple-element.39), channel_id=1, source_target_pairs={{0,16},{16,0},{32,48},{48,32},{64,80},{80,64},{96,112},{112,96},{1... | collective-permute-start | bytes 184328 | tf_op jit(solution)/shard_map/ppermute | solution.py:697
  76.7 0.7 collective-permute-done.10.odd
  77.4 1.7 %collective-permute-done.11.even = bf16[30,8,128]{2,1,0:T(8,128)(2,1)S(1)} collective-permute-done((bf16[30,8,128]{2,1,0:T(8,128)(2,1)S(1)}, bf16[30,8,128]{2,1,0:T(8,128)(2,1)S(1)}, u32[]{:S(2)}, u32[]{:S(2)}) %collective-permute-start.11) | collective-permute-done | bytes 61472 | tf_op jit(solution)/shard_map/ppermute | solution.py:697
  79.1 0.0 copy-done.8
  79.1 0.0 copy-done.9
  79.1 0.0 copy-done.10
  79.1 4.7 %caa.1 = f32[4,128,128]{2,1,0:T(8,128)} custom-call(f32[4,128,128]{2,1,0:T(8,128)S(1)} %bitcast.17, f32[3,128,128]{2,1,0:T(8,128)S(1)} %bitcast.19, f32[2,3,16,8,128]{4,3,2,1,0:T(8,128)S(1)} %get-tuple-element.33.own, bf16[72,8,128]{2,1,0:T(8,128)(2,1)S(1)} %collective-permute-done.8.below, bf16[72,8,128]{2,1,0:T(8,128)(2,1)S(1)} %collective-permute-done.9.above, ...), custom_call_target="tpu_custom_call" | custom-call | tf_op jit(solution)/shard_map/caa/pallas_call | solution.py:682
  (3 shorter events, 0.0 us)
Async XLA Ops:
  0.6 25.7 %copy-start = (s32[48,24,2]{0,2,1:T(2,128)S(1)}, s32[48,24,2]{0,2,1:T(2,128)}, u32[]{:S(2)}) copy-start(s32[48,24,2]{0,2,1:T(2,128)} %param.19) | copy-start | bytes 27652
  0.6 9.1 %copy-start.1 = (f32[3,8,16,128]{3,2,1,0:T(8,128)S(1)}, f32[3,8,16,128]{3,2,1,0:T(8,128)}, u32[]{:S(2)}) copy-start(f32[3,8,16,128]{3,2,1,0:T(8,128)} %param.14) | copy-start | bytes 589828
  0.7 9.1 %copy-start.2 = (f32[3,8,16,128]{3,2,1,0:T(8,128)S(1)}, f32[3,8,16,128]{3,2,1,0:T(8,128)}, u32[]{:S(2)}) copy-start(f32[3,8,16,128]{3,2,1,0:T(8,128)} %param.13) | copy-start | bytes 589828
  1.8 4.4 %collective-permute-start = (f32[15,8,128]{2,1,0:T(8,128)S(1)}, f32[15,8,128]{2,1,0:T(8,128)S(1)}, u32[]{:S(2)}, u32[]{:S(2)}) collective-permute-start(f32[15,8,128]{2,1,0:T(8,128)S(1)} %get-tuple-element.21), channel_id=1, source_target_pairs={{0,1},{1,2},{2,3},{3,4},{4,5},{5,6},{6,7},{7,8},{8,9},{9,10},{10,1... | collective-permute-start | bytes 184328 | tf_op jit(solution)/shard_map/ppermute | solution.py:704
  4.9 4.9 %collective-permute-start.1 = (f32[15,8,128]{2,1,0:T(8,128)S(1)}, f32[15,8,128]{2,1,0:T(8,128)S(1)}, u32[]{:S(2)}, u32[]{:S(2)}) collective-permute-start(f32[15,8,128]{2,1,0:T(8,128)S(1)} %get-tuple-element.22), channel_id=1, source_target_pairs={{1,0},{2,1},{3,2},{4,3},{5,4},{6,5},{7,6},{8,7},{9,8},{10,9},{11,1... | collective-permute-start | bytes 184328 | tf_op jit(solution)/shard_map/ppermute | solution.py:705
  9.7 19.1 %copy-start.4 = (bf16[2,256,256]{2,1,0:T(8,128)(2,1)S(1)}, bf16[2,256,256]{2,1,0:T(8,128)(2,1)}, u32[]{:S(2)}) copy-start(bf16[2,256,256]{2,1,0:T(8,128)(2,1)} %constant.41.clone.weights) | copy-start | bytes 786436
  9.8 19.1 %copy-start.7 = (f32[16,8,128]{2,1,0:T(8,128)S(1)}, f32[16,8,128]{2,1,0:T(8,128)}, u32[]{:S(2)}) copy-start(f32[16,8,128]{2,1,0:T(8,128)} %constant.42.clone.coef) | copy-start | bytes 196612
  10.1 16.9 %collective-permute-start.2 = (f32[4,8,128]{2,1,0:T(8,128)S(1)}, f32[4,8,128]{2,1,0:T(8,128)S(1)}, u32[]{:S(2)}, u32[]{:S(2)}) collective-permute-start(f32[4,8,128]{2,1,0:T(8,128)S(1)} %get-tuple-element.23), channel_id=1, source_target_pairs={{16,32},{32,16},{48,64},{64,48},{80,96},{96,80},{112,128},{128,112... | collective-permute-start | bytes 49160 | tf_op jit(solution)/shard_map/ppermute | solution.py:696
  24.4 4.5 %collective-permute-start.3 = (f32[4,8,128]{2,1,0:T(8,128)S(1)}, f32[4,8,128]{2,1,0:T(8,128)S(1)}, u32[]{:S(2)}, u32[]{:S(2)}) collective-permute-start(f32[4,8,128]{2,1,0:T(8,128)S(1)} %get-tuple-element.24), channel_id=1, source_target_pairs={{0,16},{16,0},{32,48},{48,32},{64,80},{80,64},{96,112},{112,96},{1... | collective-permute-start | bytes 49160 | tf_op jit(solution)/shard_map/ppermute | solution.py:697
  31.8 5.1 %copy-start.3 = (f32[4,8,16,128]{3,2,1,0:T(8,128)S(1)}, f32[4,8,16,128]{3,2,1,0:T(8,128)}, u32[]{:S(2)}) copy-start(f32[4,8,16,128]{3,2,1,0:T(8,128)} %param.15) | copy-start | bytes 786436
  31.8 5.1 %copy-start.5 = (f32[3,8,16,128]{3,2,1,0:T(8,128)S(1)}, f32[3,8,16,128]{3,2,1,0:T(8,128)}, u32[]{:S(2)}) copy-start(f32[3,8,16,128]{3,2,1,0:T(8,128)} %param.16) | copy-start | bytes 589828
  31.8 29.4 %all-to-all-start = ((bf16[24,96,128]{2,1,0:T(8,128)(2,1)}), bf16[24,96,128]{2,1,0:T(8,128)(2,1)S(1)}, u32[]{:S(2)}, u32[]{:S(2)}) async-start(bf16[24,96,128]{2,1,0:T(8,128)(2,1)} %bitcast.2), calls=%async_computation | async-start | bytes 1179648 | tf_op jit(solution)/shard_map/all_to_all | solution.py:752
  36.9 2.2 %copy-start.11 = (s32[16,4]{0,1:T(4,128)S(1)}, s32[16,4]{0,1:T(4,128)}, u32[]{:S(2)}) copy-start(s32[16,4]{0,1:T(4,128)} %param.17) | copy-start | bytes 772
  36.9 9.1 %copy-start.6 = (bf16[2,128,128]{2,1,0:T(8,128)(2,1)S(1)}, bf16[2,128,128]{2,1,0:T(8,128)(2,1)}, u32[]{:S(2)}) copy-start(bf16[2,128,128]{2,1,0:T(8,128)(2,1)} %constant.46.clone.order) | copy-start | bytes 196612
  37.1 5.0 %collective-permute-start.4 = (bf16[112,8,128]{2,1,0:T(8,128)(2,1)S(1)}, bf16[112,8,128]{2,1,0:T(8,128)(2,1)S(1)}, u32[]{:S(2)}, u32[]{:S(2)}) collective-permute-start(bf16[112,8,128]{2,1,0:T(8,128)(2,1)S(1)} %narrow.1.both), channel_id=1, source_target_pairs={{0,1},{1,2},{2,3},{3,4},{4,5},{5,6},{6,7},{7,8},{8,9},{9,10},{10,1... | collective-permute-start | bytes 688136 | tf_op jit(solution)/shard_map/ppermute | solution.py:704
  39.1 7.0 %collective-permute-start.5 = (bf16[112,8,128]{2,1,0:T(8,128)(2,1)S(1)}, bf16[112,8,128]{2,1,0:T(8,128)(2,1)S(1)}, u32[]{:S(2)}, u32[]{:S(2)}) collective-permute-start(bf16[112,8,128]{2,1,0:T(8,128)(2,1)S(1)} %narrow.1.both), channel_id=1, source_target_pairs={{1,0},{2,1},{3,2},{4,3},{5,4},{6,5},{7,6},{8,7},{9,8},{10,9},{11,1... | collective-permute-start | bytes 688136 | tf_op jit(solution)/shard_map/ppermute | solution.py:705
  46.6 6.4 %copy-start.12 = (s32[16]{0:T(128)S(1)}, s32[16]{0:T(128)}, u32[]{:S(2)}) copy-start(s32[16]{0:T(128)} %param.18) | copy-start | bytes 196
  46.6 12.9 %collective-permute-start.6 = (bf16[42,8,128]{2,1,0:T(8,128)(2,1)S(1)}, bf16[42,8,128]{2,1,0:T(8,128)(2,1)S(1)}, u32[]{:S(2)}, u32[]{:S(2)}) collective-permute-start(bf16[42,8,128]{2,1,0:T(8,128)(2,1)S(1)} %get-tuple-element.26), channel_id=1, source_target_pairs={{16,32},{32,16},{48,64},{64,48},{80,96},{96,80},{112,128},{128,112... | collective-permute-start | bytes 258056 | tf_op jit(solution)/shard_map/ppermute | solution.py:696
  51.0 8.5 %collective-permute-start.7 = (bf16[42,8,128]{2,1,0:T(8,128)(2,1)S(1)}, bf16[42,8,128]{2,1,0:T(8,128)(2,1)S(1)}, u32[]{:S(2)}, u32[]{:S(2)}) collective-permute-start(bf16[42,8,128]{2,1,0:T(8,128)(2,1)S(1)} %get-tuple-element.27), channel_id=1, source_target_pairs={{0,16},{16,0},{32,48},{48,32},{64,80},{80,64},{96,112},{112,96},{1... | collective-permute-start | bytes 258056 | tf_op jit(solution)/shard_map/ppermute | solution.py:697
  62.7 3.5 %collective-permute-start.8 = (bf16[72,8,128]{2,1,0:T(8,128)(2,1)S(1)}, bf16[72,8,128]{2,1,0:T(8,128)(2,1)S(1)}, u32[]{:S(2)}, u32[]{:S(2)}) collective-permute-start(bf16[72,8,128]{2,1,0:T(8,128)(2,1)S(1)} %get-tuple-element.34), channel_id=1, source_target_pairs={{0,1},{1,2},{2,3},{3,4},{4,5},{5,6},{6,7},{7,8},{8,9},{9,10},{10,1... | collective-permute-start | bytes 442376 | tf_op jit(solution)/shard_map/ppermute | solution.py:704
  64.1 5.8 %collective-permute-start.9 = (bf16[72,8,128]{2,1,0:T(8,128)(2,1)S(1)}, bf16[72,8,128]{2,1,0:T(8,128)(2,1)S(1)}, u32[]{:S(2)}, u32[]{:S(2)}) collective-permute-start(bf16[72,8,128]{2,1,0:T(8,128)(2,1)S(1)} %get-tuple-element.35), channel_id=1, source_target_pairs={{1,0},{2,1},{3,2},{4,3},{5,4},{6,5},{7,6},{8,7},{9,8},{10,9},{11,1... | collective-permute-start | bytes 442376 | tf_op jit(solution)/shard_map/ppermute | solution.py:705
  69.9 9.2 %copy-start.8 = (bf16[2,128,256]{2,1,0:T(8,128)(2,1)S(1)}, bf16[2,128,256]{2,1,0:T(8,128)(2,1)}, u32[]{:S(2)}) copy-start(bf16[2,128,256]{2,1,0:T(8,128)(2,1)} %constant.43.clone.weights) | copy-start | bytes 393220
  69.9 9.2 %copy-start.9 = (f32[10,8,128]{2,1,0:T(8,128)S(1)}, f32[10,8,128]{2,1,0:T(8,128)}, u32[]{:S(2)}) copy-start(f32[10,8,128]{2,1,0:T(8,128)} %constant.44.clone.coef) | copy-start | bytes 122884
  69.9 9.2 %copy-start.10 = (bf16[160,80]{1,0:T(8,128)(2,1)S(1)}, bf16[160,80]{1,0:T(8,128)(2,1)}, u32[]{:S(2)}) copy-start(bf16[160,80]{1,0:T(8,128)(2,1)} %constant.45.clone.upward) | copy-start | bytes 76804
  70.3 7.1 %collective-permute-start.10 = (bf16[30,8,128]{2,1,0:T(8,128)(2,1)S(1)}, bf16[30,8,128]{2,1,0:T(8,128)(2,1)S(1)}, u32[]{:S(2)}, u32[]{:S(2)}) collective-permute-start(bf16[30,8,128]{2,1,0:T(8,128)(2,1)S(1)} %get-tuple-element.38), channel_id=1, source_target_pairs={{16,32},{32,16},{48,64},{64,48},{80,96},{96,80},{112,128},{128,112... | collective-permute-start | bytes 184328 | tf_op jit(solution)/shard_map/ppermute | solution.py:696
  74.1 5.0 %collective-permute-start.11 = (bf16[30,8,128]{2,1,0:T(8,128)(2,1)S(1)}, bf16[30,8,128]{2,1,0:T(8,128)(2,1)S(1)}, u32[]{:S(2)}, u32[]{:S(2)}) collective-permute-start(bf16[30,8,128]{2,1,0:T(8,128)(2,1)S(1)} %get-tuple-element.39), channel_id=1, source_target_pairs={{0,16},{16,0},{32,48},{48,32},{64,80},{80,64},{96,112},{112,96},{1... | collective-permute-start | bytes 184328 | tf_op jit(solution)/shard_map/ppermute | solution.py:697
